TPU v7x, 128 devices: a whole 4x4x4 slice. The times are simulated.
128 devices in a mesh: tm: 8 (over z, y_hi), dof: 16 (over x, y_lo, core).
Axes of the slice: x: 4, y: 4 (y_hi: 2, y_lo: 2; y = y_hi * 2 + y_lo), z: 4, core: 2. Of those that a mesh axis runs over, the one named last changes fastest.
Arguments:
- loads: bfloat16 [3072, 8192], P('tm', 'dof'), may hold values from -6 to 6
- phi: bfloat16 [12288, 4096], P('dof'), may hold values from -0.09375 to 0.09375
- load_index: int32 [8192], P('dof'), may hold values from 0 to 12287, as said below
- damping: float32 [4096], P('dof'), may hold values from 6.510417e-05 to 0.05
- frequency: float32 [4096], P('dof'), may hold values from 0.05 to 1.5
- gains: float32 [3072], P('tm'), may hold values from 0.25 to 1
- shapes: bfloat16 [4096, 32768], P(None, 'dof'), may hold values from -0.09375 to 0.09375
Outputs:
- field: bfloat16 [3072, 32768], P('tm', 'dof')
- history: float32 [4096, 3072], P('dof', 'tm')
Inputs may be any that keep to these rules, and one draw needn't show every extreme that they name: `load_index`: entries k * 512 to (k + 1) * 512 - 1 name rows k * 768 to (k + 1) * 768 - 1; rows may repeat.
All inputs are finite; a program needn't handle non-finite values.
Results may differ from a plain program's by a relative error of at most 0.0049.
Values may be sent and summed in bfloat16 or wider, within the bound.
No kernel may reach another device: no remote copies, remote signals or barrier semaphores. Data moves between devices by JAX's collectives and lax.ppermute only.
A program may use at most 128 MiB of HBM per device.

v0:
```python
import jax
import jax.numpy as jnp
from jax import lax
from jax.sharding import PartitionSpec as P


def carried_in(value, axis, join, neutral):
    count, mine = (lax.axis_size(axis), lax.axis_index(axis))
    pieces = jax.tree.map(lambda part: lax.all_gather(part, axis), value)
    subtotal = jax.tree.map(
        lambda part, zero: jnp.full_like(part, 0) + jnp.asarray(zero, part.dtype), value, neutral
    )

    def step(position, subtotal):
        longer = join(subtotal, jax.tree.map(lambda part: part[position], pieces))
        return jax.tree.map(lambda new, old: jnp.where(position < mine, new, old), longer, subtotal)

    return lax.fori_loop(0, count - 1, step, subtotal)


def combine(earlier, later):
    ear, eai, ebr, ebi = earlier
    lar, lai, lbr, lbi = later
    return (
        lar * ear - lai * eai,
        lar * eai + lai * ear,
        lar * ebr - lai * ebi + lbr,
        lar * ebi + lai * ebr + lbi,
    )


def body(loads, phi, load_index, damping, frequency, gains, shapes):
    owned = damping.shape[0]
    steps = loads.shape[0]
    rows_here = phi.shape[0]
    local_index = load_index - lax.axis_index("dof") * rows_here
    selected = jnp.take(phi, local_index, axis=0)
    modal = lax.psum_scatter(
        lax.dot_general(
            selected, loads, (((0,), (1,)), ((), ())), preferred_element_type=jnp.float32
        ),
        "dof",
        scatter_dimension=0,
        tiled=True,
    )
    drive = jnp.sqrt(-jnp.expm1(-2.0 * damping))
    width = min(128, steps)
    blocks = steps // width
    log_gain = jnp.cumsum(jnp.log(gains).reshape(blocks, width), axis=1)
    rise = jnp.exp(log_gain)
    fall = jnp.exp(-log_gain)
    offsets = jnp.arange(width, dtype=jnp.float32)
    lag = offsets[:, None] - offsets[None, :]
    lower = lag >= 0.0
    lag_pos = jnp.where(lower, lag, 0.0)
    decay = jnp.exp(-damping[:, None, None] * lag_pos[None, :, :])
    turn = frequency[:, None, None] * lag_pos[None, :, :]
    kernel_re = jnp.where(lower[None, :, :], decay * jnp.cos(turn), 0.0)
    kernel_im = jnp.where(lower[None, :, :], decay * jnp.sin(turn), 0.0)
    pushed = (drive[:, None] * modal).reshape(owned, blocks, width) * fall[None, :, :]
    local_re = (
        jnp.einsum("mts,mns->mnt", kernel_re, pushed, precision=lax.Precision.HIGHEST)
        * rise[None, :, :]
    )
    local_im = (
        jnp.einsum("mts,mns->mnt", kernel_im, pushed, precision=lax.Precision.HIGHEST)
        * rise[None, :, :]
    )
    ahead = offsets + 1.0
    power_mag = jnp.exp(-damping[:, None] * ahead[None, :])
    power_re = power_mag * jnp.cos(frequency[:, None] * ahead[None, :])
    power_im = power_mag * jnp.sin(frequency[:, None] * ahead[None, :])
    carry_re_all = power_re[:, None, :] * rise[None, :, :]
    carry_im_all = power_im[:, None, :] * rise[None, :, :]
    unit = jnp.ones((owned,), jnp.float32)
    nothing = jnp.zeros((owned,), jnp.float32)
    running = (unit, nothing, nothing, nothing)
    entering = []
    for index in range(blocks):
        entering.append(running)
        piece = (
            carry_re_all[:, index, width - 1],
            carry_im_all[:, index, width - 1],
            local_re[:, index, width - 1],
            local_im[:, index, width - 1],
        )
        running = combine(running, piece)
    incoming = carried_in(running, "tm", combine, (unit, nothing, nothing, nothing))
    state_re = []
    state_im = []
    for index in range(blocks):
        joined = combine(incoming, entering[index])
        state_re.append(joined[2])
        state_im.append(joined[3])
    enter_re = jnp.stack(state_re, axis=1)
    enter_im = jnp.stack(state_im, axis=1)
    history = (
        carry_re_all * enter_re[:, :, None] - carry_im_all * enter_im[:, :, None] + local_re
    ).reshape(owned, steps)
    rounded = history.astype(jnp.bfloat16)
    field = lax.dot_general(
        lax.all_gather(rounded, "dof", axis=0, tiled=True),
        shapes,
        (((0,), (0,)), ((), ())),
        preferred_element_type=jnp.float32,
    )
    return (field.astype(jnp.bfloat16), history)


def solution(mesh):
    placed = (P("tm", "dof"), P("dof", None), P("dof"), P("dof"), P("dof"), P("tm"), P(None, "dof"))
    return jax.shard_map(
        body,
        mesh=mesh,
        in_specs=placed,
        out_specs=(P("tm", "dof"), P("dof", "tm")),
        check_vma=False,
    )
```

profile of v0, /device:TPU:1, one launch (start us, length us, event | category | flops | bytes accessed | tf_op | source)
XLA Modules:
  0.0 433.7 jit_solution(16857751007489199846)
XLA Ops:
  7.2 0.0 copy-start
  7.2 0.0 reduce-scatter.2.cloned.1.call-start
  7.2 0.7 compare_and_fusion
  8.0 12.3 %gather_fusion = bf16[512,4096]{1,0:T(8,128)(2,1)} fusion(bf16[768,4096]{1,0:T(8,128)(2,1)} %param.10, s32[1024]{0:T(1024)S(1)} %pad_clamp_fusion), kind=kCustom, calls=%fused_computation | custom fusion | bytes 8390656 | tf_op jit(solution)/shard_map/jit(_take)/gather | solution.py:37
  20.2 0.0 copy-start.1
  20.2 0.0 copy-start.3
  20.2 0.0 copy-start.2
  20.2 0.0 copy-done
  20.2 7.5 %fusion.18 = f32[4096,384]{1,0:T(8,128)} fusion(bf16[384,512]{1,0:T(8,128)(2,1)S(1)} %copy-done, bf16[512,4096]{1,0:T(8,128)(2,1)} %gather_fusion, pred[512]{0:T(512)(128)(4,1)S(1)} %get-tuple-element.215), kind=kOutput, calls=%fused_computation.28 | convolution fusion | flops 1612709888 | bytes 10879488 | tf_op jit(solution)/shard_map/dot_general | solution.py:39
  27.7 0.0 reduce-scatter.2.cloned.1.call-update
  27.7 0.2 all-gather.6.cloned.1.call-start
  28.0 0.0 copy-done.1
  28.0 0.3 reduce_window_sum.11
  28.4 0.0 copy-done.3
  28.4 0.0 copy-done.2
  28.4 0.5 fusion.28
  29.0 0.2 broadcast_multiply_fusion.1
  29.2 6.2 %slice_reduce_fusion.6 = (f32[256]{0:T(256)S(1)}, f32[256]{0:T(256)S(1)}, f32[256]{0:T(256)S(1)}, f32[256]{0:T(256)S(1)}, f32[256]{0:T(256)S(1)}, /*index=5*/f32[256]{0:T(256)S(1)}) fusion(f32[256,3,128]{2,1,0:T(4,128)S(1)} %get-tuple-element.237, f32[256,3,128]{2,1,0:T(4,128)S(1)} %get-tuple-element.236), kind=kLoop, calls=%fused_computation.50 | loop fusion | bytes 12288 | tf_op jit(solution)/shard_map/slice | solution.py:83
  35.3 71.8 %reduce-scatter.2.cloned.1.call-done = f32[256,384]{1,0:T(8,128)} async-done(((f32[4096,384]{1,0:T(8,128)}), f32[256,384]{1,0:T(8,128)}) %reduce-scatter.2.cloned.1.call-update) | async-done | bytes 393232 | tf_op jit(solution)/shard_map/reduce_scatter | solution.py:38
  107.1 1.1 broadcast_multiply_fusion.3
  108.2 0.2 copy.16
  108.4 0.1 broadcast_multiply_fusion.2
  108.5 0.2 copy.17
  108.7 80.8 %fusion.25 = f32[256,3,128]{2,1,0:T(4,128)S(1)} fusion(f32[256,3,128]{2,1,0:T(4,128)S(1)} %copy.17, f32[256]{0:T(256)S(1)} %copy-done.2, f32[128,128]{1,0:T(8,128)S(1)} %fusion.30, f32[256]{0:T(256)S(1)} %get-tuple-element.240, pred[128,128]{1,0:T(8,128)(4,1)S(1)} %fusion.31, f32[3,128]{1,0:T(4,128)S(1)} %get-tuple-element.238), kind=kOutput, calls=%fused_computation.34 | convolution fusion | flops 167870464 | bytes 871936 | tf_op jit(solution)/shard_map/mts,mns->mnt/dot_general | solution.py:62
  189.5 94.7 %fusion.22 = f32[256,3,128]{2,1,0:T(4,128)S(1)} fusion(f32[256,3,128]{2,1,0:T(4,128)S(1)} %copy.17, f32[256]{0:T(256)S(1)} %copy-done.2, f32[128,128]{1,0:T(8,128)S(1)} %fusion.30, f32[256]{0:T(256)S(1)} %get-tuple-element.240, pred[128,128]{1,0:T(8,128)(4,1)S(1)} %fusion.31, f32[3,128]{1,0:T(4,128)S(1)} %get-tuple-element.238), kind=kOutput, calls=%fused_computation.33 | convolution fusion | flops 167870464 | bytes 871936 | tf_op jit(solution)/shard_map/mts,mns->mnt/dot_general | solution.py:66
  284.3 6.2 %slice_reduce_fusion = (f32[256]{0:T(256)S(1)}, f32[256]{0:T(256)S(1)}, f32[256]{0:T(256)S(1)}, f32[256]{0:T(256)S(1)}, f32[256]{0:T(256)S(1)}, /*index=5*/f32[256]{0:T(256)S(1)}) fusion(f32[256,3,128]{2,1,0:T(4,128)S(1)} %fusion.22, f32[256,3,128]{2,1,0:T(4,128)S(1)} %fusion.25), kind=kLoop, calls=%fused_computation.44 | loop fusion | bytes 12288 | tf_op jit(solution)/shard_map/slice | solution.py:85
  290.5 20.5 %all-gather.2 = f32[8,1,256]{2,1,0:T(1,128)S(1)} all-gather(f32[1,1,256]{2,1,0:T(1,128)S(1)} %get-tuple-element.234), channel_id=1, replica_groups=mesh['tm'=8,'dof'=16] {'tm'}, dimensions={0}, use_global_device_ids=true | all-gather | bytes 9216 | tf_op jit(solution)/shard_map/all_gather | solution.py:9
  311.0 14.6 %all-gather = f32[8,1,256]{2,1,0:T(1,128)S(1)} all-gather(f32[1,1,256]{2,1,0:T(1,128)S(1)} %get-tuple-element.235), channel_id=1, replica_groups=mesh['tm'=8,'dof'=16] {'tm'}, dimensions={0}, use_global_device_ids=true | all-gather | bytes 9216 | tf_op jit(solution)/shard_map/all_gather | solution.py:9
  325.6 18.1 %all-gather.3 = f32[8,1,256]{2,1,0:T(1,128)S(1)} all-gather(f32[1,1,256]{2,1,0:T(1,128)S(1)} %get-tuple-element.209), channel_id=1, replica_groups=mesh['tm'=8,'dof'=16] {'tm'}, dimensions={0}, use_global_device_ids=true | all-gather | bytes 9216 | tf_op jit(solution)/shard_map/all_gather | solution.py:9
  343.7 14.6 %all-gather.1 = f32[8,1,256]{2,1,0:T(1,128)S(1)} all-gather(f32[1,1,256]{2,1,0:T(1,128)S(1)} %get-tuple-element.223), channel_id=1, replica_groups=mesh['tm'=8,'dof'=16] {'tm'}, dimensions={0}, use_global_device_ids=true | all-gather | bytes 9216 | tf_op jit(solution)/shard_map/all_gather | solution.py:9
  358.4 0.5 while.16
  358.9 0.1 copy.19
  359.1 0.1 copy.20
  359.2 0.7 subtract_add_fusion
  360.0 0.2 copy.21
  360.2 0.7 bitcast_convert_fusion
  360.9 0.0 all-gather.6.cloned.1.call-update
  360.9 0.9 copy.22
  361.8 52.8 %all-gather.6.cloned.1.call-done = bf16[4096,384]{0,1:T(8,128)(2,1)} async-done(((bf16[256,384]{0,1:T(8,128)(2,1)}), bf16[4096,384]{0,1:T(8,128)(2,1)}) %all-gather.6.cloned.1.call-update) | async-done | bytes 3145744 | tf_op jit(solution)/shard_map/all_gather | solution.py:102
  414.6 12.0 %convolution_convert_fusion = bf16[384,2048]{1,0:T(8,128)(2,1)} fusion(bf16[4096,384]{0,1:T(8,128)(2,1)} %all-gather.6.cloned.1.call-done, bf16[4096,2048]{1,0:T(8,128)(2,1)} %param.15), kind=kOutput, calls=%fused_computation.31 | convolution fusion | flops 6443237376 | bytes 21495808 | tf_op jit(solution)/shard_map/dot_general | solution.py:101
  (41 shorter events, 0.4 us)
Async XLA Ops:
  7.2 13.1 %copy-start = (bf16[384,512]{1,0:T(8,128)(2,1)S(1)}, bf16[384,512]{1,0:T(8,128)(2,1)}, u32[]{:S(2)}) copy-start(bf16[384,512]{1,0:T(8,128)(2,1)} %param.9) | copy-start | bytes 1179652
  7.2 99.9 %reduce-scatter.2.cloned.1.call-start = ((), (), s32[]{:S(2)}) async-start(), calls=%async_computation.1 | async-start | bytes 6684672 | tf_op jit(solution)/shard_map/reduce_scatter | solution.py:38
  20.2 7.7 %copy-start.1 = (f32[384]{0:T(512)S(1)}, f32[384]{0:T(512)}, u32[]{:S(2)}) copy-start(f32[384]{0:T(512)} %param.14) | copy-start | bytes 4612
  20.2 8.2 %copy-start.3 = (f32[256]{0:T(256)S(1)}, f32[256]{0:T(256)}, u32[]{:S(2)}) copy-start(f32[256]{0:T(256)} %param.12) | copy-start | bytes 3076
  20.2 8.2 %copy-start.2 = (f32[256]{0:T(256)S(1)}, f32[256]{0:T(256)}, u32[]{:S(2)}) copy-start(f32[256]{0:T(256)} %param.13) | copy-start | bytes 3076
  27.7 386.9 %all-gather.6.cloned.1.call-start = ((), (), s32[]{:S(2)}) async-start(), calls=%async_computation.2 | async-start | bytes 3342336 | tf_op jit(solution)/shard_map/all_gather | solution.py:102
Sparse Core Ops, SparseCore 0:
  27.8 79.2 reduce-scatter.1
  361.0 53.5 all-gather.5
where the time goes:
time: 439 us; the launch traced here: 434 us
  matrix products  195 us (44%)
  waiting for transfers between devices  125 us (28%)
  blocking collectives  67.9 us (15%)
  local copies, waits for them, and re-layouts  26.5 us (6%)
  between operations  14.5 us (3%)
  other arithmetic  4.69 us (1%)
    dot_general x1, matrix products, body(): jnp.einsum('mts,mns->mnt', kernel_im, pushed, precision=lax.Precision.HIG...  94.7 us
    dot_general x1, matrix products, body(): jnp.einsum('mts,mns->mnt', kernel_re, pushed, precision=lax.Precision.HIG...  80.8 us
    reduce_scatter x1, waiting for transfers between devices, body(): lax.psum_scatter(lax.dot_general(selected, loads, (((0,), (1,)), ((), ())...  71.8 us
    all_gather x4, blocking collectives, carried_in(): pieces = jax.tree.map(lambda part: lax.all_gather(part, axis), value)  67.9 us
    all_gather x1, waiting for transfers between devices, body(): lax.all_gather(rounded, 'dof', axis=0, tiled=True)  52.8 us
    gather x1, local copies, waits for them, and re-layouts, body(): selected = jnp.take(phi, local_index, axis=0)  12.3 us
    dot_general x1, matrix products, body(): lax.dot_general(lax.all_gather(rounded, 'dof', axis=0, tiled=True), shape...  12 us
  transfers between devices with their start and end apart: 2, of which 2 were waited for; matrix products, arithmetic and copies ran while one was open for 2% of the time, Pallas kernels for 0%

commit v1 on v0

v1 whole, which is shorter than its diff:
```python
import jax
import jax.numpy as jnp
from jax import lax
from jax.experimental import pallas as pl
from jax.experimental.pallas import tpu as pltpu
from jax.sharding import Mesh, PartitionSpec as P

TM = ("z", "yh")
XY = ("x", "yl")
DOF = ("x", "yl", "core")
F32 = jnp.float32
BF16 = jnp.bfloat16
LIMIT = 48 * 1024 * 1024


def vmem():
    return pl.BlockSpec(memory_space=pltpu.VMEM)


def scatter_kernel(index_ref, loads_ref, hi_ref, lo_ref):
    rows = hi_ref.shape[1]
    channels = index_ref.shape[1]
    place = lax.broadcasted_iota(jnp.int32, (rows, channels), 0)
    onehot = jnp.where(place == index_ref[...], 1.0, 0.0).astype(BF16)
    summed = lax.dot_general(
        loads_ref[...], onehot, (((1,), (1,)), ((), ())), preferred_element_type=F32
    )
    high = summed.astype(BF16)
    hi_ref[...] = high
    lo_ref[...] = (summed - high.astype(F32)).astype(BF16)


def scatter_loads(index_row, loads, rows):
    steps = loads.shape[0]
    shape = jax.ShapeDtypeStruct((steps, rows), BF16)
    return pl.pallas_call(
        scatter_kernel,
        out_shape=(shape, shape),
        in_specs=[vmem(), vmem()],
        out_specs=(vmem(), vmem()),
        name="scatter_loads",
    )(index_row, loads)


def partial_kernel(which_ref, hi_ref, lo_ref, phi_ref, out_ref):
    block = phi_ref[...]
    total = jnp.dot(hi_ref[...], block, preferred_element_type=F32)
    total += jnp.dot(lo_ref[...], block, preferred_element_type=F32)
    out_ref[0] = total.astype(out_ref.dtype)


def partial_modal(which, high, low, phi, owned, dtype):
    steps, rows = high.shape
    count = phi.shape[1] // owned // 2
    return pl.pallas_call(
        partial_kernel,
        out_shape=jax.ShapeDtypeStruct((count, steps, owned), dtype),
        grid_spec=pltpu.PrefetchScalarGridSpec(
            num_scalar_prefetch=1,
            grid=(count,),
            in_specs=[
                pl.BlockSpec((steps, rows), lambda i, w: (0, 0)),
                pl.BlockSpec((steps, rows), lambda i, w: (0, 0)),
                pl.BlockSpec((rows, owned), lambda i, w: (0, 2 * i + w[0])),
            ],
            out_specs=pl.BlockSpec((1, steps, owned), lambda i, w: (i, 0, 0)),
        ),
        cost_estimate=pl.CostEstimate(
            flops=4 * steps * rows * owned * count,
            bytes_accessed=rows * owned * count * 2,
            transcendentals=0,
        ),
        name="partial_modal",
    )(which, high, low, phi)


def coef_kernel(gain_ref, rows_ref, cr_ref, ci_ref, qr_ref, qi_ref, pre_ref, whole_ref):
    inner = gain_ref.shape[0]
    lanes = rows_ref.shape[1]
    zr = rows_ref[0:1, :]
    zi = rows_ref[1:2, :]
    reps = lanes // gain_ref.shape[2]
    qr = jnp.ones((8, lanes), F32)
    qi = jnp.zeros((8, lanes), F32)
    product = jnp.ones((8, gain_ref.shape[2]), F32)
    for j in range(inner):
        gain = gain_ref[j]
        product = product * gain
        gain = jnp.concatenate([gain] * reps, axis=1)
        cr = gain * zr
        ci = gain * zi
        cr_ref[j] = cr
        ci_ref[j] = ci
        qr, qi = qr * cr - qi * ci, qr * ci + qi * cr
        qr_ref[j] = qr
        qi_ref[j] = qi
    pr = jnp.ones((1, lanes), F32)
    pi = jnp.zeros((1, lanes), F32)
    total = jnp.ones((1, gain_ref.shape[2]), F32)
    for b in range(8):
        pre_ref[0, b : b + 1, :] = pr
        pre_ref[1, b : b + 1, :] = pi
        br = qr[b : b + 1, :]
        bi = qi[b : b + 1, :]
        pr, pi = pr * br - pi * bi, pr * bi + pi * br
        total = total * product[b : b + 1, :]
    whole_ref[...] = jnp.broadcast_to(jnp.concatenate([pr, pi], axis=1), whole_ref.shape)


def coefficients(gain_blocks, rows):
    inner = gain_blocks.shape[0]
    lanes = rows.shape[1]
    full = jax.ShapeDtypeStruct((inner, 8, lanes), F32)
    return pl.pallas_call(
        coef_kernel,
        out_shape=(
            full,
            full,
            full,
            full,
            jax.ShapeDtypeStruct((2, 8, lanes), F32),
            jax.ShapeDtypeStruct((8, 2 * lanes), F32),
        ),
        in_specs=[vmem(), vmem()],
        out_specs=(vmem(),) * 6,
        name="coefficients",
    )(gain_blocks, rows)


def local_kernel(parts_ref, rows_ref, cr_ref, ci_ref, qr_ref, qi_ref, whole_ref,
                 w_ref, enter_ref, send_ref, push_ref):
    count, steps, lanes = parts_ref.shape
    inner = steps // 8
    drive = rows_ref[2:3, :]
    tile = 64
    for s in range(0, steps, tile):
        total = parts_ref[0, s : s + tile, :].astype(F32)
        for c in range(1, count):
            total += parts_ref[c, s : s + tile, :].astype(F32)
        total *= drive
        push_ref[0, s : s + tile, :] = total[:, : lanes // 2]
        push_ref[1, s : s + tile, :] = total[:, lanes // 2 :]
    wr = jnp.zeros((8, lanes), F32)
    wi = jnp.zeros((8, lanes), F32)
    for j in range(inner):
        push = jnp.concatenate(
            [push_ref[h, pl.ds(j, 8, stride=inner), :] for h in range(2)], axis=1
        )
        cr = cr_ref[j]
        ci = ci_ref[j]
        wr, wi = cr * wr - ci * wi + push, cr * wi + ci * wr
        w_ref[j] = wr
    qr = qr_ref[inner - 1]
    qi = qi_ref[inner - 1]
    sr = jnp.zeros((1, lanes), F32)
    si = jnp.zeros((1, lanes), F32)
    for b in range(8):
        enter_ref[0, b : b + 1, :] = sr
        enter_ref[1, b : b + 1, :] = si
        br = qr[b : b + 1, :]
        bi = qi[b : b + 1, :]
        sr, si = (
            br * sr - bi * si + wr[b : b + 1, :],
            br * si + bi * sr + wi[b : b + 1, :],
        )
    send_ref[...] = jnp.concatenate(
        [jnp.broadcast_to(jnp.concatenate([sr, si], axis=1), (8, 2 * lanes)), whole_ref[...]],
        axis=1,
    )


def local_recurrence(parts, rows, cr, ci, qr, qi, whole):
    count, steps, lanes = parts.shape
    inner = steps // 8
    return pl.pallas_call(
        local_kernel,
        out_shape=(
            jax.ShapeDtypeStruct((inner, 8, lanes), F32),
            jax.ShapeDtypeStruct((2, 8, lanes), F32),
            jax.ShapeDtypeStruct((8, 4 * lanes), F32),
        ),
        in_specs=[vmem()] * 7,
        out_specs=(vmem(),) * 3,
        scratch_shapes=[pltpu.VMEM((2, steps, lanes // 2), F32)],
        compiler_params=pltpu.CompilerParams(vmem_limit_bytes=LIMIT),
        name="local_recurrence",
    )(parts, rows, cr, ci, qr, qi, whole)


def history_kernel(mine_ref, got_ref, enter_ref, pre_ref, w_ref, qr_ref, qi_ref,
                   history_ref, rounded_ref, hist_ref):
    inner, _, lanes = w_ref.shape
    mine = mine_ref[0]
    sr = jnp.zeros((1, lanes), F32)
    si = jnp.zeros((1, lanes), F32)
    for k in range(7):
        row = got_ref[k : k + 1, :]
        br = row[:, 0:lanes]
        bi = row[:, lanes : 2 * lanes]
        ar = row[:, 2 * lanes : 3 * lanes]
        ai = row[:, 3 * lanes : 4 * lanes]
        nr = ar * sr - ai * si + br
        ni = ar * si + ai * sr + bi
        take = jnp.full((1, lanes), mine, jnp.int32) > k
        sr = jnp.where(take, nr, sr)
        si = jnp.where(take, ni, si)
    er = enter_ref[0] + pre_ref[0] * sr - pre_ref[1] * si
    ei = enter_ref[1] + pre_ref[0] * si + pre_ref[1] * sr
    for j in range(inner):
        value = w_ref[j] + qr_ref[j] * er - qi_ref[j] * ei
        for h in range(2):
            hist_ref[h, pl.ds(j, 8, stride=inner), :] = value[
                :, h * (lanes // 2) : (h + 1) * (lanes // 2)
            ]
    for h in range(2):
        half = hist_ref[h]
        rounded_ref[:, h * (lanes // 2) : (h + 1) * (lanes // 2)] = half.astype(BF16)
        history_ref[h * (lanes // 2) : (h + 1) * (lanes // 2), :] = half.T


def make_history(mine, got, enter, pre, w, qr, qi):
    inner, _, lanes = w.shape
    steps = inner * 8
    return pl.pallas_call(
        history_kernel,
        out_shape=(
            jax.ShapeDtypeStruct((lanes, steps), F32),
            jax.ShapeDtypeStruct((steps, lanes), BF16),
        ),
        in_specs=[pl.BlockSpec(memory_space=pltpu.SMEM)] + [vmem()] * 6,
        out_specs=(vmem(), vmem()),
        scratch_shapes=[pltpu.VMEM((2, steps, lanes // 2), F32)],
        name="make_history",
    )(mine, got, enter, pre, w, qr, qi)


def field_kernel(core_ref, near_ref, far_ref, even_ref, odd_ref, out_ref, acc_ref):
    step = pl.program_id(0)
    core = core_ref[0]

    @pl.when(step == 0)
    def _():
        acc_ref[...] = jnp.zeros_like(acc_ref)

    total = jnp.dot(near_ref[0], even_ref[0, 0], preferred_element_type=F32)
    total += jnp.dot(far_ref[0], odd_ref[0, 0], preferred_element_type=F32)
    acc_ref[...] += total

    @pl.when(step == pl.num_programs(0) - 1)
    def _():
        out_ref[...] = acc_ref[...].astype(BF16)


def make_field(core, near, far, shapes):
    count, steps, lanes = near.shape
    points = shapes.shape[1]
    view = shapes.reshape(count, 2, lanes, points)
    return pl.pallas_call(
        field_kernel,
        out_shape=jax.ShapeDtypeStruct((steps, points), BF16),
        grid_spec=pltpu.PrefetchScalarGridSpec(
            num_scalar_prefetch=1,
            grid=(count,),
            in_specs=[
                pl.BlockSpec((1, steps, lanes), lambda i, c: (i, 0, 0)),
                pl.BlockSpec((1, steps, lanes), lambda i, c: (i, 0, 0)),
                pl.BlockSpec((1, 1, lanes, points), lambda i, c: (i, c[0], 0, 0)),
                pl.BlockSpec((1, 1, lanes, points), lambda i, c: (i, 1 - c[0], 0, 0)),
            ],
            out_specs=pl.BlockSpec((steps, points), lambda i, c: (0, 0)),
            scratch_shapes=[pltpu.VMEM((steps, points), F32)],
        ),
        compiler_params=pltpu.CompilerParams(vmem_limit_bytes=LIMIT),
        name="make_field",
    )(core, near, far, view, view)


def body(loads, phi, load_index, damping, frequency, gains, shapes):
    owned = damping.shape[0]
    steps = loads.shape[0]
    rows_here = phi.shape[0]
    inner = steps // 8
    core = lax.axis_index("core").astype(jnp.int32).reshape(1)
    pair = [(0, 1), (1, 0)]
    index_row = (load_index - lax.axis_index(DOF) * rows_here).reshape(1, -1)

    high, low = scatter_loads(index_row, loads, rows_here)
    send = partial_modal(1 - core, high, low, phi, owned, BF16)
    got = lax.ppermute(send, "core", pair)
    keep = partial_modal(core, high, low, phi, owned, F32)

    radius = jnp.exp(-damping)
    drive = jnp.sqrt(-jnp.expm1(-2.0 * damping))
    nothing = jnp.zeros_like(drive)
    rows = jnp.stack(
        [radius * jnp.cos(frequency), radius * jnp.sin(frequency), drive] + [nothing] * 5
    )
    gain_blocks = jnp.broadcast_to(gains.reshape(8, inner).T[:, :, None], (inner, 8, 128))
    cr, ci, qr, qi, pre, whole = coefficients(gain_blocks, rows)

    summed = (keep + got.astype(F32)).astype(BF16)
    parts = lax.all_to_all(summed, XY, 0, 0)
    w, enter, payload = local_recurrence(parts, rows, cr, ci, qr, qi, whole)
    states = lax.all_to_all(payload, TM, 0, 0)
    mine = lax.axis_index(TM).astype(jnp.int32).reshape(1)
    history, rounded = make_history(mine, states, enter, pre, w, qr, qi)
    near = lax.all_to_all(jnp.broadcast_to(rounded[None], (8,) + rounded.shape), XY, 0, 0)
    far = lax.ppermute(near, "core", pair)
    field = make_field(core, near, far, shapes)
    return field, history


def solution(mesh):
    grid = Mesh(mesh.devices.reshape(4, 2, 4, 2, 2), ("z", "yh", "x", "yl", "core"))
    placed = (
        P(TM, DOF),
        P(DOF, None),
        P(DOF),
        P(DOF),
        P(DOF),
        P(TM),
        P(None, DOF),
    )
    return jax.shard_map(
        body,
        mesh=grid,
        in_specs=placed,
        out_specs=(P(TM, DOF), P(DOF, TM)),
        check_vma=False,
    )
```

time: 439 us -> 122 us (0.28)
  matrix products: 195 us -> 0 us
  waiting for transfers between devices: 125 us -> 29.9 us
  blocking collectives: 67.9 us -> 20.6 us
  Pallas kernels: 0 us -> 36.4 us
  starting transfers between devices: 0.26 us -> 17.8 us
  local copies, waits for them, and re-layouts: 26.5 us -> 10.6 us
  between operations: 14.5 us -> 0.7 us
    dot_general x4 -> x0, matrix products: 195 us -> none  [the longest x1 94.7 us: body(): jnp.einsum('mts,mns->mnt', kernel_im, pushed, precision=lax.Precision.HIG...]
    reduce_scatter x1 -> x0, waiting for transfers between devices: 71.8 us -> none  [body(): lax.psum_scatter(lax.dot_general(selected, loads, (((0,), (1,)), ((), ())...]
    all_gather x4 -> x0, blocking collectives: 67.9 us -> none  [carried_in(): pieces = jax.tree.map(lambda part: lax.all_gather(part, axis), value)]
    all_gather x1 -> x0, waiting for transfers between devices: 52.8 us -> none  [body(): lax.all_gather(rounded, 'dof', axis=0, tiled=True)]
    pallas_call x0 -> x7, Pallas kernels: none -> 36.4 us  [the longest x2 16 us: partial_modal(): pl.pallas_call(partial_kernel, out_shape=jax.ShapeDtypeStruct((count, ste...]
    all_to_all x0 -> x2, waiting for transfers between devices: none -> 26.9 us  [the longest x1 20.2 us: body(): parts = lax.all_to_all(summed, XY, 0, 0)]
    all_to_all x0 -> x1, blocking collectives: none -> 20.6 us  [body(): lax.all_to_all(jnp.broadcast_to(rounded[None], (8,) + rounded.shape), XY,...]
    all_to_all x0 -> x2, starting transfers between devices: none -> 12.6 us  [the longest x1 7.39 us: body(): states = lax.all_to_all(payload, TM, 0, 0)]
  transfers between devices with their start and end apart: 2 -> 4, of which waited for: 2 -> 3; matrix products, arithmetic and copies ran while one was open for 2% -> 1% of each run, Pallas kernels for 0% -> 9%
where the time goes in v1:
time: 122 us; the launch traced here: 121 us
  Pallas kernels  36.4 us (30%)
  waiting for transfers between devices  29.9 us (25%)
  blocking collectives  20.6 us (17%)
  starting transfers between devices  17.8 us (15%)
  local copies, waits for them, and re-layouts  10.6 us (9%)
  other arithmetic  4.71 us (4%)
    all_to_all x1, blocking collectives, body(): lax.all_to_all(jnp.broadcast_to(rounded[None], (8,) + rounded.shape), XY,...  20.6 us
    all_to_all x1, waiting for transfers between devices, body(): parts = lax.all_to_all(summed, XY, 0, 0)  20.2 us
    pallas_call x2, Pallas kernels, partial_modal(): pl.pallas_call(partial_kernel, out_shape=jax.ShapeDtypeStruct((count, ste...  16 us
    pallas_call x1, Pallas kernels, make_field(): pl.pallas_call(field_kernel, out_shape=jax.ShapeDtypeStruct((steps, point...  13 us
    all_to_all x1, starting transfers between devices, body(): states = lax.all_to_all(payload, TM, 0, 0)  7.39 us
    unnamed x23, local copies, waits for them, and re-layouts  7.35 us
    all_to_all x1, waiting for transfers between devices, body(): states = lax.all_to_all(payload, TM, 0, 0)  6.61 us
    all_to_all x1, starting transfers between devices, body(): parts = lax.all_to_all(summed, XY, 0, 0)  5.25 us
  transfers between devices with their start and end apart: 4, of which 3 were waited for; matrix products, arithmetic and copies ran while one was open for 1% of the time, Pallas kernels for 9%

profile of v1, /device:TPU:1, one launch (start us, length us, event | category | flops | bytes accessed | tf_op | source)
XLA Modules:
  0.0 120.8 jit_solution(1421584357512705759)
XLA Ops:
  0.6 1.3 %broadcast_subtract_fusion = s32[512]{0:T(512)} fusion(s32[512]{0:T(512)} %param.9, s32[]{:T(128)S(6)} %mul.27), kind=kLoop, calls=%fused_computation.6 | loop fusion | flops 512 | bytes 4100 | tf_op jit(solution)/shard_map/sub | solution.py:285
  1.9 2.5 %scatter_loads.1 = (bf16[384,768]{1,0:T(8,128)(2,1)}, bf16[384,768]{1,0:T(8,128)(2,1)}) custom-call(s32[1,512]{1,0:T(1,128)} %bitcast.17, bf16[384,512]{1,0:T(8,128)(2,1)} %loads_ref.1), custom_call_target="tpu_custom_call" | custom-call | tf_op jit(solution)/shard_map/scatter_loads/pallas_call | solution.py:36
  4.4 7.9 %partial_modal.3 = bf16[8,384,256]{2,1,0:T(8,128)(2,1)} custom-call(s32[1]{0:T(128)S(6)} %sub.11.which_ref, bf16[384,768]{1,0:T(8,128)(2,1)} %get-tuple-element.15.hi_ref, bf16[384,768]{1,0:T(8,128)(2,1)} %get-tuple-element.16.lo_ref, bf16[768,4096]{1,0:T(8,128)(2,1)} %phi_ref.3), custom_call_target="tpu_custom_call" | custom-call | flops 2415919104 | bytes 3145728 | tf_op jit(solution)/shard_map/partial_modal/pallas_call | solution.py:55
  12.3 1.4 %collective-permute-start = (bf16[8,384,256]{2,1,0:T(8,128)(2,1)}, bf16[8,384,256]{2,1,0:T(8,128)(2,1)S(1)}, u32[]{:S(2)}, u32[]{:S(2)}) collective-permute-start(bf16[8,384,256]{2,1,0:T(8,128)(2,1)} %partial_modal.3), channel_id=1, source_target_pairs={{0,1},{1,0},{2,3},{3,2},{4,5},{5,4},{6,7},{7,6},{8,9},{9,8},{10,11... | collective-permute-start | bytes 4718600 | tf_op jit(solution)/shard_map/ppermute | solution.py:289
  13.7 8.1 %partial_modal.2 = f32[8,384,256]{2,1,0:T(8,128)} custom-call(s32[1]{0:T(128)} %bitcast.which_ref.core_ref, bf16[384,768]{1,0:T(8,128)(2,1)} %get-tuple-element.15.hi_ref, bf16[384,768]{1,0:T(8,128)(2,1)} %get-tuple-element.16.lo_ref, bf16[768,4096]{1,0:T(8,128)(2,1)} %phi_ref.3), custom_call_target="tpu_custom_call" | custom-call | flops 2415919104 | bytes 3145728 | tf_op jit(solution)/shard_map/partial_modal/pallas_call | solution.py:55
  21.9 0.0 collective-permute-done
  21.9 3.4 %add_convert_fusion = bf16[8,384,256]{2,1,0:T(8,128)(2,1)} fusion(f32[8,384,256]{2,1,0:T(8,128)} %partial_modal.2, bf16[8,384,256]{2,1,0:T(8,128)(2,1)S(1)} %collective-permute-done), kind=kLoop, calls=%fused_computation | loop fusion | flops 2359296 | bytes 6291456 | tf_op jit(solution)/shard_map/convert_element_type | solution.py:301
  25.3 0.0 copy-start.8
  25.3 0.0 copy-start.9
  25.3 0.0 copy-start.10
  25.3 5.2 %all-to-all-start = ((bf16[8,384,256]{2,1,0:T(8,128)(2,1)}), bf16[8,384,256]{2,1,0:T(8,128)(2,1)S(1)}, u32[]{:S(2)}, u32[]{:S(2)}) async-start(bf16[8,384,256]{2,1,0:T(8,128)(2,1)} %add_convert_fusion), calls=%async_computation | async-start | bytes 3145728 | tf_op jit(solution)/shard_map/all_to_all | solution.py:302
  30.5 0.0 copy-done.8
  30.5 0.1 reshape.26
  30.6 0.1 copy.10
  30.7 0.0 copy-done.9
  30.7 0.0 copy-done.10
  30.8 0.6 stack.19.rows_ref
  31.4 0.8 broadcast_in_dim.4.gain_ref
  32.2 2.2 %coefficients.1 = (f32[48,8,256]{2,1,0:T(8,128)}, f32[48,8,256]{2,1,0:T(8,128)}, f32[48,8,256]{2,1,0:T(8,128)}, f32[48,8,256]{2,1,0:T(8,128)}, f32[2,8,256]{2,1,0:T(8,128)}, /*index=5*/f32[8,512]{1,0:T(8,128)}) custom-call(f32[48,8,128]{2,1,0:T(8,128)} %broadcast_in_dim.4.gain_ref, f32[8,256]{1,0:T(8,128)} %stack.19.rows_ref), custom_call_target="tpu_custom_call" | custom-call | tf_op jit(solution)/shard_map/coefficients/pallas_call | solution.py:114
  34.3 20.2 %all-to-all-done.parts_ref = bf16[8,384,256]{2,1,0:T(8,128)(2,1)S(1)} async-done(((bf16[8,384,256]{2,1,0:T(8,128)(2,1)}), bf16[8,384,256]{2,1,0:T(8,128)(2,1)S(1)}, u32[]{:S(2)}, u32[]{:S(2)}) %all-to-all-start) | async-done | bytes 1572896 | tf_op jit(solution)/shard_map/all_to_all | solution.py:302
  54.6 0.0 copy-start
  54.6 1.0 copy-done
  55.6 0.0 copy-start.1
  55.6 1.0 copy-done.1
  56.6 0.0 copy-start.2
  56.6 1.0 copy-done.2
  57.6 0.0 copy-start.3
  57.6 1.0 copy-done.3
  58.6 0.0 copy-start.5
  58.6 0.7 copy-done.5
  59.3 0.0 copy-start.7
  59.3 0.7 copy-done.7
  60.0 0.4 local_recurrence.1
  60.4 0.0 copy-start.4
  60.4 0.7 copy-done.4
  61.1 0.0 copy-start.6
  61.1 0.6 copy-done.6
  61.7 0.6 copy.11
  62.4 7.4 %all-to-all-start.1 = ((f32[8,1,1024]{2,1,0:T(1,128)}), f32[8,1,1024]{2,1,0:T(1,128)S(1)}, u32[]{:S(2)}, u32[]{:S(2)}) async-start(f32[8,1,1024]{2,1,0:T(1,128)} %copy.11), calls=%async_computation.1 | async-start | bytes 65536 | tf_op jit(solution)/shard_map/all_to_all | solution.py:304
  69.8 6.6 %all-to-all-done.1 = f32[8,1,1024]{2,1,0:T(1,128)S(1)} async-done(((f32[8,1,1024]{2,1,0:T(1,128)}), f32[8,1,1024]{2,1,0:T(1,128)S(1)}, u32[]{:S(2)}, u32[]{:S(2)}) %all-to-all-start.1) | async-done | bytes 32800 | tf_op jit(solution)/shard_map/all_to_all | solution.py:304
  76.4 0.6 copy.14
  77.0 2.4 %make_history.1 = (f32[256,384]{1,0:T(8,128)}, bf16[384,256]{1,0:T(8,128)(2,1)}) custom-call(s32[1]{0:T(128)} %bitcast.1.mine_ref, f32[8,1024]{1,0:T(8,128)} %bitcast.15, f32[2,8,256]{2,1,0:T(8,128)} %copy-done.6, f32[2,8,256]{2,1,0:T(8,128)} %get-tuple-element.24.pre_ref, f32[48,8,256]{2,1,0:T(8,128)} %copy-done.4, f32[48,8,256]{2,1,0:T(8,128)} %get-tuple-element.19.qr_ref, ...), custom_call_target="tpu_custom_call" | custom-call | tf_op jit(solution)/shard_map/make_history/pallas_call | solution.py:224
  79.3 1.0 broadcast_in_dim.5
  80.4 20.6 %all_to_all.21.near_ref = bf16[8,384,256]{2,1,0:T(8,128)(2,1)S(1)} all-to-all(bf16[8,384,256]{2,1,0:T(8,128)(2,1)S(1)} %broadcast_in_dim.5), channel_id=1, replica_groups=mesh['z'=4,'yh'=2,'x'=4,'yl'=2,'core'=2] {'x','yl'}, dimensions={0} | all-to-all | bytes 3145728 | tf_op jit(solution)/shard_map/all_to_all | solution.py:307
  101.0 3.7 %collective-permute-start.1 = (bf16[8,384,256]{2,1,0:T(8,128)(2,1)S(1)}, bf16[8,384,256]{2,1,0:T(8,128)(2,1)S(1)}, u32[]{:S(2)}, u32[]{:S(2)}) collective-permute-start(bf16[8,384,256]{2,1,0:T(8,128)(2,1)S(1)} %all_to_all.21.near_ref), channel_id=1, source_target_pairs={{0,1},{1,0},{2,3},{3,2},{4,5},{5,4},{6,7},{7,6},{8,9},{9,8},{10,11... | collective-permute-start | bytes 4718600 | tf_op jit(solution)/shard_map/ppermute | solution.py:308
  104.7 3.0 %collective-permute-done.1.far_ref = bf16[8,384,256]{2,1,0:T(8,128)(2,1)S(1)} collective-permute-done((bf16[8,384,256]{2,1,0:T(8,128)(2,1)S(1)}, bf16[8,384,256]{2,1,0:T(8,128)(2,1)S(1)}, u32[]{:S(2)}, u32[]{:S(2)}) %collective-permute-start.1) | collective-permute-done | bytes 1572896 | tf_op jit(solution)/shard_map/ppermute | solution.py:308
  107.8 13.0 %make_field.1 = bf16[384,2048]{1,0:T(8,128)(2,1)} custom-call(s32[1]{0:T(128)} %bitcast.which_ref.core_ref, bf16[8,384,256]{2,1,0:T(8,128)(2,1)S(1)} %all_to_all.21.near_ref, bf16[8,384,256]{2,1,0:T(8,128)(2,1)S(1)} %collective-permute-done.1.far_ref, bf16[8,2,256,2048]{3,2,1,0:T(8,128)(2,1)} %bitcast.13, bf16[8,2,256,2048]{3,2,1,0:T(8,128)(2,1)} %bitcast.14), custom_call_target="tpu_custom_call" | custom-call | tf_op jit(solution)/shard_map/make_field/pallas_call | solution.py:258
  (3 shorter events, 0.0 us)
Async XLA Ops:
  12.3 9.6 %collective-permute-start = (bf16[8,384,256]{2,1,0:T(8,128)(2,1)}, bf16[8,384,256]{2,1,0:T(8,128)(2,1)S(1)}, u32[]{:S(2)}, u32[]{:S(2)}) collective-permute-start(bf16[8,384,256]{2,1,0:T(8,128)(2,1)} %partial_modal.3), channel_id=1, source_target_pairs={{0,1},{1,0},{2,3},{3,2},{4,5},{5,4},{6,7},{7,6},{8,9},{9,8},{10,11... | collective-permute-start | bytes 4718600 | tf_op jit(solution)/shard_map/ppermute | solution.py:289
  25.3 5.3 %copy-start.8 = (f32[384]{0:T(512)S(1)}, f32[384]{0:T(512)}, u32[]{:S(2)}) copy-start(f32[384]{0:T(512)} %param.12) | copy-start | bytes 4612
  25.3 5.4 %copy-start.9 = (f32[256]{0:T(256)S(1)}, f32[256]{0:T(256)}, u32[]{:S(2)}) copy-start(f32[256]{0:T(256)} %param.11) | copy-start | bytes 3076
  25.3 5.4 %copy-start.10 = (f32[256]{0:T(256)S(1)}, f32[256]{0:T(256)}, u32[]{:S(2)}) copy-start(f32[256]{0:T(256)} %param.10) | copy-start | bytes 3076
  25.3 29.3 %all-to-all-start = ((bf16[8,384,256]{2,1,0:T(8,128)(2,1)}), bf16[8,384,256]{2,1,0:T(8,128)(2,1)S(1)}, u32[]{:S(2)}, u32[]{:S(2)}) async-start(bf16[8,384,256]{2,1,0:T(8,128)(2,1)} %add_convert_fusion), calls=%async_computation | async-start | bytes 3145728 | tf_op jit(solution)/shard_map/all_to_all | solution.py:302
  54.6 1.0 copy-start
  55.6 1.0 copy-start.1
  56.6 1.0 copy-start.2
  57.6 1.0 copy-start.3
  58.6 0.7 copy-start.5
  59.3 0.7 copy-start.7
  60.4 0.7 copy-start.4
  61.1 0.6 copy-start.6
  62.4 14.0 %all-to-all-start.1 = ((f32[8,1,1024]{2,1,0:T(1,128)}), f32[8,1,1024]{2,1,0:T(1,128)S(1)}, u32[]{:S(2)}, u32[]{:S(2)}) async-start(f32[8,1,1024]{2,1,0:T(1,128)} %copy.11), calls=%async_computation.1 | async-start | bytes 65536 | tf_op jit(solution)/shard_map/all_to_all | solution.py:304
  101.0 6.8 %collective-permute-start.1 = (bf16[8,384,256]{2,1,0:T(8,128)(2,1)S(1)}, bf16[8,384,256]{2,1,0:T(8,128)(2,1)S(1)}, u32[]{:S(2)}, u32[]{:S(2)}) collective-permute-start(bf16[8,384,256]{2,1,0:T(8,128)(2,1)S(1)} %all_to_all.21.near_ref), channel_id=1, source_target_pairs={{0,1},{1,0},{2,3},{3,2},{4,5},{5,4},{6,7},{7,6},{8,9},{9,8},{10,11... | collective-permute-start | bytes 4718600 | tf_op jit(solution)/shard_map/ppermute | solution.py:308

commit v2 on v1

v2 whole, which is shorter than its diff:
```python
import jax
import jax.numpy as jnp
from jax import lax
from jax.experimental import pallas as pl
from jax.experimental.pallas import tpu as pltpu
from jax.sharding import Mesh, PartitionSpec as P

TM = ("z", "yh")
XY = ("x", "yl")
DOF = ("x", "yl", "core")
F32 = jnp.float32
BF16 = jnp.bfloat16
LANES = 256
HALF = 128
MID = 24 * 1024 * 1024
BIG = 40 * 1024 * 1024
STEPS = ((1, 0), (3, 0), (2, 0), (0, 1), (1, 1), (3, 1), (2, 1), (0, 0))
FIRST, LAST = (0, 1, 2, 3), (4, 5, 6, 7)


def vmem():
    return pl.BlockSpec(memory_space=pltpu.VMEM)


def cost(flops, moved):
    return pl.CostEstimate(flops=int(flops), bytes_accessed=int(moved), transcendentals=0)


def fetch_columns(columns_ref, phi_ref, held_ref, sems, chosen):
    copies = []
    for slot, q in enumerate(chosen):
        place = pl.multiple_of(columns_ref[q] * LANES, LANES)
        copies.append(
            pltpu.make_async_copy(
                phi_ref.at[:, pl.ds(place, LANES)], held_ref.at[slot], sems.at[slot]
            )
        )
    for copy in copies:
        copy.start()
    return copies


def open_kernel(chosen, columns_ref, index_ref, loads_ref, phi_ref, scat_ref, *refs):
    outs, held_ref, sems = refs[:-2], refs[-2], refs[-1]
    copies = fetch_columns(columns_ref, phi_ref, held_ref, sems, chosen)
    rows = scat_ref.shape[1]
    channels = index_ref.shape[1]
    local = index_ref[...] - lax.axis_index(DOF) * rows
    place = lax.broadcasted_iota(jnp.int32, (rows, channels), 0)
    onehot = jnp.where(place == local, 1.0, 0.0).astype(BF16)
    summed = lax.dot_general(
        loads_ref[...], onehot, (((1,), (1,)), ((), ())), preferred_element_type=F32
    )
    scat_ref[...] = summed.astype(BF16)
    for base in range(0, len(copies), 4):
        for copy in copies[base : base + 4]:
            copy.wait()
        block = jnp.concatenate([held_ref[base + q] for q in range(4)], axis=1)
        total = jnp.dot(scat_ref[...], block, preferred_element_type=F32)
        for q in range(4):
            outs[base + q][...] = total[:, q * LANES : (q + 1) * LANES].astype(BF16)


def more_kernel(chosen, mates, columns_ref, scat_ref, phi_ref, *refs):
    got, outs, held_ref, sems = refs[:mates], refs[mates:-2], refs[-2], refs[-1]
    copies = fetch_columns(columns_ref, phi_ref, held_ref, sems, chosen)
    for copy in copies:
        copy.wait()
    block = jnp.concatenate([held_ref[q] for q in range(len(copies))], axis=1)
    total = jnp.dot(scat_ref[...], block, preferred_element_type=F32)
    for q in range(len(copies)):
        value = total[:, q * LANES : (q + 1) * LANES] + got[q][...].astype(F32)
        outs[q][...] = value.astype(BF16)


def smem():
    return pl.BlockSpec(memory_space=pltpu.SMEM)


def hbm():
    return pl.BlockSpec(memory_space=pltpu.HBM)


def open_partial(columns, index_row, loads, phi, chosen):
    steps, channels = loads.shape
    rows = phi.shape[0]
    count = len(chosen)
    return pl.pallas_call(
        lambda *refs: open_kernel(chosen, *refs),
        out_shape=(jax.ShapeDtypeStruct((steps, rows), BF16),)
        + (jax.ShapeDtypeStruct((steps, LANES), BF16),) * count,
        in_specs=[smem(), vmem(), vmem(), hbm()],
        out_specs=(vmem(),) * (count + 1),
        scratch_shapes=[
            pltpu.VMEM((count, rows, LANES), BF16),
            pltpu.SemaphoreType.DMA((count,)),
        ],
        cost_estimate=cost(
            2 * steps * rows * (channels + count * LANES), 2 * rows * count * LANES
        ),
        compiler_params=pltpu.CompilerParams(vmem_limit_bytes=MID),
        name="open_partial",
    )(columns, index_row, loads, phi)


def more_partial(columns, scat, phi, chosen, got):
    steps, rows = scat.shape
    count = len(chosen)
    return pl.pallas_call(
        lambda *refs: more_kernel(chosen, len(got), *refs),
        out_shape=(jax.ShapeDtypeStruct((steps, LANES), BF16),) * count,
        in_specs=[smem(), vmem(), hbm()] + [vmem()] * len(got),
        out_specs=(vmem(),) * count,
        scratch_shapes=[
            pltpu.VMEM((count, rows, LANES), BF16),
            pltpu.SemaphoreType.DMA((count,)),
        ],
        cost_estimate=cost(2 * steps * rows * count * LANES, 2 * rows * count * LANES),
        compiler_params=pltpu.CompilerParams(vmem_limit_bytes=MID),
        name="more_partial",
    )(columns, scat, phi, *got)


def coef_kernel(gain_ref, rows_ref, cr_ref, ci_ref, qr_ref, qi_ref, pre_ref, whole_ref):
    inner = gain_ref.shape[0]
    zr = rows_ref[0:1, :]
    zi = rows_ref[1:2, :]
    qr = jnp.ones((8, LANES), F32)
    qi = jnp.zeros((8, LANES), F32)
    for j in range(inner):
        gain = jnp.concatenate([gain_ref[j]] * 2, axis=1)
        cr = gain * zr
        ci = gain * zi
        cr_ref[j] = cr
        ci_ref[j] = ci
        qr, qi = qr * cr - qi * ci, qr * ci + qi * cr
        qr_ref[j] = qr
        qi_ref[j] = qi
    pr = jnp.ones((1, LANES), F32)
    pi = jnp.zeros((1, LANES), F32)
    for b in range(8):
        pre_ref[0, b : b + 1, :] = pr
        pre_ref[1, b : b + 1, :] = pi
        br = qr[b : b + 1, :]
        bi = qi[b : b + 1, :]
        pr, pi = pr * br - pi * bi, pr * bi + pi * br
    whole_ref[0:1, :] = pr
    whole_ref[1:2, :] = pi
    whole_ref[2:3, :] = rows_ref[2:3, :]
    whole_ref[3:8, :] = jnp.zeros((5, LANES), F32)


def coefficients(gain_blocks, rows):
    inner = gain_blocks.shape[0]
    full = jax.ShapeDtypeStruct((inner, 8, LANES), F32)
    return pl.pallas_call(
        coef_kernel,
        out_shape=(
            full,
            full,
            full,
            full,
            jax.ShapeDtypeStruct((2, 8, LANES), F32),
            jax.ShapeDtypeStruct((8, LANES), F32),
        ),
        in_specs=[vmem(), vmem()],
        out_specs=(vmem(),) * 6,
        cost_estimate=cost(inner * 8 * LANES * 8, inner * 8 * LANES * 20),
        name="coefficients",
    )(gain_blocks, rows)


def local_kernel(*refs):
    parts = refs[:-9]
    cr_ref, ci_ref, qr_ref, qi_ref, whole_ref, w_ref, enter_ref, send_ref, push_ref = refs[-9:]
    steps = parts[0].shape[0]
    inner = steps // 8
    drive = whole_ref[2:3, :]
    tile = 64
    for s in range(0, steps, tile):
        total = parts[0][s : s + tile, :].astype(F32)
        for part in parts[1:]:
            total += part[s : s + tile, :].astype(F32)
        total = total * drive
        for h in range(2):
            push_ref[h, s : s + tile, :] = total[:, h * HALF : (h + 1) * HALF]
    wr = jnp.zeros((8, LANES), F32)
    wi = jnp.zeros((8, LANES), F32)
    for j in range(inner):
        push = jnp.concatenate(
            [push_ref[h, pl.ds(j, 8, stride=inner), :] for h in range(2)], axis=1
        )
        cr = cr_ref[j]
        ci = ci_ref[j]
        wr, wi = cr * wr - ci * wi + push, cr * wi + ci * wr
        w_ref[j] = wr
    qr = qr_ref[inner - 1]
    qi = qi_ref[inner - 1]
    sr = jnp.zeros((1, LANES), F32)
    si = jnp.zeros((1, LANES), F32)
    for b in range(8):
        enter_ref[0, b : b + 1, :] = sr
        enter_ref[1, b : b + 1, :] = si
        br = qr[b : b + 1, :]
        bi = qi[b : b + 1, :]
        sr, si = (
            br * sr - bi * si + wr[b : b + 1, :],
            br * si + bi * sr + wi[b : b + 1, :],
        )
    row = lax.broadcasted_iota(jnp.int32, (8, LANES), 0)
    tile = jnp.where(row == 0, sr, jnp.where(row == 1, si, 0.0))
    tile = jnp.where(row == 2, whole_ref[0:1, :], jnp.where(row == 3, whole_ref[1:2, :], tile))
    for k in range(send_ref.shape[0]):
        send_ref[k] = tile


def local_recurrence(parts, cr, ci, qr, qi, whole, groups):
    count, steps = len(parts), parts[0].shape[0]
    inner = steps // 8
    return pl.pallas_call(
        local_kernel,
        out_shape=(
            jax.ShapeDtypeStruct((inner, 8, LANES), F32),
            jax.ShapeDtypeStruct((2, 8, LANES), F32),
            jax.ShapeDtypeStruct((groups, 8, LANES), F32),
        ),
        in_specs=[vmem()] * (count + 5),
        out_specs=(vmem(),) * 3,
        scratch_shapes=[pltpu.VMEM((2, steps, HALF), F32)],
        cost_estimate=cost(steps * LANES * 16, steps * LANES * (2 * count + 12)),
        name="local_recurrence",
    )(*parts, cr, ci, qr, qi, whole)


def history_kernel(got_ref, enter_ref, pre_ref, w_ref, qr_ref, qi_ref, history_ref, out_ref, hist_ref):
    inner = w_ref.shape[0]
    mine = lax.axis_index(TM)
    sr = jnp.zeros((1, LANES), F32)
    si = jnp.zeros((1, LANES), F32)
    for k in range(got_ref.shape[0] - 1):
        tile = got_ref[k]
        br, bi, ar, ai = (tile[r : r + 1, :] for r in range(4))
        nr = ar * sr - ai * si + br
        ni = ar * si + ai * sr + bi
        take = mine > k
        sr = jnp.where(take, nr, sr)
        si = jnp.where(take, ni, si)
    er = enter_ref[0] + pre_ref[0] * sr - pre_ref[1] * si
    ei = enter_ref[1] + pre_ref[0] * si + pre_ref[1] * sr
    for j in range(inner):
        value = w_ref[j] + qr_ref[j] * er - qi_ref[j] * ei
        for h in range(2):
            hist_ref[h, pl.ds(j, 8, stride=inner), :] = value[:, h * HALF : (h + 1) * HALF]
    natural = jnp.concatenate([hist_ref[h] for h in range(2)], axis=1)
    history_ref[...] = natural
    rounded = natural.astype(BF16)
    for k in range(out_ref.shape[0]):
        out_ref[k] = rounded


def make_history(got, enter, pre, w, qr, qi, copies):
    inner = w.shape[0]
    steps = inner * 8
    return pl.pallas_call(
        history_kernel,
        out_shape=(
            jax.ShapeDtypeStruct((steps, LANES), F32),
            jax.ShapeDtypeStruct((copies, steps, LANES), BF16),
        ),
        in_specs=[vmem()] * 6,
        out_specs=(vmem(), vmem()),
        scratch_shapes=[pltpu.VMEM((2, steps, HALF), F32)],
        cost_estimate=cost(steps * LANES * 4, steps * LANES * 18),
        name="make_history",
    )(got, enter, pre, w, qr, qi)


def turn_kernel(natural_ref, out_ref):
    for h in range(2):
        part = slice(h * HALF, (h + 1) * HALF)
        out_ref[part, :] = natural_ref[:, part].T


def turn_history(natural):
    steps, lanes = natural.shape
    return pl.pallas_call(
        turn_kernel,
        out_shape=jax.ShapeDtypeStruct((lanes, steps), F32),
        in_specs=[vmem()],
        out_specs=vmem(),
        cost_estimate=cost(steps * lanes, steps * lanes * 8),
        name="turn_history",
    )(natural)


def field_kernel(which_ref, held_ref, shapes_ref, *refs):
    out_ref = refs[-1]
    total = None
    for i in range(held_ref.shape[0]):
        part = jnp.dot(held_ref[i], shapes_ref[i, 0], preferred_element_type=F32)
        total = part if total is None else total + part
    if len(refs) == 2:
        total = total + refs[0][...]
    out_ref[...] = total.astype(out_ref.dtype)


def add_field(which, held, shapes, before=None):
    count, steps, _ = held.shape
    points = shapes.shape[1]
    wide = 512
    view = shapes.reshape(count, 2, LANES, points)
    result = pl.BlockSpec((steps, wide), lambda n, c: (0, n))
    extra = [] if before is None else [before]
    return pl.pallas_call(
        field_kernel,
        out_shape=jax.ShapeDtypeStruct((steps, points), F32 if before is None else BF16),
        grid_spec=pltpu.PrefetchScalarGridSpec(
            num_scalar_prefetch=1,
            grid=(points // wide,),
            in_specs=[
                pl.BlockSpec((count, steps, LANES), lambda n, c: (0, 0, 0)),
                pl.BlockSpec((count, 1, LANES, wide), lambda n, c: (0, c[0], 0, n)),
            ]
            + [result] * len(extra),
            out_specs=result,
        ),
        compiler_params=pltpu.CompilerParams(vmem_limit_bytes=BIG),
        cost_estimate=cost(2 * count * LANES * steps * points, 2 * count * LANES * points),
        name="add_field",
    )(which, held, view, *extra)


def step_pairs(dx, dy):
    nx, ny = 4, 2
    return [
        (x * ny + y, (x + dx) % nx * ny + (y + dy) % ny) for x in range(nx) for y in range(ny)
    ]


def body(loads, phi, load_index, damping, frequency, gains, shapes):
    steps = loads.shape[0]
    inner = steps // 8
    groups = lax.axis_size(TM)
    core = lax.axis_index("core").astype(jnp.int32)
    x = lax.axis_index("x").astype(jnp.int32)
    y = lax.axis_index("yl").astype(jnp.int32)
    pair = [(0, 1), (1, 0)]
    ahead = jnp.stack([((x + dx) % 4) * 2 + (y + dy) % 2 for dx, dy in STEPS])

    theirs, ours = 2 * ahead + 1 - core, 2 * ahead + core
    phi = pltpu.with_memory_space_constraint(phi, pltpu.HBM)
    scat, *sent = open_partial(theirs, load_index.reshape(1, -1), loads, phi, FIRST + LAST)
    mates = [lax.ppermute(part, "core", pair) for part in sent]
    first, last = mates[:4], mates[4:]
    parts = []
    for chosen, mates in ((FIRST, first), (LAST, last)):
        summed = more_partial(ours, scat, phi, chosen, mates)
        for q, part in zip(chosen, summed):
            here = STEPS[q] == (0, 0)
            parts.append(part if here else lax.ppermute(part, XY, step_pairs(*STEPS[q])))

    radius = jnp.exp(-damping)
    drive = jnp.sqrt(-jnp.expm1(-2.0 * damping))
    nothing = jnp.zeros_like(drive)
    rows = jnp.stack(
        [radius * jnp.cos(frequency), radius * jnp.sin(frequency), drive] + [nothing] * 5
    )
    gain_blocks = jnp.broadcast_to(gains.reshape(8, inner).T[:, :, None], (inner, 8, HALF))

    cr, ci, qr, qi, pre, whole = coefficients(gain_blocks, rows)
    w, enter, payload = local_recurrence(parts, cr, ci, qr, qi, whole, groups)
    states = lax.all_to_all(payload, TM, 0, 0)
    natural, out = make_history(states, enter, pre, w, qr, qi, lax.axis_size(XY))
    near = lax.all_to_all(out, XY, 0, 0)
    history = turn_history(natural)
    far = lax.ppermute(near, "core", pair)
    which = core.reshape(1)
    field = add_field(which, near, shapes)
    field = add_field(1 - which, far, shapes, field)
    return field, history


def solution(mesh):
    grid = Mesh(mesh.devices.reshape(4, 2, 4, 2, 2), ("z", "yh", "x", "yl", "core"))
    placed = (
        P(TM, DOF),
        P(DOF, None),
        P(DOF),
        P(DOF),
        P(DOF),
        P(TM),
        P(None, DOF),
    )
    return jax.shard_map(
        body,
        mesh=grid,
        in_specs=placed,
        out_specs=(P(TM, DOF), P(DOF, TM)),
        check_vma=False,
    )
```

time: 122 us -> 99.2 us (0.81)
  waiting for transfers between devices: 29.9 us -> 5.33 us
  blocking collectives: 20.6 us -> 34.5 us
  other arithmetic: 4.71 us -> 0.05 us
  local copies, waits for them, and re-layouts: 10.6 us -> 6.08 us
  Pallas kernels: 36.4 us -> 33.2 us
    all_to_all x2 -> x0, waiting for transfers between devices: 26.9 us -> none  [the longest x1 20.2 us: body(): parts = lax.all_to_all(summed, XY, 0, 0)]
    all_to_all x1 -> x2, blocking collectives: 20.6 us -> 34.5 us  [the longest x1 20.1 us: body(): near = lax.all_to_all(out, XY, 0, 0)]
    all_to_all x2 -> x0, starting transfers between devices: 12.6 us -> none  [the longest x1 7.39 us: body(): states = lax.all_to_all(payload, TM, 0, 0)]
    ppermute x1 -> x15, starting transfers between devices: 1.42 us -> 12.7 us  [the longest x7 9.27 us: body(): lax.ppermute(part, XY, step_pairs(*STEPS[q]))]
    ppermute x1 -> x15, waiting for transfers between devices: 0.01 us -> 5.33 us  [the longest x7 5.26 us: body(): lax.ppermute(part, XY, step_pairs(*STEPS[q]))]
    unnamed x23 -> x26, local copies, waits for them, and re-layouts: 7.35 us -> 3.05 us
    convert_element_type x1 -> x0, other arithmetic: 3.4 us -> none  [body(): summed = (keep + got.astype(F32)).astype(BF16)]
    pallas_call x6 -> x8, Pallas kernels: 34.3 us -> 31 us  [the longest x2 13.8 us: add_field(): pl.pallas_call(field_kernel, out_shape=jax.ShapeDtypeStruct((steps, point...]
  transfers between devices with their start and end apart: 4 -> 16, of which waited for: 3 -> 2; matrix products, arithmetic and copies ran while one was open for 1% -> 3% of each run, Pallas kernels for 9% -> 16%
where the time goes in v2:
time: 99.2 us; the launch traced here: 98.5 us
  blocking collectives  34.5 us (35%)
  Pallas kernels  33.2 us (33%)
  starting transfers between devices  18.5 us (19%)
  local copies, waits for them, and re-layouts  6.08 us (6%)
  waiting for transfers between devices  5.33 us (5%)
    all_to_all x1, blocking collectives, body(): near = lax.all_to_all(out, XY, 0, 0)  20.1 us
    all_to_all x1, blocking collectives, body(): states = lax.all_to_all(payload, TM, 0, 0)  14.5 us
    pallas_call x2, Pallas kernels, add_field(): pl.pallas_call(field_kernel, out_shape=jax.ShapeDtypeStruct((steps, point...  13.8 us
    ppermute x7, starting transfers between devices, body(): lax.ppermute(part, XY, step_pairs(*STEPS[q]))  9.27 us
    ppermute x1, starting transfers between devices, body(): far = lax.ppermute(near, 'core', pair)  5.8 us
    pallas_call x2, Pallas kernels, more_partial(): pl.pallas_call(lambda *refs: more_kernel(chosen, len(got), *refs), out_sh...  5.45 us
    ppermute x7, waiting for transfers between devices, body(): lax.ppermute(part, XY, step_pairs(*STEPS[q]))  5.26 us
    pallas_call x1, Pallas kernels, open_partial(): pl.pallas_call(lambda *refs: open_kernel(chosen, *refs), out_shape=(jax.S...  3.85 us
  transfers between devices with their start and end apart: 16, of which 2 were waited for; matrix products, arithmetic and copies ran while one was open for 3% of the time, Pallas kernels for 16%

profile of v2, /device:TPU:1, one launch (start us, length us, event | category | flops | bytes accessed | tf_op | source)
XLA Modules:
  0.0 98.5 jit_solution(7602467451085589381)
XLA Ops:
  0.7 0.1 stack.50
  0.8 1.0 %copy-done = bf16[384,512]{1,0:T(8,128)(2,1)S(1)} copy-done((bf16[384,512]{1,0:T(8,128)(2,1)S(1)}, bf16[384,512]{1,0:T(8,128)(2,1)}, u32[]{:S(2)}) %copy-start) | copy-done | bytes 393240
  1.8 0.7 copy-done.2
  2.5 3.9 %open_partial.1 = (bf16[384,768]{1,0:T(8,128)(2,1)S(1)}, bf16[384,256]{1,0:T(8,128)(2,1)S(1)}, bf16[384,256]{1,0:T(8,128)(2,1)S(1)}, bf16[384,256]{1,0:T(8,128)(...) custom-call(s32[8]{0:T(128)S(1)} %get-tuple-element.61.refs_0_, ...), custom_call_target="tpu_custom_call" | custom-call | flops 1509949440 | bytes 3145728 | tf_op jit(solution)/shard_map/open_partial/pallas_call | solution.py:88
  6.3 1.5 %collective-permute-start = (bf16[384,256]{1,0:T(8,128)(2,1)S(1)}, bf16[384,256]{1,0:T(8,128)(2,1)S(1)}, u32[]{:S(2)}, u32[]{:S(2)}) collective-permute-start(bf16[384,256]{1,0:T(8,128)(2,1)S(1)} %get-tuple-element.31), channel_id=1, source_target_pairs={{0,1},{1,0},{2,3},{3,2},{4,5},{5,4},{6,7},{7,6},{8,9},{9,8},{10,11... | collective-permute-start | bytes 589832 | tf_op jit(solution)/shard_map/ppermute | solution.py:353
  7.8 0.1 collective-permute-start.1
  7.9 0.4 collective-permute-start.2
  8.3 0.1 collective-permute-start.3
  8.4 0.4 collective-permute-start.8
  8.9 0.0 collective-permute-done.refs_3_
  8.9 0.4 collective-permute-start.9
  9.3 0.0 collective-permute-done.1.refs_4_
  9.3 0.3 collective-permute-start.10
  9.6 0.0 collective-permute-done.2.refs_5_
  9.6 0.3 collective-permute-start.11
  9.8 0.0 collective-permute-done.3.refs_6_
  9.8 2.7 %more_partial.2 = (bf16[384,256]{1,0:T(8,128)(2,1)S(1)}, bf16[384,256]{1,0:T(8,128)(2,1)S(1)}, bf16[384,256]{1,0:T(8,128)(2,1)S(1)}, bf16[384,256]{1,0:T(8,128)(2,1)S(1)}) custom-call(s32[8]{0:T(128)S(1)} %get-tuple-element.62.refs_0_, bf16[384,768]{1,0:T(8,128)(2,1)S(1)} %get-tuple-element.30.refs_1_, bf16[768,4096]{1,0:T(8,128)(2,1)} %refs_2_.5, ...), custom_call_target="tpu_custom_call" | custom-call | flops 603979776 | bytes 1572864 | tf_op jit(solution)/shard_map/more_partial/pallas_call | solution.py:109
  12.6 1.4 %collective-permute-start.4 = (bf16[384,256]{1,0:T(8,128)(2,1)S(1)}, bf16[384,256]{1,0:T(8,128)(2,1)S(1)}, u32[]{:S(2)}, u32[]{:S(2)}) collective-permute-start(bf16[384,256]{1,0:T(8,128)(2,1)S(1)} %get-tuple-element.35), channel_id=1, source_target_pairs={{0,4},{2,6},{4,8},{6,10},{8,12},{10,14},{12,0},{14,2},{1,5},{3,7},... | collective-permute-start | bytes 589832 | tf_op jit(solution)/shard_map/ppermute | solution.py:360
  13.9 0.0 collective-permute-done.8.refs_3_
  13.9 1.4 %collective-permute-start.5 = (bf16[384,256]{1,0:T(8,128)(2,1)S(1)}, bf16[384,256]{1,0:T(8,128)(2,1)S(1)}, u32[]{:S(2)}, u32[]{:S(2)}) collective-permute-start(bf16[384,256]{1,0:T(8,128)(2,1)S(1)} %get-tuple-element.36), channel_id=1, source_target_pairs={{0,12},{2,14},{4,0},{6,2},{8,4},{10,6},{12,8},{14,10},{1,13},{3,15... | collective-permute-start | bytes 589832 | tf_op jit(solution)/shard_map/ppermute | solution.py:360
  15.3 0.1 reshape.20
  15.4 0.7 copy.9
  16.1 0.0 collective-permute-done.9.refs_4_
  16.1 1.6 %collective-permute-start.6 = (bf16[384,256]{1,0:T(8,128)(2,1)S(1)}, bf16[384,256]{1,0:T(8,128)(2,1)S(1)}, u32[]{:S(2)}, u32[]{:S(2)}) collective-permute-start(bf16[384,256]{1,0:T(8,128)(2,1)S(1)} %get-tuple-element.37), channel_id=1, source_target_pairs={{0,8},{2,10},{4,12},{6,14},{8,0},{10,2},{12,4},{14,6},{1,9},{3,11}... | collective-permute-start | bytes 589832 | tf_op jit(solution)/shard_map/ppermute | solution.py:360
  17.7 0.0 collective-permute-done.10.refs_5_
  17.7 1.3 %collective-permute-start.7 = (bf16[384,256]{1,0:T(8,128)(2,1)S(1)}, bf16[384,256]{1,0:T(8,128)(2,1)S(1)}, u32[]{:S(2)}, u32[]{:S(2)}) collective-permute-start(bf16[384,256]{1,0:T(8,128)(2,1)S(1)} %get-tuple-element.38), channel_id=1, source_target_pairs={{0,2},{2,0},{4,6},{6,4},{8,10},{10,8},{12,14},{14,12},{1,3},{3,1},... | collective-permute-start | bytes 589832 | tf_op jit(solution)/shard_map/ppermute | solution.py:360
  19.0 0.0 collective-permute-done.11.refs_6_
  19.0 2.7 %more_partial.3 = (bf16[384,256]{1,0:T(8,128)(2,1)S(1)}, bf16[384,256]{1,0:T(8,128)(2,1)S(1)}, bf16[384,256]{1,0:T(8,128)(2,1)S(1)}, bf16[384,256]{1,0:T(8,128)(2,1)S(1)}) custom-call(s32[8]{0:T(128)S(1)} %get-tuple-element.62.refs_0_, bf16[384,768]{1,0:T(8,128)(2,1)S(1)} %get-tuple-element.30.refs_1_, bf16[768,4096]{1,0:T(8,128)(2,1)} %refs_2_.5, ...), custom_call_target="tpu_custom_call" | custom-call | flops 603979776 | bytes 1572864 | tf_op jit(solution)/shard_map/more_partial/pallas_call | solution.py:109
  21.8 0.7 copy-done.1
  22.5 0.2 collective-permute-start.12
  22.7 3.4 %collective-permute-start.13 = (bf16[384,256]{1,0:T(8,128)(2,1)S(1)}, bf16[384,256]{1,0:T(8,128)(2,1)S(1)}, u32[]{:S(2)}, u32[]{:S(2)}) collective-permute-start(bf16[384,256]{1,0:T(8,128)(2,1)S(1)} %get-tuple-element.44), channel_id=1, source_target_pairs={{0,14},{2,12},{4,2},{6,0},{8,6},{10,4},{12,10},{14,8},{1,15},{3,13... | collective-permute-start | bytes 589832 | tf_op jit(solution)/shard_map/ppermute | solution.py:360
  26.0 0.0 collective-permute-done.5.refs_1_
  26.0 0.0 collective-permute-start.14
  26.1 0.6 stack.55.rows_ref
  26.8 1.6 %broadcast_in_dim.2.gain_ref = f32[48,8,128]{2,1,0:T(8,128)} broadcast(f32[48,8]{1,0:T(8,128)} %copy.9), dimensions={0,1} | broadcast | bytes 198144 | tf_op jit(solution)/shard_map/broadcast_in_dim | solution.py:368
  28.3 2.2 %coefficients.1 = (f32[48,8,256]{2,1,0:T(8,128)}, f32[48,8,256]{2,1,0:T(8,128)}, f32[48,8,256]{2,1,0:T(8,128)}, f32[48,8,256]{2,1,0:T(8,128)}, f32[2,8,256]{2,1,0:T(8,128)}, /*index=5*/f32[8,256]{1,0:T(8,128)}) custom-call(f32[48,8,128]{2,1,0:T(8,128)} %broadcast_in_dim.2.gain_ref, f32[8,256]{1,0:T(8,128)} %stack.55.rows_ref), custom_call_target="tpu_custom_call" | custom-call | flops 786432 | bytes 1966080 | tf_op jit(solution)/shard_map/coefficients/pallas_call | solution.py:156
  30.5 0.0 collective-permute-done.7.refs_3_
  30.5 0.7 collective-permute-done.12.refs_4_
  31.2 4.6 %collective-permute-done.14.refs_6_ = bf16[384,256]{1,0:T(8,128)(2,1)S(1)} collective-permute-done((bf16[384,256]{1,0:T(8,128)(2,1)S(1)}, bf16[384,256]{1,0:T(8,128)(2,1)S(1)}, u32[]{:S(2)}, u32[]{:S(2)}) %collective-permute-start.14) | collective-permute-done | bytes 196640 | tf_op jit(solution)/shard_map/ppermute | solution.py:360
  35.8 0.7 copy-done.9
  36.5 3.1 %local_recurrence.1 = (f32[48,8,256]{2,1,0:T(8,128)}, f32[2,8,256]{2,1,0:T(8,128)}, f32[8,8,256]{2,1,0:T(8,128)}) custom-call(bf16[384,256]{1,0:T(8,128)(2,1)} %copy-done.3, bf16[384,256]{1,0:T(8,128)(2,1)} %copy-done.4, bf16[384,256]{1,0:T(8,128)(2,1)} %copy-done.5, bf16[384,256]{1,0:T(8,128)(2,1)} %copy-done.6, bf16[384,256]{1,0:T(8,128)(2,1)} %copy-done.7, ...), custom_call_target="tpu_custom_call" | custom-call | flops 1572864 | bytes 2752512 | tf_op jit(solution)/shard_map/local_recurrence/pallas_call | solution.py:220
  39.6 14.5 %all_to_all.10.got_ref = f32[8,8,256]{2,1,0:T(8,128)} all-to-all(f32[8,8,256]{2,1,0:T(8,128)} %get-tuple-element.52), channel_id=1, replica_groups=mesh['z'=4,'yh'=2,'x'=4,'yl'=2,'core'=2] {'z','yh'}, dimensions={0} | all-to-all | bytes 131072 | tf_op jit(solution)/shard_map/all_to_all | solution.py:372
  54.0 2.9 %make_history.1 = (f32[384,256]{1,0:T(8,128)}, bf16[8,384,256]{2,1,0:T(8,128)(2,1)}) custom-call(f32[8,8,256]{2,1,0:T(8,128)} %all_to_all.10.got_ref, f32[2,8,256]{2,1,0:T(8,128)} %get-tuple-element.53.enter_ref, f32[2,8,256]{2,1,0:T(8,128)} %get-tuple-element.54.pre_ref, f32[48,8,256]{2,1,0:T(8,128)} %get-tuple-element.55.w_ref, ...), custom_call_target="tpu_custom_call" | custom-call | flops 393216 | bytes 1769472 | tf_op jit(solution)/shard_map/make_history/pallas_call | solution.py:264
  56.9 20.1 %all_to_all.11.held_ref = bf16[8,384,256]{2,1,0:T(8,128)(2,1)S(1)} all-to-all(bf16[8,384,256]{2,1,0:T(8,128)(2,1)} %get-tuple-element.56), channel_id=1, replica_groups=mesh['z'=4,'yh'=2,'x'=4,'yl'=2,'core'=2] {'x','yl'}, dimensions={0} | all-to-all | bytes 3145728 | tf_op jit(solution)/shard_map/all_to_all | solution.py:374
  77.0 5.8 %collective-permute-start.15 = (bf16[8,384,256]{2,1,0:T(8,128)(2,1)S(1)}, bf16[8,384,256]{2,1,0:T(8,128)(2,1)S(1)}, u32[]{:S(2)}, u32[]{:S(2)}) collective-permute-start(bf16[8,384,256]{2,1,0:T(8,128)(2,1)S(1)} %all_to_all.11.held_ref), channel_id=1, source_target_pairs={{0,1},{1,0},{2,3},{3,2},{4,5},{5,4},{6,7},{7,6},{8,9},{9,8},{10,11... | collective-permute-start | bytes 4718600 | tf_op jit(solution)/shard_map/ppermute | solution.py:376
  82.8 1.9 %turn_history.1 = f32[256,384]{1,0:T(8,128)} custom-call(f32[384,256]{1,0:T(8,128)} %get-tuple-element.57.natural_ref), custom_call_target="tpu_custom_call" | custom-call | flops 98304 | bytes 786432 | tf_op jit(solution)/shard_map/turn_history/pallas_call | solution.py:286
  84.7 6.5 %add_field.2.refs_0_ = f32[384,2048]{1,0:T(8,128)S(1)} custom-call(s32[1]{0:T(128)} %bitcast.which_ref, bf16[8,384,256]{2,1,0:T(8,128)(2,1)S(1)} %all_to_all.11.held_ref, bf16[8,2,256,2048]{3,2,1,0:T(8,128)(2,1)} %bitcast.16), custom_call_target="tpu_custom_call" | custom-call | flops 3221225472 | bytes 8388608 | tf_op jit(solution)/shard_map/add_field/pallas_call | solution.py:314
  91.2 7.3 %add_field.3 = bf16[384,2048]{1,0:T(8,128)(2,1)} custom-call(s32[1]{0:T(128)S(6)} %sub.7.which_ref, bf16[8,384,256]{2,1,0:T(8,128)(2,1)S(1)} %collective-permute-done.15.held_ref, bf16[8,2,256,2048]{3,2,1,0:T(8,128)(2,1)} %bitcast.17, f32[384,2048]{1,0:T(8,128)S(1)} %add_field.2.refs_0_), custom_call_target="tpu_custom_call" | custom-call | flops 3221225472 | bytes 8388608 | tf_op jit(solution)/shard_map/add_field/pallas_call | solution.py:314
  (30 shorter events, 0.1 us)
Async XLA Ops:
  0.8 1.0 %copy-start = (bf16[384,512]{1,0:T(8,128)(2,1)S(1)}, bf16[384,512]{1,0:T(8,128)(2,1)}, u32[]{:S(2)}) copy-start(bf16[384,512]{1,0:T(8,128)(2,1)} %refs_2_.3) | copy-start | bytes 1179652
  1.8 0.7 copy-start.2
  6.3 2.6 %collective-permute-start = (bf16[384,256]{1,0:T(8,128)(2,1)S(1)}, bf16[384,256]{1,0:T(8,128)(2,1)S(1)}, u32[]{:S(2)}, u32[]{:S(2)}) collective-permute-start(bf16[384,256]{1,0:T(8,128)(2,1)S(1)} %get-tuple-element.31), channel_id=1, source_target_pairs={{0,1},{1,0},{2,3},{3,2},{4,5},{5,4},{6,7},{7,6},{8,9},{9,8},{10,11... | collective-permute-start | bytes 589832 | tf_op jit(solution)/shard_map/ppermute | solution.py:353
  7.8 1.4 %collective-permute-start.1 = (bf16[384,256]{1,0:T(8,128)(2,1)S(1)}, bf16[384,256]{1,0:T(8,128)(2,1)S(1)}, u32[]{:S(2)}, u32[]{:S(2)}) collective-permute-start(bf16[384,256]{1,0:T(8,128)(2,1)S(1)} %get-tuple-element.32), channel_id=1, source_target_pairs={{0,1},{1,0},{2,3},{3,2},{4,5},{5,4},{6,7},{7,6},{8,9},{9,8},{10,11... | collective-permute-start | bytes 589832 | tf_op jit(solution)/shard_map/ppermute | solution.py:353
  7.9 1.6 %collective-permute-start.2 = (bf16[384,256]{1,0:T(8,128)(2,1)S(1)}, bf16[384,256]{1,0:T(8,128)(2,1)S(1)}, u32[]{:S(2)}, u32[]{:S(2)}) collective-permute-start(bf16[384,256]{1,0:T(8,128)(2,1)S(1)} %get-tuple-element.33), channel_id=1, source_target_pairs={{0,1},{1,0},{2,3},{3,2},{4,5},{5,4},{6,7},{7,6},{8,9},{9,8},{10,11... | collective-permute-start | bytes 589832 | tf_op jit(solution)/shard_map/ppermute | solution.py:353
  8.3 1.5 %collective-permute-start.3 = (bf16[384,256]{1,0:T(8,128)(2,1)S(1)}, bf16[384,256]{1,0:T(8,128)(2,1)S(1)}, u32[]{:S(2)}, u32[]{:S(2)}) collective-permute-start(bf16[384,256]{1,0:T(8,128)(2,1)S(1)} %get-tuple-element.34), channel_id=1, source_target_pairs={{0,1},{1,0},{2,3},{3,2},{4,5},{5,4},{6,7},{7,6},{8,9},{9,8},{10,11... | collective-permute-start | bytes 589832 | tf_op jit(solution)/shard_map/ppermute | solution.py:353
  8.4 5.5 %collective-permute-start.8 = (bf16[384,256]{1,0:T(8,128)(2,1)S(1)}, bf16[384,256]{1,0:T(8,128)(2,1)S(1)}, u32[]{:S(2)}, u32[]{:S(2)}) collective-permute-start(bf16[384,256]{1,0:T(8,128)(2,1)S(1)} %get-tuple-element.39), channel_id=1, source_target_pairs={{0,1},{1,0},{2,3},{3,2},{4,5},{5,4},{6,7},{7,6},{8,9},{9,8},{10,11... | collective-permute-start | bytes 589832 | tf_op jit(solution)/shard_map/ppermute | solution.py:353
  8.9 7.2 %collective-permute-start.9 = (bf16[384,256]{1,0:T(8,128)(2,1)S(1)}, bf16[384,256]{1,0:T(8,128)(2,1)S(1)}, u32[]{:S(2)}, u32[]{:S(2)}) collective-permute-start(bf16[384,256]{1,0:T(8,128)(2,1)S(1)} %get-tuple-element.40), channel_id=1, source_target_pairs={{0,1},{1,0},{2,3},{3,2},{4,5},{5,4},{6,7},{7,6},{8,9},{9,8},{10,11... | collective-permute-start | bytes 589832 | tf_op jit(solution)/shard_map/ppermute | solution.py:353
  9.3 8.4 %collective-permute-start.10 = (bf16[384,256]{1,0:T(8,128)(2,1)S(1)}, bf16[384,256]{1,0:T(8,128)(2,1)S(1)}, u32[]{:S(2)}, u32[]{:S(2)}) collective-permute-start(bf16[384,256]{1,0:T(8,128)(2,1)S(1)} %get-tuple-element.41), channel_id=1, source_target_pairs={{0,1},{1,0},{2,3},{3,2},{4,5},{5,4},{6,7},{7,6},{8,9},{9,8},{10,11... | collective-permute-start | bytes 589832 | tf_op jit(solution)/shard_map/ppermute | solution.py:353
  9.6 9.5 %collective-permute-start.11 = (bf16[384,256]{1,0:T(8,128)(2,1)S(1)}, bf16[384,256]{1,0:T(8,128)(2,1)S(1)}, u32[]{:S(2)}, u32[]{:S(2)}) collective-permute-start(bf16[384,256]{1,0:T(8,128)(2,1)S(1)} %get-tuple-element.42), channel_id=1, source_target_pairs={{0,1},{1,0},{2,3},{3,2},{4,5},{5,4},{6,7},{7,6},{8,9},{9,8},{10,11... | collective-permute-start | bytes 589832 | tf_op jit(solution)/shard_map/ppermute | solution.py:353
  9.8 5.5 %copy-start.10 = (f32[384]{0:T(512)S(1)}, f32[384]{0:T(512)}, u32[]{:S(2)}) copy-start(f32[384]{0:T(512)} %param.12) | copy-start | bytes 4612
  12.6 10.1 %collective-permute-start.4 = (bf16[384,256]{1,0:T(8,128)(2,1)S(1)}, bf16[384,256]{1,0:T(8,128)(2,1)S(1)}, u32[]{:S(2)}, u32[]{:S(2)}) collective-permute-start(bf16[384,256]{1,0:T(8,128)(2,1)S(1)} %get-tuple-element.35), channel_id=1, source_target_pairs={{0,4},{2,6},{4,8},{6,10},{8,12},{10,14},{12,0},{14,2},{1,5},{3,7},... | collective-permute-start | bytes 589832 | tf_op jit(solution)/shard_map/ppermute | solution.py:360
  13.9 12.1 %collective-permute-start.5 = (bf16[384,256]{1,0:T(8,128)(2,1)S(1)}, bf16[384,256]{1,0:T(8,128)(2,1)S(1)}, u32[]{:S(2)}, u32[]{:S(2)}) collective-permute-start(bf16[384,256]{1,0:T(8,128)(2,1)S(1)} %get-tuple-element.36), channel_id=1, source_target_pairs={{0,12},{2,14},{4,0},{6,2},{8,4},{10,6},{12,8},{14,10},{1,13},{3,15... | collective-permute-start | bytes 589832 | tf_op jit(solution)/shard_map/ppermute | solution.py:360
  16.1 14.4 %collective-permute-start.6 = (bf16[384,256]{1,0:T(8,128)(2,1)S(1)}, bf16[384,256]{1,0:T(8,128)(2,1)S(1)}, u32[]{:S(2)}, u32[]{:S(2)}) collective-permute-start(bf16[384,256]{1,0:T(8,128)(2,1)S(1)} %get-tuple-element.37), channel_id=1, source_target_pairs={{0,8},{2,10},{4,12},{6,14},{8,0},{10,2},{12,4},{14,6},{1,9},{3,11}... | collective-permute-start | bytes 589832 | tf_op jit(solution)/shard_map/ppermute | solution.py:360
  17.7 8.4 %copy-start.11 = (f32[256]{0:T(256)S(1)}, f32[256]{0:T(256)}, u32[]{:S(2)}) copy-start(f32[256]{0:T(256)} %param.11) | copy-start | bytes 3076
  17.7 8.4 %copy-start.12 = (f32[256]{0:T(256)S(1)}, f32[256]{0:T(256)}, u32[]{:S(2)}) copy-start(f32[256]{0:T(256)} %param.10) | copy-start | bytes 3076
  17.7 12.8 %collective-permute-start.7 = (bf16[384,256]{1,0:T(8,128)(2,1)S(1)}, bf16[384,256]{1,0:T(8,128)(2,1)S(1)}, u32[]{:S(2)}, u32[]{:S(2)}) collective-permute-start(bf16[384,256]{1,0:T(8,128)(2,1)S(1)} %get-tuple-element.38), channel_id=1, source_target_pairs={{0,2},{2,0},{4,6},{6,4},{8,10},{10,8},{12,14},{14,12},{1,3},{3,1},... | collective-permute-start | bytes 589832 | tf_op jit(solution)/shard_map/ppermute | solution.py:360
  21.8 0.7 copy-start.1
  22.5 8.7 %collective-permute-start.12 = (bf16[384,256]{1,0:T(8,128)(2,1)S(1)}, bf16[384,256]{1,0:T(8,128)(2,1)S(1)}, u32[]{:S(2)}, u32[]{:S(2)}) collective-permute-start(bf16[384,256]{1,0:T(8,128)(2,1)S(1)} %get-tuple-element.43), channel_id=1, source_target_pairs={{0,6},{2,4},{4,10},{6,8},{8,14},{10,12},{12,2},{14,0},{1,7},{3,5},... | collective-permute-start | bytes 589832 | tf_op jit(solution)/shard_map/ppermute | solution.py:360
  22.7 13.1 %copy-start.3 = (bf16[384,256]{1,0:T(8,128)(2,1)}, bf16[384,256]{1,0:T(8,128)(2,1)S(1)}, u32[]{:S(2)}) copy-start(bf16[384,256]{1,0:T(8,128)(2,1)S(1)} %collective-permute-done.4.refs_0_) | copy-start | bytes 589828
  22.7 8.5 %collective-permute-start.13 = (bf16[384,256]{1,0:T(8,128)(2,1)S(1)}, bf16[384,256]{1,0:T(8,128)(2,1)S(1)}, u32[]{:S(2)}, u32[]{:S(2)}) collective-permute-start(bf16[384,256]{1,0:T(8,128)(2,1)S(1)} %get-tuple-element.44), channel_id=1, source_target_pairs={{0,14},{2,12},{4,2},{6,0},{8,6},{10,4},{12,10},{14,8},{1,15},{3,13... | collective-permute-start | bytes 589832 | tf_op jit(solution)/shard_map/ppermute | solution.py:360
  26.0 9.7 %copy-start.4 = (bf16[384,256]{1,0:T(8,128)(2,1)}, bf16[384,256]{1,0:T(8,128)(2,1)S(1)}, u32[]{:S(2)}) copy-start(bf16[384,256]{1,0:T(8,128)(2,1)S(1)} %collective-permute-done.5.refs_1_) | copy-start | bytes 589828
  26.0 9.7 %collective-permute-start.14 = (bf16[384,256]{1,0:T(8,128)(2,1)S(1)}, bf16[384,256]{1,0:T(8,128)(2,1)S(1)}, u32[]{:S(2)}, u32[]{:S(2)}) collective-permute-start(bf16[384,256]{1,0:T(8,128)(2,1)S(1)} %get-tuple-element.45), channel_id=1, source_target_pairs={{0,10},{2,8},{4,14},{6,12},{8,2},{10,0},{12,6},{14,4},{1,11},{3,9}... | collective-permute-start | bytes 589832 | tf_op jit(solution)/shard_map/ppermute | solution.py:360
  30.5 5.3 %copy-start.5 = (bf16[384,256]{1,0:T(8,128)(2,1)}, bf16[384,256]{1,0:T(8,128)(2,1)S(1)}, u32[]{:S(2)}) copy-start(bf16[384,256]{1,0:T(8,128)(2,1)S(1)} %collective-permute-done.6.refs_2_) | copy-start | bytes 589828
  30.5 5.3 %copy-start.6 = (bf16[384,256]{1,0:T(8,128)(2,1)}, bf16[384,256]{1,0:T(8,128)(2,1)S(1)}, u32[]{:S(2)}) copy-start(bf16[384,256]{1,0:T(8,128)(2,1)S(1)} %collective-permute-done.7.refs_3_) | copy-start | bytes 589828
  31.2 4.6 %copy-start.7 = (bf16[384,256]{1,0:T(8,128)(2,1)}, bf16[384,256]{1,0:T(8,128)(2,1)S(1)}, u32[]{:S(2)}) copy-start(bf16[384,256]{1,0:T(8,128)(2,1)S(1)} %collective-permute-done.12.refs_4_) | copy-start | bytes 589828
  31.2 4.6 %copy-start.8 = (bf16[384,256]{1,0:T(8,128)(2,1)}, bf16[384,256]{1,0:T(8,128)(2,1)S(1)}, u32[]{:S(2)}) copy-start(bf16[384,256]{1,0:T(8,128)(2,1)S(1)} %collective-permute-done.13.refs_5_) | copy-start | bytes 589828
  35.8 0.7 copy-start.9
  77.0 14.2 %collective-permute-start.15 = (bf16[8,384,256]{2,1,0:T(8,128)(2,1)S(1)}, bf16[8,384,256]{2,1,0:T(8,128)(2,1)S(1)}, u32[]{:S(2)}, u32[]{:S(2)}) collective-permute-start(bf16[8,384,256]{2,1,0:T(8,128)(2,1)S(1)} %all_to_all.11.held_ref), channel_id=1, source_target_pairs={{0,1},{1,0},{2,3},{3,2},{4,5},{5,4},{6,7},{7,6},{8,9},{9,8},{10,11... | collective-permute-start | bytes 4718600 | tf_op jit(solution)/shard_map/ppermute | solution.py:376

commit v3 on v2

v3 whole, which is shorter than its diff:
```python
import jax
import jax.numpy as jnp
from jax import lax
from jax.experimental import pallas as pl
from jax.experimental.pallas import tpu as pltpu
from jax.sharding import Mesh, PartitionSpec as P

TM = ("z", "yh")
XY = ("x", "yl")
DOF = ("x", "yl", "core")
F32 = jnp.float32
BF16 = jnp.bfloat16
LANES = 256
HALF = 128
MID = 12 * 1024 * 1024
STEPS = ((1, 0), (3, 0), (2, 0), (0, 1), (1, 1), (3, 1), (2, 1), (0, 0))


def vmem():
    return pl.BlockSpec(memory_space=pltpu.VMEM)


def cost(flops, moved):
    return pl.CostEstimate(flops=int(flops), bytes_accessed=int(moved), transcendentals=0)


def smem():
    return pl.BlockSpec(memory_space=pltpu.SMEM)


def hbm():
    return pl.BlockSpec(memory_space=pltpu.HBM)


def in_hbm(value):
    return pltpu.with_memory_space_constraint(value, pltpu.HBM)


def block_of(step, other):
    dx, dy = step
    x = lax.rem(lax.axis_index("x") + dx, 4)
    y = lax.rem(lax.axis_index("yl") + dy, 2)
    core = lax.axis_index("core")
    core = 1 - core if other else core
    return pl.multiple_of((2 * (2 * x + y) + core) * LANES, LANES)


def column_copies(steps, other, phi_ref, held_ref, sems):
    copies = []
    for q, step in enumerate(steps):
        columns = pl.ds(block_of(step, other), LANES)
        copies.append(
            pltpu.make_async_copy(phi_ref.at[:, columns], held_ref.at[q], sems.at[q])
        )
    return copies


def four_products(scat, held_ref, first):
    block = jnp.concatenate([held_ref[first + q] for q in range(4)], axis=1)
    total = jnp.dot(scat, block, preferred_element_type=F32)
    return [total[:, q * LANES : (q + 1) * LANES] for q in range(4)]


def open_kernel(index_hbm, loads_hbm, phi_ref, scat_ref, sent_ref, later_ref, kept_ref,
                index_ref, loads_ref, held_ref, sems, later_sems, kept_sems, load_sems):
    index_copy = pltpu.make_async_copy(index_hbm, index_ref, load_sems.at[0])
    loads_copy = pltpu.make_async_copy(loads_hbm, loads_ref, load_sems.at[1])
    copies = column_copies(STEPS[:4], True, phi_ref, held_ref, sems)
    after = column_copies(STEPS[4:], True, phi_ref, later_ref, later_sems)
    after += column_copies(STEPS, False, phi_ref, kept_ref, kept_sems)
    for copy in [index_copy, loads_copy] + copies + after:
        copy.start()
    rows = scat_ref.shape[1]
    channels = index_ref.shape[1]
    place = lax.broadcasted_iota(jnp.int32, (rows, channels), 0)
    index_copy.wait()
    local = index_ref[...] - lax.axis_index(DOF) * rows
    onehot = jnp.where(place == local, 1.0, 0.0).astype(BF16)
    loads_copy.wait()
    summed = lax.dot_general(
        loads_ref[...], onehot, (((1,), (1,)), ((), ())), preferred_element_type=F32
    )
    scat_ref[...] = summed.astype(BF16)
    for copy in copies:
        copy.wait()
    for q, value in enumerate(four_products(scat_ref[...], held_ref, 0)):
        sent_ref[q] = value.astype(BF16)
    for copy in after:
        copy.wait()


def open_partial(index_row, loads, phi):
    steps, channels = loads.shape
    rows = phi.shape[0]
    return pl.pallas_call(
        open_kernel,
        out_shape=(
            pltpu.VMEM((steps, rows), BF16),
            jax.ShapeDtypeStruct((4, steps, LANES), BF16),
            pltpu.VMEM((4, rows, LANES), BF16),
            pltpu.VMEM((8, rows, LANES), BF16),
        ),
        in_specs=[hbm(), hbm(), hbm()],
        out_specs=(vmem(),) * 4,
        scratch_shapes=[
            pltpu.VMEM((1, channels), jnp.int32),
            pltpu.VMEM((steps, channels), BF16),
            pltpu.VMEM((4, rows, LANES), BF16),
            pltpu.SemaphoreType.DMA((4,)),
            pltpu.SemaphoreType.DMA((4,)),
            pltpu.SemaphoreType.DMA((8,)),
            pltpu.SemaphoreType.DMA((2,)),
        ],
        cost_estimate=cost(2 * steps * rows * (channels + 4 * LANES), 32 * rows * LANES),
        compiler_params=pltpu.CompilerParams(vmem_limit_bytes=MID),
        name="open_partial",
    )(in_hbm(index_row), in_hbm(loads), in_hbm(phi))


def rest_kernel(scat_ref, later_ref, sent_ref):
    for q, value in enumerate(four_products(scat_ref[...], later_ref, 0)):
        sent_ref[q] = value.astype(BF16)


def rest_partial(scat, later):
    steps, rows = scat.shape
    return pl.pallas_call(
        rest_kernel,
        out_shape=jax.ShapeDtypeStruct((4, steps, LANES), BF16),
        in_specs=[vmem(), vmem()],
        out_specs=vmem(),
        cost_estimate=cost(8 * steps * rows * LANES, 8 * rows * LANES),
        compiler_params=pltpu.CompilerParams(vmem_limit_bytes=MID),
        name="rest_partial",
    )(scat, later)


def more_kernel(first, scat_ref, kept_ref, got_ref, *outs):
    for q, value in enumerate(four_products(scat_ref[...], kept_ref, first)):
        outs[q][...] = (value + got_ref[q].astype(F32)).astype(BF16)


def more_partial(scat, kept, first, got):
    steps, rows = scat.shape
    return pl.pallas_call(
        lambda *refs: more_kernel(first, *refs),
        out_shape=(jax.ShapeDtypeStruct((steps, LANES), BF16),) * 4,
        in_specs=[vmem()] * 3,
        out_specs=(vmem(),) * 4,
        cost_estimate=cost(8 * steps * rows * LANES, 8 * rows * LANES),
        compiler_params=pltpu.CompilerParams(vmem_limit_bytes=MID),
        name="more_partial",
    )(scat, kept, got)


def coef_kernel(gains_ref, zr_ref, zi_ref, drive_ref, shapes_ref,
                cr_ref, ci_ref, qr_ref, qi_ref, pre_ref, whole_ref, staged_ref, sems):
    tall = staged_ref.shape[0] // 8
    copies = []
    for q in range(8):
        part = pl.ds(q * tall, tall)
        copies.append(pltpu.make_async_copy(shapes_ref.at[part], staged_ref.at[part], sems.at[q]))
    for copy in copies:
        copy.start()
    steps = gains_ref.shape[1]
    inner = steps // 8
    row = lax.broadcasted_iota(jnp.int32, (steps, steps), 0)
    wanted = lax.rem(row, 8) * inner + lax.div(row, 8)
    hit = lax.broadcasted_iota(jnp.int32, (steps, steps), 1) == wanted
    left = gains_ref[...]
    gain_all = jnp.zeros((steps, LANES), F32)
    ones = jnp.ones((steps, LANES), BF16)
    for _ in range(3):
        term = left.astype(BF16)
        left = left - term.astype(F32)
        chosen = jnp.where(hit, term.astype(F32), 0.0).astype(BF16)
        gain_all = gain_all + jnp.dot(chosen, ones, preferred_element_type=F32)
    zr = zr_ref[...]
    zi = zi_ref[...]
    qr = jnp.ones((8, LANES), F32)
    qi = jnp.zeros((8, LANES), F32)
    for j in range(inner):
        gain = gain_all[8 * j : 8 * j + 8, :]
        cr = gain * zr
        ci = gain * zi
        cr_ref[j] = cr
        ci_ref[j] = ci
        qr, qi = qr * cr - qi * ci, qr * ci + qi * cr
        qr_ref[j] = qr
        qi_ref[j] = qi
    pr = jnp.ones((1, LANES), F32)
    pi = jnp.zeros((1, LANES), F32)
    for b in range(8):
        pre_ref[0, b : b + 1, :] = pr
        pre_ref[1, b : b + 1, :] = pi
        br = qr[b : b + 1, :]
        bi = qi[b : b + 1, :]
        pr, pi = pr * br - pi * bi, pr * bi + pi * br
    whole_ref[0:1, :] = pr
    whole_ref[1:2, :] = pi
    whole_ref[2:3, :] = drive_ref[...]
    whole_ref[3:8, :] = jnp.zeros((5, LANES), F32)
    for copy in copies:
        copy.wait()


def coefficients(gains, zr, zi, drive, shapes):
    inner = gains.shape[1] // 8
    full = jax.ShapeDtypeStruct((inner, 8, LANES), F32)
    return pl.pallas_call(
        coef_kernel,
        out_shape=(
            full,
            full,
            full,
            full,
            jax.ShapeDtypeStruct((2, 8, LANES), F32),
            jax.ShapeDtypeStruct((8, LANES), F32),
            pltpu.VMEM(shapes.shape, shapes.dtype),
        ),
        in_specs=[vmem()] * 4 + [hbm()],
        out_specs=(vmem(),) * 7,
        scratch_shapes=[pltpu.SemaphoreType.DMA((8,))],
        cost_estimate=cost(inner * 64 * LANES, 2 * shapes.size),
        compiler_params=pltpu.CompilerParams(vmem_limit_bytes=MID),
        name="coefficients",
    )(gains, zr, zi, drive, in_hbm(shapes))


def local_kernel(*refs):
    parts = refs[:-9]
    cr_ref, ci_ref, qr_ref, qi_ref, whole_ref, w_ref, enter_ref, send_ref, push_ref = refs[-9:]
    steps = parts[0].shape[0]
    inner = steps // 8
    drive = whole_ref[2:3, :]
    tile = 64
    for s in range(0, steps, tile):
        total = parts[0][s : s + tile, :].astype(F32)
        for part in parts[1:]:
            total += part[s : s + tile, :].astype(F32)
        total = total * drive
        for h in range(2):
            push_ref[h, s : s + tile, :] = total[:, h * HALF : (h + 1) * HALF]
    wr = jnp.zeros((8, LANES), F32)
    wi = jnp.zeros((8, LANES), F32)
    for j in range(inner):
        push = jnp.concatenate(
            [push_ref[h, pl.ds(j, 8, stride=inner), :] for h in range(2)], axis=1
        )
        cr = cr_ref[j]
        ci = ci_ref[j]
        wr, wi = cr * wr - ci * wi + push, cr * wi + ci * wr
        w_ref[j] = wr
    qr = qr_ref[inner - 1]
    qi = qi_ref[inner - 1]
    sr = jnp.zeros((1, LANES), F32)
    si = jnp.zeros((1, LANES), F32)
    for b in range(8):
        enter_ref[0, b : b + 1, :] = sr
        enter_ref[1, b : b + 1, :] = si
        br = qr[b : b + 1, :]
        bi = qi[b : b + 1, :]
        sr, si = (
            br * sr - bi * si + wr[b : b + 1, :],
            br * si + bi * sr + wi[b : b + 1, :],
        )
    row = lax.broadcasted_iota(jnp.int32, (8, LANES), 0)
    tile = jnp.where(row == 0, sr, jnp.where(row == 1, si, 0.0))
    tile = jnp.where(row == 2, whole_ref[0:1, :], jnp.where(row == 3, whole_ref[1:2, :], tile))
    for k in range(send_ref.shape[0]):
        send_ref[k] = tile


def local_recurrence(parts, cr, ci, qr, qi, whole, groups):
    count, steps = len(parts), parts[0].shape[0]
    inner = steps // 8
    return pl.pallas_call(
        local_kernel,
        out_shape=(
            jax.ShapeDtypeStruct((inner, 8, LANES), F32),
            jax.ShapeDtypeStruct((2, 8, LANES), F32),
            jax.ShapeDtypeStruct((groups, 8, LANES), F32),
        ),
        in_specs=[vmem()] * (count + 5),
        out_specs=(vmem(),) * 3,
        scratch_shapes=[pltpu.VMEM((2, steps, HALF), F32)],
        compiler_params=pltpu.CompilerParams(vmem_limit_bytes=MID),
        cost_estimate=cost(steps * LANES * 16, steps * LANES * (2 * count + 12)),
        name="local_recurrence",
    )(*parts, cr, ci, qr, qi, whole)


def history_kernel(got_ref, enter_ref, pre_ref, w_ref, qr_ref, qi_ref, history_ref, out_ref, hist_ref):
    inner = w_ref.shape[0]
    mine = lax.axis_index(TM)
    sr = jnp.zeros((1, LANES), F32)
    si = jnp.zeros((1, LANES), F32)
    for k in range(got_ref.shape[0] - 1):
        tile = got_ref[k]
        br, bi, ar, ai = (tile[r : r + 1, :] for r in range(4))
        nr = ar * sr - ai * si + br
        ni = ar * si + ai * sr + bi
        take = mine > k
        sr = jnp.where(take, nr, sr)
        si = jnp.where(take, ni, si)
    er = enter_ref[0] + pre_ref[0] * sr - pre_ref[1] * si
    ei = enter_ref[1] + pre_ref[0] * si + pre_ref[1] * sr
    for j in range(inner):
        value = w_ref[j] + qr_ref[j] * er - qi_ref[j] * ei
        for h in range(2):
            hist_ref[h, pl.ds(j, 8, stride=inner), :] = value[:, h * HALF : (h + 1) * HALF]
    natural = jnp.concatenate([hist_ref[h] for h in range(2)], axis=1)
    history_ref[...] = natural
    rounded = natural.astype(BF16)
    for k in range(out_ref.shape[0]):
        out_ref[k] = rounded


def make_history(got, enter, pre, w, qr, qi, copies):
    inner = w.shape[0]
    steps = inner * 8
    return pl.pallas_call(
        history_kernel,
        out_shape=(
            jax.ShapeDtypeStruct((steps, LANES), F32),
            jax.ShapeDtypeStruct((copies, steps, LANES), BF16),
        ),
        in_specs=[vmem()] * 6,
        out_specs=(vmem(), vmem()),
        scratch_shapes=[pltpu.VMEM((2, steps, HALF), F32)],
        compiler_params=pltpu.CompilerParams(vmem_limit_bytes=MID),
        cost_estimate=cost(steps * LANES * 4, steps * LANES * 18),
        name="make_history",
    )(got, enter, pre, w, qr, qi)


def turn_kernel(natural_ref, out_ref):
    for h in range(2):
        part = slice(h * HALF, (h + 1) * HALF)
        out_ref[part, :] = natural_ref[:, part].T


def turn_history(natural):
    steps, lanes = natural.shape
    return pl.pallas_call(
        turn_kernel,
        out_shape=jax.ShapeDtypeStruct((lanes, steps), F32),
        in_specs=[vmem()],
        out_specs=vmem(),
        compiler_params=pltpu.CompilerParams(vmem_limit_bytes=MID),
        cost_estimate=cost(steps * lanes, steps * lanes * 8),
        name="turn_history",
    )(natural)


def field_kernel(other, held_ref, shapes_ref, *refs):
    before, out_ref = refs[:-1], refs[-1]
    core = lax.axis_index("core")
    core = 1 - core if other else core
    wide = 512
    for n in range(0, out_ref.shape[1], wide):
        across = slice(n, n + wide)
        total = before[0][:, across] if before else None
        for q in range(held_ref.shape[0]):
            place = pl.multiple_of((2 * q + core) * LANES, LANES)
            part = jnp.dot(
                held_ref[q],
                shapes_ref[pl.ds(place, LANES), across],
                preferred_element_type=F32,
            )
            total = part if total is None else total + part
        out_ref[:, across] = total.astype(out_ref.dtype)


def add_field(other, held, staged, before=None):
    count, steps, _ = held.shape
    points = staged.shape[1]
    extra = [] if before is None else [before]
    return pl.pallas_call(
        lambda *refs: field_kernel(other, *refs),
        out_shape=jax.ShapeDtypeStruct((steps, points), F32 if before is None else BF16),
        in_specs=[vmem()] * (2 + len(extra)),
        out_specs=vmem(),
        compiler_params=pltpu.CompilerParams(vmem_limit_bytes=MID),
        cost_estimate=cost(2 * count * LANES * steps * points, 2 * count * LANES * points),
        name="add_field",
    )(held, staged, *extra)


def step_pairs(dx, dy):
    nx, ny = 4, 2
    return [
        (x * ny + y, (x + dx) % nx * ny + (y + dy) % ny) for x in range(nx) for y in range(ny)
    ]


def body(loads, phi, load_index, damping, frequency, gains, shapes):
    steps = loads.shape[0]
    inner = steps // 8
    groups = lax.axis_size(TM)
    pair = [(0, 1), (1, 0)]
    scat, sent, later, kept = open_partial(load_index.reshape(1, -1), loads, phi)
    first = lax.ppermute(sent, "core", pair)
    last = lax.ppermute(rest_partial(scat, later), "core", pair)
    parts = []
    for start, mates in ((0, first), (4, last)):
        for q, part in enumerate(more_partial(scat, kept, start, mates), start):
            here = STEPS[q] == (0, 0)
            parts.append(part if here else lax.ppermute(part, XY, step_pairs(*STEPS[q])))

    radius = jnp.exp(-damping)
    zr = (radius * jnp.cos(frequency)).reshape(1, -1)
    zi = (radius * jnp.sin(frequency)).reshape(1, -1)
    drive = jnp.sqrt(-jnp.expm1(-2.0 * damping)).reshape(1, -1)
    late, parts[7] = lax.optimization_barrier((shapes, parts[7]))
    *coef, staged = coefficients(gains.reshape(1, -1), zr, zi, drive, late)
    cr, ci, qr, qi, pre, whole = coef
    w, enter, payload = local_recurrence(parts, cr, ci, qr, qi, whole, groups)
    states = lax.all_to_all(payload, TM, 0, 0)
    natural, out = make_history(states, enter, pre, w, qr, qi, lax.axis_size(XY))
    near = lax.all_to_all(out, XY, 0, 0)
    natural, near = lax.optimization_barrier((natural, near))
    far = lax.ppermute(near, "core", pair)
    history = turn_history(natural)
    field = add_field(False, near, staged)
    field = add_field(True, far, staged, field)
    return field, history


def solution(mesh):
    grid = Mesh(mesh.devices.reshape(4, 2, 4, 2, 2), ("z", "yh", "x", "yl", "core"))
    placed = (
        P(TM, DOF),
        P(DOF, None),
        P(DOF),
        P(DOF),
        P(DOF),
        P(TM),
        P(None, DOF),
    )
    return jax.shard_map(
        body,
        mesh=grid,
        in_specs=placed,
        out_specs=(P(TM, DOF), P(DOF, TM)),
        check_vma=False,
    )
```

time: 99.2 us -> 83.7 us (0.84)
  Pallas kernels: 33.2 us -> 22.2 us
  local copies, waits for them, and re-layouts: 6.08 us -> 0.02 us
  waiting for transfers between devices: 5.33 us -> 7.61 us
  starting transfers between devices: 18.5 us -> 17 us
  blocking collectives: 34.5 us -> 35.9 us
    pallas_call x5 -> x6, Pallas kernels: 23.1 us -> 14.5 us  [the longest x2 7.96 us: add_field(): pl.pallas_call(lambda *refs: field_kernel(other, *refs), out_shape=jax.Sh...]
    pallas_call x1, Pallas kernels: 2.16 us -> 6.06 us  [coefficients(): pl.pallas_call(coef_kernel, out_shape=(full, full, full, full, jax.ShapeD...]
    unnamed x26 -> x6, local copies, waits for them, and re-layouts: 3.05 us -> 0.02 us
    all_to_all x1, blocking collectives: 20.1 us -> 22.8 us  [body(): near = lax.all_to_all(out, XY, 0, 0)]
    pallas_call x1, Pallas kernels: 3.09 us -> 0.41 us  [local_recurrence(): pl.pallas_call(local_kernel, out_shape=(jax.ShapeDtypeStruct((inner, 8, L...]
    pallas_call x1, Pallas kernels: 2.89 us -> 0.35 us  [make_history(): pl.pallas_call(history_kernel, out_shape=(jax.ShapeDtypeStruct((steps, LA...]
    ppermute x8 -> x2, starting transfers between devices: 3.46 us -> 1.59 us  [the longest x1 1.5 us: body(): last = lax.ppermute(rest_partial(scat, later), 'core', pair)]
    ppermute x8 -> x2, waiting for transfers between devices: 0.07 us -> 1.82 us  [the longest x1 1.82 us: body(): last = lax.ppermute(rest_partial(scat, later), 'core', pair)]
  transfers between devices with their start and end apart: 16 -> 10, of which waited for: 2 -> 3; matrix products, arithmetic and copies ran while one was open for 3% -> 0% of each run, Pallas kernels for 16% -> 14%
where the time goes in v3:
time: 83.7 us; the launch traced here: 83.5 us
  blocking collectives  35.9 us (43%)
  Pallas kernels  22.2 us (27%)
  starting transfers between devices  17 us (20%)
  waiting for transfers between devices  7.61 us (9%)
    all_to_all x1, blocking collectives, body(): near = lax.all_to_all(out, XY, 0, 0)  22.8 us
    all_to_all x1, blocking collectives, body(): states = lax.all_to_all(payload, TM, 0, 0)  13 us
    ppermute x7, starting transfers between devices, body(): lax.ppermute(part, XY, step_pairs(*STEPS[q]))  10.6 us
    pallas_call x2, Pallas kernels, add_field(): pl.pallas_call(lambda *refs: field_kernel(other, *refs), out_shape=jax.Sh...  7.96 us
    pallas_call x1, Pallas kernels, coefficients(): pl.pallas_call(coef_kernel, out_shape=(full, full, full, full, jax.ShapeD...  6.06 us
    ppermute x7, waiting for transfers between devices, body(): lax.ppermute(part, XY, step_pairs(*STEPS[q]))  5.79 us
    ppermute x1, starting transfers between devices, body(): far = lax.ppermute(near, 'core', pair)  4.76 us
    pallas_call x1, Pallas kernels, open_partial(): pl.pallas_call(open_kernel, out_shape=(pltpu.VMEM((steps, rows), BF16), j...  4.21 us
  transfers between devices with their start and end apart: 10, of which 3 were waited for; matrix products, arithmetic and copies ran while one was open for 0% of the time, Pallas kernels for 14%

profile of v3, /device:TPU:1, one launch (start us, length us, event | category | flops | bytes accessed | tf_op | source)
XLA Modules:
  0.0 83.5 jit_solution(66606397854837281)
XLA Ops:
  0.6 4.2 %open_partial.1 = (bf16[384,768]{1,0:T(8,128)(2,1)S(1)}, bf16[4,384,256]{2,1,0:T(8,128)(2,1)S(1)}, bf16[4,768,256]{2,1,0:T(8,128)(2,1)S(1)}, bf16[8,768,256]{2,1,0:T(8,128)(2,1)S(1)}) custom-call(s32[1,512]{1,0:T(1,128)} %bitcast.7, bf16[384,512]{1,0:T(8,128)(2,1)} %loads_hbm.1, bf16[768,4096]{1,0:T(8,128)(2,1)} %phi_ref.1), custom_call_target="tpu_custom_call" | custom-call | flops 905969664 | bytes 6291456 | tf_op jit(solution)/shard_map/open_partial/pallas_call | solution.py:95
  4.8 0.0 copy-start
  4.9 0.8 rest_partial.1
  5.6 1.5 %collective-permute-start.5 = (bf16[4,384,256]{2,1,0:T(8,128)(2,1)S(1)}, bf16[4,384,256]{2,1,0:T(8,128)(2,1)S(1)}, u32[]{:S(2)}, u32[]{:S(2)}) collective-permute-start(bf16[4,384,256]{2,1,0:T(8,128)(2,1)S(1)} %rest_partial.1), channel_id=1, source_target_pairs={{0,1},{1,0},{2,3},{3,2},{4,5},{5,4},{6,7},{7,6},{8,9},{9,8},{10,11... | collective-permute-start | bytes 2359304 | tf_op jit(solution)/shard_map/ppermute | solution.py:404
  7.1 0.1 collective-permute-start
  7.2 1.8 %collective-permute-done.5.refs_2_ = bf16[4,384,256]{2,1,0:T(8,128)(2,1)S(1)} collective-permute-done((bf16[4,384,256]{2,1,0:T(8,128)(2,1)S(1)}, bf16[4,384,256]{2,1,0:T(8,128)(2,1)S(1)}, u32[]{:S(2)}, u32[]{:S(2)}) %collective-permute-start.5) | collective-permute-done | bytes 786464 | tf_op jit(solution)/shard_map/ppermute | solution.py:404
  9.1 0.8 more_partial.3
  9.8 0.0 copy-start.1
  9.8 0.0 copy-start.2
  9.9 2.4 %collective-permute-start.6 = (bf16[384,256]{1,0:T(8,128)(2,1)S(1)}, bf16[384,256]{1,0:T(8,128)(2,1)S(1)}, u32[]{:S(2)}, u32[]{:S(2)}) collective-permute-start(bf16[384,256]{1,0:T(8,128)(2,1)S(1)} %get-tuple-element.38), channel_id=1, source_target_pairs={{0,6},{2,4},{4,10},{6,8},{8,14},{10,12},{12,2},{14,0},{1,7},{3,5},... | collective-permute-start | bytes 589832 | tf_op jit(solution)/shard_map/ppermute | solution.py:409
  12.2 1.3 %collective-permute-start.7 = (bf16[384,256]{1,0:T(8,128)(2,1)S(1)}, bf16[384,256]{1,0:T(8,128)(2,1)S(1)}, u32[]{:S(2)}, u32[]{:S(2)}) collective-permute-start(bf16[384,256]{1,0:T(8,128)(2,1)S(1)} %get-tuple-element.39), channel_id=1, source_target_pairs={{0,14},{2,12},{4,2},{6,0},{8,6},{10,4},{12,10},{14,8},{1,15},{3,13... | collective-permute-start | bytes 589832 | tf_op jit(solution)/shard_map/ppermute | solution.py:409
  13.6 0.0 copy-done
  13.6 2.5 %collective-permute-start.8 = (bf16[384,256]{1,0:T(8,128)(2,1)S(1)}, bf16[384,256]{1,0:T(8,128)(2,1)S(1)}, u32[]{:S(2)}, u32[]{:S(2)}) collective-permute-start(bf16[384,256]{1,0:T(8,128)(2,1)S(1)} %get-tuple-element.40), channel_id=1, source_target_pairs={{0,10},{2,8},{4,14},{6,12},{8,2},{10,0},{12,6},{14,4},{1,11},{3,9}... | collective-permute-start | bytes 589832 | tf_op jit(solution)/shard_map/ppermute | solution.py:409
  16.1 0.0 collective-permute-done.refs_2_
  16.1 0.8 more_partial.2
  16.9 0.4 collective-permute-start.1
  17.3 2.4 %collective-permute-start.2 = (bf16[384,256]{1,0:T(8,128)(2,1)S(1)}, bf16[384,256]{1,0:T(8,128)(2,1)S(1)}, u32[]{:S(2)}, u32[]{:S(2)}) collective-permute-start(bf16[384,256]{1,0:T(8,128)(2,1)S(1)} %get-tuple-element.34), channel_id=1, source_target_pairs={{0,12},{2,14},{4,0},{6,2},{8,4},{10,6},{12,8},{14,10},{1,13},{3,15... | collective-permute-start | bytes 589832 | tf_op jit(solution)/shard_map/ppermute | solution.py:409
  19.7 0.0 collective-permute-done.6.refs_4_
  19.7 1.3 %collective-permute-start.3 = (bf16[384,256]{1,0:T(8,128)(2,1)S(1)}, bf16[384,256]{1,0:T(8,128)(2,1)S(1)}, u32[]{:S(2)}, u32[]{:S(2)}) collective-permute-start(bf16[384,256]{1,0:T(8,128)(2,1)S(1)} %get-tuple-element.35), channel_id=1, source_target_pairs={{0,8},{2,10},{4,12},{6,14},{8,0},{10,2},{12,4},{14,6},{1,9},{3,11}... | collective-permute-start | bytes 589832 | tf_op jit(solution)/shard_map/ppermute | solution.py:409
  21.0 2.3 %collective-permute-done.7.refs_5_ = bf16[384,256]{1,0:T(8,128)(2,1)S(1)} collective-permute-done((bf16[384,256]{1,0:T(8,128)(2,1)S(1)}, bf16[384,256]{1,0:T(8,128)(2,1)S(1)}, u32[]{:S(2)}, u32[]{:S(2)}) %collective-permute-start.7) | collective-permute-done | bytes 196640 | tf_op jit(solution)/shard_map/ppermute | solution.py:409
  23.2 0.3 collective-permute-start.4
  23.5 0.0 copy-done.1
  23.5 0.0 copy-done.2
  23.6 6.1 %coefficients.1 = (f32[48,8,256]{2,1,0:T(8,128)S(1)}, f32[48,8,256]{2,1,0:T(8,128)S(1)}, f32[48,8,256]{2,1,0:T(8,128)S(1)}, f32[48,8,256]{2,1,0:T(8,128)S(1)}, f...) custom-call(f32[1,384]{1,0:T(1,128)S(1)} %reshape.20.gains_ref, ...), custom_call_target="tpu_custom_call" | custom-call | flops 786432 | bytes 16777216 | tf_op jit(solution)/shard_map/coefficients/pallas_call | solution.py:210
  29.7 0.0 collective-permute-done.8.refs_6_
  29.7 0.0 collective-permute-done.1.refs_0_
  29.7 0.0 collective-permute-done.2.refs_1_
  29.7 3.5 %collective-permute-done.3.refs_2_ = bf16[384,256]{1,0:T(8,128)(2,1)S(1)} collective-permute-done((bf16[384,256]{1,0:T(8,128)(2,1)S(1)}, bf16[384,256]{1,0:T(8,128)(2,1)S(1)}, u32[]{:S(2)}, u32[]{:S(2)}) %collective-permute-start.3) | collective-permute-done | bytes 196640 | tf_op jit(solution)/shard_map/ppermute | solution.py:409
  33.2 0.0 collective-permute-done.4.refs_3_
  33.2 0.4 local_recurrence.1
  33.6 13.0 %all_to_all.10.got_ref = f32[8,8,256]{2,1,0:T(8,128)S(1)} all-to-all(f32[8,8,256]{2,1,0:T(8,128)S(1)} %get-tuple-element.49), channel_id=1, replica_groups=mesh['z'=4,'yh'=2,'x'=4,'yl'=2,'core'=2] {'z','yh'}, dimensions={0} | all-to-all | bytes 131072 | tf_op jit(solution)/shard_map/all_to_all | solution.py:419
  46.7 0.4 make_history.1
  47.0 22.8 %all_to_all.11.refs_0_ = bf16[8,384,256]{2,1,0:T(8,128)(2,1)S(1)} all-to-all(bf16[8,384,256]{2,1,0:T(8,128)(2,1)S(1)} %get-tuple-element.54), channel_id=1, replica_groups=mesh['z'=4,'yh'=2,'x'=4,'yl'=2,'core'=2] {'x','yl'}, dimensions={0} | all-to-all | bytes 3145728 | tf_op jit(solution)/shard_map/all_to_all | solution.py:421
  69.9 4.8 %collective-permute-start.9 = (bf16[8,384,256]{2,1,0:T(8,128)(2,1)S(1)}, bf16[8,384,256]{2,1,0:T(8,128)(2,1)S(1)}, u32[]{:S(2)}, u32[]{:S(2)}) collective-permute-start(bf16[8,384,256]{2,1,0:T(8,128)(2,1)S(1)} %all_to_all.11.refs_0_), channel_id=1, source_target_pairs={{0,1},{1,0},{2,3},{3,2},{4,5},{5,4},{6,7},{7,6},{8,9},{9,8},{10,11... | collective-permute-start | bytes 4718600 | tf_op jit(solution)/shard_map/ppermute | solution.py:423
  74.6 0.9 %turn_history.1 = f32[256,384]{1,0:T(8,128)} custom-call(f32[384,256]{1,0:T(8,128)S(1)} %get-tuple-element.57.natural_ref), custom_call_target="tpu_custom_call" | custom-call | flops 98304 | bytes 786432 | tf_op jit(solution)/shard_map/turn_history/pallas_call | solution.py:345
  75.5 3.4 %add_field.2.refs_2_ = f32[384,2048]{1,0:T(8,128)S(1)} custom-call(bf16[8,384,256]{2,1,0:T(8,128)(2,1)S(1)} %all_to_all.11.refs_0_, bf16[4096,2048]{1,0:T(8,128)(2,1)S(1)} %get-tuple-element.56.refs_1_), custom_call_target="tpu_custom_call" | custom-call | flops 3221225472 | bytes 8388608 | tf_op jit(solution)/shard_map/add_field/pallas_call | solution.py:379
  78.9 0.0 collective-permute-done.9.refs_0_
  78.9 4.6 %add_field.3 = bf16[384,2048]{1,0:T(8,128)(2,1)} custom-call(bf16[8,384,256]{2,1,0:T(8,128)(2,1)S(1)} %collective-permute-done.9.refs_0_, bf16[4096,2048]{1,0:T(8,128)(2,1)S(1)} %get-tuple-element.56.refs_1_, f32[384,2048]{1,0:T(8,128)S(1)} %add_field.2.refs_2_), custom_call_target="tpu_custom_call" | custom-call | flops 3221225472 | bytes 8388608 | tf_op jit(solution)/shard_map/add_field/pallas_call | solution.py:379
  (2 shorter events, 0.0 us)
Async XLA Ops:
  4.8 8.7 %copy-start = (f32[384]{0:T(512)S(1)}, f32[384]{0:T(512)}, u32[]{:S(2)}) copy-start(f32[384]{0:T(512)} %param.12) | copy-start | bytes 4612
  5.6 3.4 %collective-permute-start.5 = (bf16[4,384,256]{2,1,0:T(8,128)(2,1)S(1)}, bf16[4,384,256]{2,1,0:T(8,128)(2,1)S(1)}, u32[]{:S(2)}, u32[]{:S(2)}) collective-permute-start(bf16[4,384,256]{2,1,0:T(8,128)(2,1)S(1)} %rest_partial.1), channel_id=1, source_target_pairs={{0,1},{1,0},{2,3},{3,2},{4,5},{5,4},{6,7},{7,6},{8,9},{9,8},{10,11... | collective-permute-start | bytes 2359304 | tf_op jit(solution)/shard_map/ppermute | solution.py:404
  7.1 9.0 %collective-permute-start = (bf16[4,384,256]{2,1,0:T(8,128)(2,1)S(1)}, bf16[4,384,256]{2,1,0:T(8,128)(2,1)S(1)}, u32[]{:S(2)}, u32[]{:S(2)}) collective-permute-start(bf16[4,384,256]{2,1,0:T(8,128)(2,1)S(1)} %get-tuple-element.32), channel_id=1, source_target_pairs={{0,1},{1,0},{2,3},{3,2},{4,5},{5,4},{6,7},{7,6},{8,9},{9,8},{10,11... | collective-permute-start | bytes 2359304 | tf_op jit(solution)/shard_map/ppermute | solution.py:403
  9.8 13.7 %copy-start.1 = (f32[256]{0:T(256)S(1)}, f32[256]{0:T(256)}, u32[]{:S(2)}) copy-start(f32[256]{0:T(256)} %param.11) | copy-start | bytes 3076
  9.8 13.7 %copy-start.2 = (f32[256]{0:T(256)S(1)}, f32[256]{0:T(256)}, u32[]{:S(2)}) copy-start(f32[256]{0:T(256)} %param.10) | copy-start | bytes 3076
  9.9 9.8 %collective-permute-start.6 = (bf16[384,256]{1,0:T(8,128)(2,1)S(1)}, bf16[384,256]{1,0:T(8,128)(2,1)S(1)}, u32[]{:S(2)}, u32[]{:S(2)}) collective-permute-start(bf16[384,256]{1,0:T(8,128)(2,1)S(1)} %get-tuple-element.38), channel_id=1, source_target_pairs={{0,6},{2,4},{4,10},{6,8},{8,14},{10,12},{12,2},{14,0},{1,7},{3,5},... | collective-permute-start | bytes 589832 | tf_op jit(solution)/shard_map/ppermute | solution.py:409
  12.2 11.0 %collective-permute-start.7 = (bf16[384,256]{1,0:T(8,128)(2,1)S(1)}, bf16[384,256]{1,0:T(8,128)(2,1)S(1)}, u32[]{:S(2)}, u32[]{:S(2)}) collective-permute-start(bf16[384,256]{1,0:T(8,128)(2,1)S(1)} %get-tuple-element.39), channel_id=1, source_target_pairs={{0,14},{2,12},{4,2},{6,0},{8,6},{10,4},{12,10},{14,8},{1,15},{3,13... | collective-permute-start | bytes 589832 | tf_op jit(solution)/shard_map/ppermute | solution.py:409
  13.6 16.1 %collective-permute-start.8 = (bf16[384,256]{1,0:T(8,128)(2,1)S(1)}, bf16[384,256]{1,0:T(8,128)(2,1)S(1)}, u32[]{:S(2)}, u32[]{:S(2)}) collective-permute-start(bf16[384,256]{1,0:T(8,128)(2,1)S(1)} %get-tuple-element.40), channel_id=1, source_target_pairs={{0,10},{2,8},{4,14},{6,12},{8,2},{10,0},{12,6},{14,4},{1,11},{3,9}... | collective-permute-start | bytes 589832 | tf_op jit(solution)/shard_map/ppermute | solution.py:409
  16.9 12.7 %collective-permute-start.1 = (bf16[384,256]{1,0:T(8,128)(2,1)S(1)}, bf16[384,256]{1,0:T(8,128)(2,1)S(1)}, u32[]{:S(2)}, u32[]{:S(2)}) collective-permute-start(bf16[384,256]{1,0:T(8,128)(2,1)S(1)} %get-tuple-element.33), channel_id=1, source_target_pairs={{0,4},{2,6},{4,8},{6,10},{8,12},{10,14},{12,0},{14,2},{1,5},{3,7},... | collective-permute-start | bytes 589832 | tf_op jit(solution)/shard_map/ppermute | solution.py:409
  17.3 12.4 %collective-permute-start.2 = (bf16[384,256]{1,0:T(8,128)(2,1)S(1)}, bf16[384,256]{1,0:T(8,128)(2,1)S(1)}, u32[]{:S(2)}, u32[]{:S(2)}) collective-permute-start(bf16[384,256]{1,0:T(8,128)(2,1)S(1)} %get-tuple-element.34), channel_id=1, source_target_pairs={{0,12},{2,14},{4,0},{6,2},{8,4},{10,6},{12,8},{14,10},{1,13},{3,15... | collective-permute-start | bytes 589832 | tf_op jit(solution)/shard_map/ppermute | solution.py:409
  19.7 13.5 %collective-permute-start.3 = (bf16[384,256]{1,0:T(8,128)(2,1)S(1)}, bf16[384,256]{1,0:T(8,128)(2,1)S(1)}, u32[]{:S(2)}, u32[]{:S(2)}) collective-permute-start(bf16[384,256]{1,0:T(8,128)(2,1)S(1)} %get-tuple-element.35), channel_id=1, source_target_pairs={{0,8},{2,10},{4,12},{6,14},{8,0},{10,2},{12,4},{14,6},{1,9},{3,11}... | collective-permute-start | bytes 589832 | tf_op jit(solution)/shard_map/ppermute | solution.py:409
  23.2 10.0 %collective-permute-start.4 = (bf16[384,256]{1,0:T(8,128)(2,1)S(1)}, bf16[384,256]{1,0:T(8,128)(2,1)S(1)}, u32[]{:S(2)}, u32[]{:S(2)}) collective-permute-start(bf16[384,256]{1,0:T(8,128)(2,1)S(1)} %get-tuple-element.36), channel_id=1, source_target_pairs={{0,2},{2,0},{4,6},{6,4},{8,10},{10,8},{12,14},{14,12},{1,3},{3,1},... | collective-permute-start | bytes 589832 | tf_op jit(solution)/shard_map/ppermute | solution.py:409
  69.9 9.1 %collective-permute-start.9 = (bf16[8,384,256]{2,1,0:T(8,128)(2,1)S(1)}, bf16[8,384,256]{2,1,0:T(8,128)(2,1)S(1)}, u32[]{:S(2)}, u32[]{:S(2)}) collective-permute-start(bf16[8,384,256]{2,1,0:T(8,128)(2,1)S(1)} %all_to_all.11.refs_0_), channel_id=1, source_target_pairs={{0,1},{1,0},{2,3},{3,2},{4,5},{5,4},{6,7},{7,6},{8,9},{9,8},{10,11... | collective-permute-start | bytes 4718600 | tf_op jit(solution)/shard_map/ppermute | solution.py:423

commit v4 on v3

--- a/solution.py
+++ b/solution.py
@@ -13,7 +13,9 @@
 LANES = 256
 HALF = 128
 MID = 12 * 1024 * 1024
-STEPS = ((1, 0), (3, 0), (2, 0), (0, 1), (1, 1), (3, 1), (2, 1), (0, 0))
+DEEP = 256
+EARLY = 2
+STEPS = ((2, 1), (1, 1), (3, 0), (2, 0), (0, 1), (1, 0), (3, 1), (0, 0))
 
 
 def vmem():
@@ -36,39 +38,37 @@
     return pltpu.with_memory_space_constraint(value, pltpu.HBM)
 
 
-def block_of(step, other):
+def block_of(step, sign, other):
     dx, dy = step
-    x = lax.rem(lax.axis_index("x") + dx, 4)
+    x = lax.rem(lax.axis_index("x") + (4 + sign * dx) % 4, 4)
     y = lax.rem(lax.axis_index("yl") + dy, 2)
     core = lax.axis_index("core")
     core = 1 - core if other else core
     return pl.multiple_of((2 * (2 * x + y) + core) * LANES, LANES)
 
 
-def column_copies(steps, other, phi_ref, held_ref, sems):
-    copies = []
-    for q, step in enumerate(steps):
-        columns = pl.ds(block_of(step, other), LANES)
-        copies.append(
-            pltpu.make_async_copy(phi_ref.at[:, columns], held_ref.at[q], sems.at[q])
-        )
-    return copies
-
-
-def four_products(scat, held_ref, first):
-    block = jnp.concatenate([held_ref[first + q] for q in range(4)], axis=1)
-    total = jnp.dot(scat, block, preferred_element_type=F32)
-    return [total[:, q * LANES : (q + 1) * LANES] for q in range(4)]
-
-
-def open_kernel(index_hbm, loads_hbm, phi_ref, scat_ref, sent_ref, later_ref, kept_ref,
-                index_ref, loads_ref, held_ref, sems, later_sems, kept_sems, load_sems):
+def products(scat_ref, phi_ref, steps, other, wait=None):
+    places = [block_of(step, 1, other) for step in steps]
+    total = None
+    for k in range(0, phi_ref.shape[0], DEEP):
+        if wait is not None:
+            wait(k // DEEP)
+        rows = slice(k, k + DEEP)
+        block = jnp.concatenate([phi_ref[rows, pl.ds(place, LANES)] for place in places], axis=1)
+        part = jnp.dot(scat_ref[:, rows], block, preferred_element_type=F32)
+        total = part if total is None else total + part
+    return [total[:, q * LANES : (q + 1) * LANES] for q in range(len(steps))]
+
+
+def open_kernel(index_hbm, loads_hbm, phi_hbm, scat_ref, sent_ref, phi_ref,
+                index_ref, loads_ref, sems, load_sems):
     index_copy = pltpu.make_async_copy(index_hbm, index_ref, load_sems.at[0])
     loads_copy = pltpu.make_async_copy(loads_hbm, loads_ref, load_sems.at[1])
-    copies = column_copies(STEPS[:4], True, phi_ref, held_ref, sems)
-    after = column_copies(STEPS[4:], True, phi_ref, later_ref, later_sems)
-    after += column_copies(STEPS, False, phi_ref, kept_ref, kept_sems)
-    for copy in [index_copy, loads_copy] + copies + after:
+    copies = []
+    for q in range(phi_ref.shape[0] // DEEP):
+        part = pl.ds(q * DEEP, DEEP)
+        copies.append(pltpu.make_async_copy(phi_hbm.at[part], phi_ref.at[part], sems.at[q]))
+    for copy in [index_copy, loads_copy] + copies:
         copy.start()
     rows = scat_ref.shape[1]
     channels = index_ref.shape[1]
@@ -81,12 +81,9 @@
         loads_ref[...], onehot, (((1,), (1,)), ((), ())), preferred_element_type=F32
     )
     scat_ref[...] = summed.astype(BF16)
-    for copy in copies:
-        copy.wait()
-    for q, value in enumerate(four_products(scat_ref[...], held_ref, 0)):
+    mine = products(scat_ref, phi_ref, STEPS[:EARLY], True, lambda k: copies[k].wait())
+    for q, value in enumerate(mine):
         sent_ref[q] = value.astype(BF16)
-    for copy in after:
-        copy.wait()
 
 
 def open_partial(index_row, loads, phi):
@@ -96,61 +93,58 @@
         open_kernel,
         out_shape=(
             pltpu.VMEM((steps, rows), BF16),
-            jax.ShapeDtypeStruct((4, steps, LANES), BF16),
-            pltpu.VMEM((4, rows, LANES), BF16),
-            pltpu.VMEM((8, rows, LANES), BF16),
+            jax.ShapeDtypeStruct((EARLY, steps, LANES), BF16),
+            pltpu.VMEM(phi.shape, BF16),
         ),
         in_specs=[hbm(), hbm(), hbm()],
-        out_specs=(vmem(),) * 4,
+        out_specs=(vmem(),) * 3,
         scratch_shapes=[
             pltpu.VMEM((1, channels), jnp.int32),
             pltpu.VMEM((steps, channels), BF16),
-            pltpu.VMEM((4, rows, LANES), BF16),
-            pltpu.SemaphoreType.DMA((4,)),
-            pltpu.SemaphoreType.DMA((4,)),
-            pltpu.SemaphoreType.DMA((8,)),
+            pltpu.SemaphoreType.DMA((rows // DEEP,)),
             pltpu.SemaphoreType.DMA((2,)),
         ],
-        cost_estimate=cost(2 * steps * rows * (channels + 4 * LANES), 32 * rows * LANES),
+        cost_estimate=cost(2 * steps * rows * (channels + EARLY * LANES), 32 * rows * LANES),
         compiler_params=pltpu.CompilerParams(vmem_limit_bytes=MID),
         name="open_partial",
     )(in_hbm(index_row), in_hbm(loads), in_hbm(phi))
 
 
-def rest_kernel(scat_ref, later_ref, sent_ref):
-    for q, value in enumerate(four_products(scat_ref[...], later_ref, 0)):
+def rest_kernel(scat_ref, phi_ref, sent_ref):
+    for q, value in enumerate(products(scat_ref, phi_ref, STEPS[EARLY:], True)):
         sent_ref[q] = value.astype(BF16)
 
 
-def rest_partial(scat, later):
+def rest_partial(scat, phi):
     steps, rows = scat.shape
     return pl.pallas_call(
         rest_kernel,
-        out_shape=jax.ShapeDtypeStruct((4, steps, LANES), BF16),
+        out_shape=jax.ShapeDtypeStruct((8 - EARLY, steps, LANES), BF16),
         in_specs=[vmem(), vmem()],
         out_specs=vmem(),
         cost_estimate=cost(8 * steps * rows * LANES, 8 * rows * LANES),
         compiler_params=pltpu.CompilerParams(vmem_limit_bytes=MID),
         name="rest_partial",
-    )(scat, later)
-
-
-def more_kernel(first, scat_ref, kept_ref, got_ref, *outs):
-    for q, value in enumerate(four_products(scat_ref[...], kept_ref, first)):
+    )(scat, phi)
+
+
+def more_kernel(chosen, scat_ref, phi_ref, got_ref, *outs):
+    for q, value in enumerate(products(scat_ref, phi_ref, chosen, False)):
         outs[q][...] = (value + got_ref[q].astype(F32)).astype(BF16)
 
 
-def more_partial(scat, kept, first, got):
+def more_partial(scat, phi, chosen, got):
     steps, rows = scat.shape
-    return pl.pallas_call(
-        lambda *refs: more_kernel(first, *refs),
-        out_shape=(jax.ShapeDtypeStruct((steps, LANES), BF16),) * 4,
+    count = len(chosen)
+    return pl.pallas_call(
+        lambda *refs: more_kernel(chosen, *refs),
+        out_shape=(jax.ShapeDtypeStruct((steps, LANES), BF16),) * count,
         in_specs=[vmem()] * 3,
-        out_specs=(vmem(),) * 4,
-        cost_estimate=cost(8 * steps * rows * LANES, 8 * rows * LANES),
+        out_specs=(vmem(),) * count,
+        cost_estimate=cost(2 * count * steps * rows * LANES, 2 * count * rows * LANES),
         compiler_params=pltpu.CompilerParams(vmem_limit_bytes=MID),
         name="more_partial",
-    )(scat, kept, got)
+    )(scat, phi, got)
 
 
 def coef_kernel(gains_ref, zr_ref, zi_ref, drive_ref, shapes_ref,
@@ -334,57 +328,89 @@
     )(got, enter, pre, w, qr, qi)
 
 
-def turn_kernel(natural_ref, out_ref):
-    for h in range(2):
-        part = slice(h * HALF, (h + 1) * HALF)
-        out_ref[part, :] = natural_ref[:, part].T
-
-
-def turn_history(natural):
-    steps, lanes = natural.shape
-    return pl.pallas_call(
-        turn_kernel,
-        out_shape=jax.ShapeDtypeStruct((lanes, steps), F32),
-        in_specs=[vmem()],
-        out_specs=vmem(),
-        compiler_params=pltpu.CompilerParams(vmem_limit_bytes=MID),
-        cost_estimate=cost(steps * lanes, steps * lanes * 8),
-        name="turn_history",
-    )(natural)
-
-
-def field_kernel(other, held_ref, shapes_ref, *refs):
-    before, out_ref = refs[:-1], refs[-1]
+WIDE = 512
+
+
+def field_tiles(other, held_ref, before, shapes_ref, store):
     core = lax.axis_index("core")
     core = 1 - core if other else core
-    wide = 512
-    for n in range(0, out_ref.shape[1], wide):
-        across = slice(n, n + wide)
+    for n in range(0, shapes_ref.shape[1], WIDE):
+        across = slice(n, n + WIDE)
         total = before[0][:, across] if before else None
         for q in range(held_ref.shape[0]):
             place = pl.multiple_of((2 * q + core) * LANES, LANES)
-            part = jnp.dot(
-                held_ref[q],
-                shapes_ref[pl.ds(place, LANES), across],
-                preferred_element_type=F32,
+            product = jnp.dot(
+                held_ref[q], shapes_ref[pl.ds(place, LANES), across], preferred_element_type=F32
             )
-            total = part if total is None else total + part
-        out_ref[:, across] = total.astype(out_ref.dtype)
-
-
-def add_field(other, held, staged, before=None):
+            total = product if total is None else total + product
+        store(n, total)
+
+
+def near_kernel(held_ref, shapes_ref, natural_ref, out_ref, history_ref):
+    piece = HALF
+
+    def store(n, total):
+        out_ref[:, n : n + WIDE] = total
+        first = n // WIDE * piece
+        if first < natural_ref.shape[0]:
+            part = slice(first, first + piece)
+            for h in range(2):
+                lanes = slice(h * HALF, (h + 1) * HALF)
+                history_ref[lanes, part] = natural_ref[part, lanes].T
+
+    field_tiles(False, held_ref, [], shapes_ref, store)
+
+
+def far_kernel(held_ref, shapes_ref, before_ref, out_hbm, out_ref, sems):
+    copies = []
+
+    def store(n, total):
+        out_ref[:, n : n + WIDE] = total.astype(BF16)
+        across = pl.ds(n, WIDE)
+        copy = pltpu.make_async_copy(
+            out_ref.at[:, across], out_hbm.at[:, across], sems.at[n // WIDE]
+        )
+        copy.start()
+        copies.append(copy)
+
+    field_tiles(True, held_ref, [before_ref], shapes_ref, store)
+    for copy in copies:
+        copy.wait()
+
+
+def near_field(held, staged, natural):
+    count, steps, lanes = held.shape
+    points = staged.shape[1]
+    return pl.pallas_call(
+        near_kernel,
+        out_shape=(
+            jax.ShapeDtypeStruct((steps, points), F32),
+            jax.ShapeDtypeStruct((lanes, steps), F32),
+        ),
+        in_specs=[vmem()] * 3,
+        out_specs=(vmem(), vmem()),
+        compiler_params=pltpu.CompilerParams(vmem_limit_bytes=MID),
+        cost_estimate=cost(2 * count * LANES * steps * points, 2 * count * LANES * points),
+        name="near_field",
+    )(held, staged, natural)
+
+
+def far_field(held, staged, before):
     count, steps, _ = held.shape
     points = staged.shape[1]
-    extra = [] if before is None else [before]
-    return pl.pallas_call(
-        lambda *refs: field_kernel(other, *refs),
-        out_shape=jax.ShapeDtypeStruct((steps, points), F32 if before is None else BF16),
-        in_specs=[vmem()] * (2 + len(extra)),
-        out_specs=vmem(),
+    return pl.pallas_call(
+        far_kernel,
+        out_shape=jax.ShapeDtypeStruct((steps, points), BF16),
+        in_specs=[vmem()] * 3,
+        out_specs=hbm(),
+        scratch_shapes=[
+            pltpu.VMEM((steps, points), BF16),
+            pltpu.SemaphoreType.DMA((points // WIDE,)),
+        ],
         compiler_params=pltpu.CompilerParams(vmem_limit_bytes=MID),
         cost_estimate=cost(2 * count * LANES * steps * points, 2 * count * LANES * points),
-        name="add_field",
-    )(held, staged, *extra)
+        name="far_field",
+    )(held, staged, before)
 
 
 def step_pairs(dx, dy):
@@ -399,14 +425,16 @@
     inner = steps // 8
     groups = lax.axis_size(TM)
     pair = [(0, 1), (1, 0)]
-    scat, sent, later, kept = open_partial(load_index.reshape(1, -1), loads, phi)
+    scat, sent, held_phi = open_partial(load_index.reshape(1, -1), loads, phi)
     first = lax.ppermute(sent, "core", pair)
-    last = lax.ppermute(rest_partial(scat, later), "core", pair)
+    sent = rest_partial(scat, held_phi)
+    summed = list(more_partial(scat, held_phi, STEPS[:EARLY], first))
+    sent, *summed = lax.optimization_barrier((sent, *summed))
+    last = lax.ppermute(sent, "core", pair)
+    summed += more_partial(scat, held_phi, STEPS[EARLY:], last)
     parts = []
-    for start, mates in ((0, first), (4, last)):
-        for q, part in enumerate(more_partial(scat, kept, start, mates), start):
-            here = STEPS[q] == (0, 0)
-            parts.append(part if here else lax.ppermute(part, XY, step_pairs(*STEPS[q])))
+    for step, part in zip(STEPS, summed):
+        parts.append(part if step == (0, 0) else lax.ppermute(part, XY, step_pairs(*step)))
 
     radius = jnp.exp(-damping)
     zr = (radius * jnp.cos(frequency)).reshape(1, -1)
@@ -419,12 +447,9 @@
     states = lax.all_to_all(payload, TM, 0, 0)
     natural, out = make_history(states, enter, pre, w, qr, qi, lax.axis_size(XY))
     near = lax.all_to_all(out, XY, 0, 0)
-    natural, near = lax.optimization_barrier((natural, near))
     far = lax.ppermute(near, "core", pair)
-    history = turn_history(natural)
-    field = add_field(False, near, staged)
-    field = add_field(True, far, staged, field)
-    return field, history
+    field, history = near_field(near, staged, natural)
+    return far_field(far, staged, field), history
 
 
 def solution(mesh):

time: 83.7 us -> 79.1 us (0.945)
  waiting for transfers between devices: 7.61 us -> 3.37 us
  blocking collectives: 35.9 us -> 34.5 us
  starting transfers between devices: 17 us -> 18.3 us
    ppermute x8, waiting for transfers between devices: 7.61 us -> 3.13 us  [the longest x7 3.13 us: body(): lax.ppermute(part, XY, step_pairs(*step))]
    all_to_all x1, blocking collectives: 22.8 us -> 20.7 us  [body(): near = lax.all_to_all(out, XY, 0, 0)]
    ppermute x1, starting transfers between devices: 0.09 us -> 1.49 us  [body(): first = lax.ppermute(sent, 'core', pair)]
    all_to_all x1, blocking collectives: 13 us -> 13.9 us  [body(): states = lax.all_to_all(payload, TM, 0, 0)]
    pallas_call x6 -> x5, Pallas kernels: 11.2 us -> 11 us  [the longest x1 4.19 us: far_field(): pl.pallas_call(far_kernel, out_shape=jax.ShapeDtypeStruct((steps, points)...]
  transfers between devices with their start and end apart: 10 -> 10, of which waited for: 3 -> 2; matrix products, arithmetic and copies ran while one was open for 0% -> 0% of each run, Pallas kernels for 14% -> 16%
where the time goes in v4:
time: 79.1 us; the launch traced here: 78.9 us
  blocking collectives  34.5 us (44%)
  Pallas kernels  21.7 us (27%)
  starting transfers between devices  18.3 us (23%)
  waiting for transfers between devices  3.37 us (4%)
  between operations  0.91 us (1%)
    all_to_all x1, blocking collectives, body(): near = lax.all_to_all(out, XY, 0, 0)  20.7 us
    all_to_all x1, blocking collectives, body(): states = lax.all_to_all(payload, TM, 0, 0)  13.9 us
    ppermute x7, starting transfers between devices, body(): lax.ppermute(part, XY, step_pairs(*step))  12.3 us
    pallas_call x1, Pallas kernels, coefficients(): pl.pallas_call(coef_kernel, out_shape=(full, full, full, full, jax.ShapeD...  6.06 us
    pallas_call x1, Pallas kernels, far_field(): pl.pallas_call(far_kernel, out_shape=jax.ShapeDtypeStruct((steps, points)...  4.19 us
    pallas_call x1, Pallas kernels, near_field(): pl.pallas_call(near_kernel, out_shape=(jax.ShapeDtypeStruct((steps, point...  4.09 us
    ppermute x1, starting transfers between devices, body(): far = lax.ppermute(near, 'core', pair)  4 us
    pallas_call x1, Pallas kernels, open_partial(): pl.pallas_call(open_kernel, out_shape=(pltpu.VMEM((steps, rows), BF16), j...  3.95 us
  transfers between devices with their start and end apart: 10, of which 2 were waited for; matrix products, arithmetic and copies ran while one was open for 0% of the time, Pallas kernels for 16%

profile of v4, /device:TPU:1, one launch (start us, length us, event | category | flops | bytes accessed | tf_op | source)
XLA Modules:
  0.0 78.9 jit_solution(11371342013596396918)
XLA Ops:
  0.6 3.9 %open_partial.1 = (bf16[384,768]{1,0:T(8,128)(2,1)S(1)}, bf16[2,384,256]{2,1,0:T(8,128)(2,1)S(1)}, bf16[768,4096]{1,0:T(8,128)(2,1)S(1)}) custom-call(s32[1,512]{1,0:T(1,128)} %bitcast.7, bf16[384,512]{1,0:T(8,128)(2,1)} %loads_hbm.1, bf16[768,4096]{1,0:T(8,128)(2,1)} %phi_hbm.1), custom_call_target="tpu_custom_call" | custom-call | flops 603979776 | bytes 6291456 | tf_op jit(solution)/shard_map/open_partial/pallas_call | solution.py:92
  4.6 1.5 %collective-permute-start = (bf16[2,384,256]{2,1,0:T(8,128)(2,1)S(1)}, bf16[2,384,256]{2,1,0:T(8,128)(2,1)S(1)}, u32[]{:S(2)}, u32[]{:S(2)}) collective-permute-start(bf16[2,384,256]{2,1,0:T(8,128)(2,1)S(1)} %get-tuple-element.34), channel_id=1, source_target_pairs={{0,1},{1,0},{2,3},{3,2},{4,5},{5,4},{6,7},{7,6},{8,9},{9,8},{10,11... | collective-permute-start | bytes 1179656 | tf_op jit(solution)/shard_map/ppermute | solution.py:429
  6.1 1.1 %rest_partial.1 = bf16[6,384,256]{2,1,0:T(8,128)(2,1)S(1)} custom-call(bf16[384,768]{1,0:T(8,128)(2,1)S(1)} %get-tuple-element.32.scat_ref.refs_0_, bf16[768,4096]{1,0:T(8,128)(2,1)S(1)} %get-tuple-element.33.phi_ref.refs_1_), custom_call_target="tpu_custom_call" | custom-call | flops 603979776 | bytes 1572864 | tf_op jit(solution)/shard_map/rest_partial/pallas_call | solution.py:120
  7.2 0.0 copy-start
  7.2 0.2 collective-permute-done.refs_2_
  7.4 0.5 more_partial.2
  7.9 0.5 collective-permute-start.3
  8.4 3.8 %collective-permute-start.1 = (bf16[384,256]{1,0:T(8,128)(2,1)S(1)}, bf16[384,256]{1,0:T(8,128)(2,1)S(1)}, u32[]{:S(2)}, u32[]{:S(2)}) collective-permute-start(bf16[384,256]{1,0:T(8,128)(2,1)S(1)} %get-tuple-element.37), channel_id=1, source_target_pairs={{0,10},{2,8},{4,14},{6,12},{8,2},{10,0},{12,6},{14,4},{1,11},{3,9}... | collective-permute-start | bytes 589832 | tf_op jit(solution)/shard_map/ppermute | solution.py:437
  12.2 0.2 collective-permute-start.2
  12.4 0.0 copy-done
  12.4 0.0 copy-start.1
  12.4 0.0 copy-start.2
  12.4 0.0 collective-permute-done.3.refs_2_
  12.4 1.1 %more_partial.3 = (bf16[384,256]{1,0:T(8,128)(2,1)S(1)}, bf16[384,256]{1,0:T(8,128)(2,1)S(1)}, bf16[384,256]{1,0:T(8,128)(2,1)S(1)}, bf16[384,256]{1,0:T(8,128)(...) custom-call(bf16[384,768]{1,0:T(8,128)(2,1)S(1)} %get-tuple-element.32.scat_ref.refs_0_, ...), custom_call_target="tpu_custom_call" | custom-call | flops 905969664 | bytes 2359296 | tf_op jit(solution)/shard_map/more_partial/pallas_call | solution.py:139
  13.6 2.4 %collective-permute-start.4 = (bf16[384,256]{1,0:T(8,128)(2,1)S(1)}, bf16[384,256]{1,0:T(8,128)(2,1)S(1)}, u32[]{:S(2)}, u32[]{:S(2)}) collective-permute-start(bf16[384,256]{1,0:T(8,128)(2,1)S(1)} %get-tuple-element.40), channel_id=1, source_target_pairs={{0,12},{2,14},{4,0},{6,2},{8,4},{10,6},{12,8},{14,10},{1,13},{3,15... | collective-permute-start | bytes 589832 | tf_op jit(solution)/shard_map/ppermute | solution.py:437
  16.0 0.0 collective-permute-start.5
  16.0 1.3 %collective-permute-start.6 = (bf16[384,256]{1,0:T(8,128)(2,1)S(1)}, bf16[384,256]{1,0:T(8,128)(2,1)S(1)}, u32[]{:S(2)}, u32[]{:S(2)}) collective-permute-start(bf16[384,256]{1,0:T(8,128)(2,1)S(1)} %get-tuple-element.42), channel_id=1, source_target_pairs={{0,2},{2,0},{4,6},{6,4},{8,10},{10,8},{12,14},{14,12},{1,3},{3,1},... | collective-permute-start | bytes 589832 | tf_op jit(solution)/shard_map/ppermute | solution.py:437
  17.3 0.0 collective-permute-done.1.refs_0_
  17.3 1.1 %collective-permute-start.7 = (bf16[384,256]{1,0:T(8,128)(2,1)S(1)}, bf16[384,256]{1,0:T(8,128)(2,1)S(1)}, u32[]{:S(2)}, u32[]{:S(2)}) collective-permute-start(bf16[384,256]{1,0:T(8,128)(2,1)S(1)} %get-tuple-element.43), channel_id=1, source_target_pairs={{0,4},{2,6},{4,8},{6,10},{8,12},{10,14},{12,0},{14,2},{1,5},{3,7},... | collective-permute-start | bytes 589832 | tf_op jit(solution)/shard_map/ppermute | solution.py:437
  18.4 3.1 %collective-permute-done.2.refs_1_ = bf16[384,256]{1,0:T(8,128)(2,1)S(1)} collective-permute-done((bf16[384,256]{1,0:T(8,128)(2,1)S(1)}, bf16[384,256]{1,0:T(8,128)(2,1)S(1)}, u32[]{:S(2)}, u32[]{:S(2)}) %collective-permute-start.2) | collective-permute-done | bytes 196640 | tf_op jit(solution)/shard_map/ppermute | solution.py:437
  21.6 3.4 %collective-permute-start.8 = (bf16[384,256]{1,0:T(8,128)(2,1)S(1)}, bf16[384,256]{1,0:T(8,128)(2,1)S(1)}, u32[]{:S(2)}, u32[]{:S(2)}) collective-permute-start(bf16[384,256]{1,0:T(8,128)(2,1)S(1)} %get-tuple-element.44), channel_id=1, source_target_pairs={{0,14},{2,12},{4,2},{6,0},{8,6},{10,4},{12,10},{14,8},{1,15},{3,13... | collective-permute-start | bytes 589832 | tf_op jit(solution)/shard_map/ppermute | solution.py:437
  25.0 0.0 copy-done.1
  25.0 0.0 copy-done.2
  25.0 6.1 %coefficients.1 = (f32[48,8,256]{2,1,0:T(8,128)S(1)}, f32[48,8,256]{2,1,0:T(8,128)S(1)}, f32[48,8,256]{2,1,0:T(8,128)S(1)}, f32[48,8,256]{2,1,0:T(8,128)S(1)}, f...) custom-call(f32[1,384]{1,0:T(1,128)S(1)} %reshape.20.gains_ref, ...), custom_call_target="tpu_custom_call" | custom-call | flops 786432 | bytes 16777216 | tf_op jit(solution)/shard_map/coefficients/pallas_call | solution.py:204
  31.1 0.0 collective-permute-done.4.refs_2_
  31.1 0.0 collective-permute-done.5.refs_3_
  31.1 0.0 collective-permute-done.6.refs_4_
  31.1 0.0 collective-permute-done.7.refs_5_
  31.1 0.0 collective-permute-done.8.refs_6_
  31.1 0.4 local_recurrence.1
  31.6 13.9 %all_to_all.10.got_ref = f32[8,8,256]{2,1,0:T(8,128)S(1)} all-to-all(f32[8,8,256]{2,1,0:T(8,128)S(1)} %get-tuple-element.53), channel_id=1, replica_groups=mesh['z'=4,'yh'=2,'x'=4,'yl'=2,'core'=2] {'z','yh'}, dimensions={0} | all-to-all | bytes 131072 | tf_op jit(solution)/shard_map/all_to_all | solution.py:447
  45.4 0.3 make_history.1
  45.8 20.7 %all_to_all.11.held_ref = bf16[8,384,256]{2,1,0:T(8,128)(2,1)S(1)} all-to-all(bf16[8,384,256]{2,1,0:T(8,128)(2,1)S(1)} %get-tuple-element.57), channel_id=1, replica_groups=mesh['z'=4,'yh'=2,'x'=4,'yl'=2,'core'=2] {'x','yl'}, dimensions={0} | all-to-all | bytes 3145728 | tf_op jit(solution)/shard_map/all_to_all | solution.py:449
  66.4 4.0 %collective-permute-start.9 = (bf16[8,384,256]{2,1,0:T(8,128)(2,1)S(1)}, bf16[8,384,256]{2,1,0:T(8,128)(2,1)S(1)}, u32[]{:S(2)}, u32[]{:S(2)}) collective-permute-start(bf16[8,384,256]{2,1,0:T(8,128)(2,1)S(1)} %all_to_all.11.held_ref), channel_id=1, source_target_pairs={{0,1},{1,0},{2,3},{3,2},{4,5},{5,4},{6,7},{7,6},{8,9},{9,8},{10,11... | collective-permute-start | bytes 4718600 | tf_op jit(solution)/shard_map/ppermute | solution.py:450
  70.4 4.1 %near_field.1 = (f32[384,2048]{1,0:T(8,128)S(1)}, f32[256,384]{1,0:T(8,128)}) custom-call(bf16[8,384,256]{2,1,0:T(8,128)(2,1)S(1)} %all_to_all.11.held_ref, bf16[4096,2048]{1,0:T(8,128)(2,1)S(1)} %get-tuple-element.58.shapes_ref, f32[384,256]{1,0:T(8,128)S(1)} %get-tuple-element.59.natural_ref), custom_call_target="tpu_custom_call" | custom-call | flops 3221225472 | bytes 8388608 | tf_op jit(solution)/shard_map/near_field/pallas_call | solution.py:384
  74.5 0.0 collective-permute-done.9.held_ref
  74.5 4.2 %far_field.1 = bf16[384,2048]{1,0:T(8,128)(2,1)} custom-call(bf16[8,384,256]{2,1,0:T(8,128)(2,1)S(1)} %collective-permute-done.9.held_ref, bf16[4096,2048]{1,0:T(8,128)(2,1)S(1)} %get-tuple-element.58.shapes_ref, f32[384,2048]{1,0:T(8,128)S(1)} %get-tuple-element.60.before_ref), custom_call_target="tpu_custom_call" | custom-call | flops 3221225472 | bytes 8388608 | tf_op jit(solution)/shard_map/far_field/pallas_call | solution.py:401
  (2 shorter events, 0.0 us)
Async XLA Ops:
  4.6 2.8 %collective-permute-start = (bf16[2,384,256]{2,1,0:T(8,128)(2,1)S(1)}, bf16[2,384,256]{2,1,0:T(8,128)(2,1)S(1)}, u32[]{:S(2)}, u32[]{:S(2)}) collective-permute-start(bf16[2,384,256]{2,1,0:T(8,128)(2,1)S(1)} %get-tuple-element.34), channel_id=1, source_target_pairs={{0,1},{1,0},{2,3},{3,2},{4,5},{5,4},{6,7},{7,6},{8,9},{9,8},{10,11... | collective-permute-start | bytes 1179656 | tf_op jit(solution)/shard_map/ppermute | solution.py:429
  7.2 5.2 %copy-start = (f32[384]{0:T(512)S(1)}, f32[384]{0:T(512)}, u32[]{:S(2)}) copy-start(f32[384]{0:T(512)} %param.12) | copy-start | bytes 4612
  7.9 4.5 %collective-permute-start.3 = (bf16[6,384,256]{2,1,0:T(8,128)(2,1)S(1)}, bf16[6,384,256]{2,1,0:T(8,128)(2,1)S(1)}, u32[]{:S(2)}, u32[]{:S(2)}) collective-permute-start(bf16[6,384,256]{2,1,0:T(8,128)(2,1)S(1)} %rest_partial.1), channel_id=1, source_target_pairs={{0,1},{1,0},{2,3},{3,2},{4,5},{5,4},{6,7},{7,6},{8,9},{9,8},{10,11... | collective-permute-start | bytes 3538952 | tf_op jit(solution)/shard_map/ppermute | solution.py:433
  8.4 8.9 %collective-permute-start.1 = (bf16[384,256]{1,0:T(8,128)(2,1)S(1)}, bf16[384,256]{1,0:T(8,128)(2,1)S(1)}, u32[]{:S(2)}, u32[]{:S(2)}) collective-permute-start(bf16[384,256]{1,0:T(8,128)(2,1)S(1)} %get-tuple-element.37), channel_id=1, source_target_pairs={{0,10},{2,8},{4,14},{6,12},{8,2},{10,0},{12,6},{14,4},{1,11},{3,9}... | collective-permute-start | bytes 589832 | tf_op jit(solution)/shard_map/ppermute | solution.py:437
  12.2 9.3 %collective-permute-start.2 = (bf16[384,256]{1,0:T(8,128)(2,1)S(1)}, bf16[384,256]{1,0:T(8,128)(2,1)S(1)}, u32[]{:S(2)}, u32[]{:S(2)}) collective-permute-start(bf16[384,256]{1,0:T(8,128)(2,1)S(1)} %get-tuple-element.38), channel_id=1, source_target_pairs={{0,6},{2,4},{4,10},{6,8},{8,14},{10,12},{12,2},{14,0},{1,7},{3,5},... | collective-permute-start | bytes 589832 | tf_op jit(solution)/shard_map/ppermute | solution.py:437
  12.4 12.6 %copy-start.1 = (f32[256]{0:T(256)S(1)}, f32[256]{0:T(256)}, u32[]{:S(2)}) copy-start(f32[256]{0:T(256)} %param.11) | copy-start | bytes 3076
  12.4 12.6 %copy-start.2 = (f32[256]{0:T(256)S(1)}, f32[256]{0:T(256)}, u32[]{:S(2)}) copy-start(f32[256]{0:T(256)} %param.10) | copy-start | bytes 3076
  13.6 17.5 %collective-permute-start.4 = (bf16[384,256]{1,0:T(8,128)(2,1)S(1)}, bf16[384,256]{1,0:T(8,128)(2,1)S(1)}, u32[]{:S(2)}, u32[]{:S(2)}) collective-permute-start(bf16[384,256]{1,0:T(8,128)(2,1)S(1)} %get-tuple-element.40), channel_id=1, source_target_pairs={{0,12},{2,14},{4,0},{6,2},{8,4},{10,6},{12,8},{14,10},{1,13},{3,15... | collective-permute-start | bytes 589832 | tf_op jit(solution)/shard_map/ppermute | solution.py:437
  16.0 15.1 %collective-permute-start.5 = (bf16[384,256]{1,0:T(8,128)(2,1)S(1)}, bf16[384,256]{1,0:T(8,128)(2,1)S(1)}, u32[]{:S(2)}, u32[]{:S(2)}) collective-permute-start(bf16[384,256]{1,0:T(8,128)(2,1)S(1)} %get-tuple-element.41), channel_id=1, source_target_pairs={{0,8},{2,10},{4,12},{6,14},{8,0},{10,2},{12,4},{14,6},{1,9},{3,11}... | collective-permute-start | bytes 589832 | tf_op jit(solution)/shard_map/ppermute | solution.py:437
  16.0 15.1 %collective-permute-start.6 = (bf16[384,256]{1,0:T(8,128)(2,1)S(1)}, bf16[384,256]{1,0:T(8,128)(2,1)S(1)}, u32[]{:S(2)}, u32[]{:S(2)}) collective-permute-start(bf16[384,256]{1,0:T(8,128)(2,1)S(1)} %get-tuple-element.42), channel_id=1, source_target_pairs={{0,2},{2,0},{4,6},{6,4},{8,10},{10,8},{12,14},{14,12},{1,3},{3,1},... | collective-permute-start | bytes 589832 | tf_op jit(solution)/shard_map/ppermute | solution.py:437
  17.3 13.8 %collective-permute-start.7 = (bf16[384,256]{1,0:T(8,128)(2,1)S(1)}, bf16[384,256]{1,0:T(8,128)(2,1)S(1)}, u32[]{:S(2)}, u32[]{:S(2)}) collective-permute-start(bf16[384,256]{1,0:T(8,128)(2,1)S(1)} %get-tuple-element.43), channel_id=1, source_target_pairs={{0,4},{2,6},{4,8},{6,10},{8,12},{10,14},{12,0},{14,2},{1,5},{3,7},... | collective-permute-start | bytes 589832 | tf_op jit(solution)/shard_map/ppermute | solution.py:437
  21.6 9.6 %collective-permute-start.8 = (bf16[384,256]{1,0:T(8,128)(2,1)S(1)}, bf16[384,256]{1,0:T(8,128)(2,1)S(1)}, u32[]{:S(2)}, u32[]{:S(2)}) collective-permute-start(bf16[384,256]{1,0:T(8,128)(2,1)S(1)} %get-tuple-element.44), channel_id=1, source_target_pairs={{0,14},{2,12},{4,2},{6,0},{8,6},{10,4},{12,10},{14,8},{1,15},{3,13... | collective-permute-start | bytes 589832 | tf_op jit(solution)/shard_map/ppermute | solution.py:437
  66.4 8.1 %collective-permute-start.9 = (bf16[8,384,256]{2,1,0:T(8,128)(2,1)S(1)}, bf16[8,384,256]{2,1,0:T(8,128)(2,1)S(1)}, u32[]{:S(2)}, u32[]{:S(2)}) collective-permute-start(bf16[8,384,256]{2,1,0:T(8,128)(2,1)S(1)} %all_to_all.11.held_ref), channel_id=1, source_target_pairs={{0,1},{1,0},{2,3},{3,2},{4,5},{5,4},{6,7},{7,6},{8,9},{9,8},{10,11... | collective-permute-start | bytes 4718600 | tf_op jit(solution)/shard_map/ppermute | solution.py:450

commit v5 on v4

--- a/solution.py
+++ b/solution.py
@@ -15,7 +15,9 @@
 MID = 12 * 1024 * 1024
 DEEP = 256
 EARLY = 2
+FLOPS = 500 * 1000 * 1000
 STEPS = ((2, 1), (1, 1), (3, 0), (2, 0), (0, 1), (1, 0), (3, 1), (0, 0))
+SPREAD = ((2, 0), (2, 1), (1, 0), (0, 1), (3, 1), (1, 1), (3, 0))
 
 
 def vmem():
@@ -72,14 +74,13 @@
         copy.start()
     rows = scat_ref.shape[1]
     channels = index_ref.shape[1]
-    place = lax.broadcasted_iota(jnp.int32, (rows, channels), 0)
+    place = lax.broadcasted_iota(jnp.int32, (channels, rows), 1).astype(F32)
     index_copy.wait()
-    local = index_ref[...] - lax.axis_index(DOF) * rows
-    onehot = jnp.where(place == local, 1.0, 0.0).astype(BF16)
+    local = (index_ref[...] - lax.axis_index(DOF) * rows).astype(F32)
+    column = jnp.broadcast_to(local, (8, channels)).T[:, 0:1]
+    onehot = jnp.where(place == column, 1.0, 0.0).astype(BF16)
     loads_copy.wait()
-    summed = lax.dot_general(
-        loads_ref[...], onehot, (((1,), (1,)), ((), ())), preferred_element_type=F32
-    )
+    summed = jnp.dot(loads_ref[...], onehot, preferred_element_type=F32)
     scat_ref[...] = summed.astype(BF16)
     mine = products(scat_ref, phi_ref, STEPS[:EARLY], True, lambda k: copies[k].wait())
     for q, value in enumerate(mine):
@@ -306,18 +307,17 @@
     natural = jnp.concatenate([hist_ref[h] for h in range(2)], axis=1)
     history_ref[...] = natural
     rounded = natural.astype(BF16)
-    for k in range(out_ref.shape[0]):
-        out_ref[k] = rounded
-
-
-def make_history(got, enter, pre, w, qr, qi, copies):
+    out_ref[...] = rounded
+
+
+def make_history(got, enter, pre, w, qr, qi):
     inner = w.shape[0]
     steps = inner * 8
     return pl.pallas_call(
         history_kernel,
         out_shape=(
             jax.ShapeDtypeStruct((steps, LANES), F32),
-            jax.ShapeDtypeStruct((copies, steps, LANES), BF16),
+            jax.ShapeDtypeStruct((steps, LANES), BF16),
         ),
         in_specs=[vmem()] * 6,
         out_specs=(vmem(), vmem()),
@@ -331,37 +331,72 @@
 WIDE = 512
 
 
-def field_tiles(other, held_ref, before, shapes_ref, store):
-    core = lax.axis_index("core")
-    core = 1 - core if other else core
+def field_tiles(whose, held, before, shapes_ref, store):
+    places = [block_of(step, -1, other) for step, other in whose]
     for n in range(0, shapes_ref.shape[1], WIDE):
         across = slice(n, n + WIDE)
         total = before[0][:, across] if before else None
-        for q in range(held_ref.shape[0]):
-            place = pl.multiple_of((2 * q + core) * LANES, LANES)
+        for place, part in zip(places, held):
             product = jnp.dot(
-                held_ref[q], shapes_ref[pl.ds(place, LANES), across], preferred_element_type=F32
+                part[...], shapes_ref[pl.ds(place, LANES), across], preferred_element_type=F32
             )
             total = product if total is None else total + product
         store(n, total)
 
 
-def near_kernel(held_ref, shapes_ref, natural_ref, out_ref, history_ref):
-    piece = HALF
+def first_kernel(whose, shapes_ref, natural_ref, *refs):
+    held, (out_ref, history_ref) = refs[:-2], refs[-2:]
 
     def store(n, total):
         out_ref[:, n : n + WIDE] = total
-        first = n // WIDE * piece
+        first = n // WIDE * HALF
         if first < natural_ref.shape[0]:
-            part = slice(first, first + piece)
+            part = slice(first, first + HALF)
             for h in range(2):
                 lanes = slice(h * HALF, (h + 1) * HALF)
                 history_ref[lanes, part] = natural_ref[part, lanes].T
 
-    field_tiles(False, held_ref, [], shapes_ref, store)
-
-
-def far_kernel(held_ref, shapes_ref, before_ref, out_hbm, out_ref, sems):
+    field_tiles(whose, held, [], shapes_ref, store)
+
+
+def first_field(whose, held, staged, natural):
+    steps, lanes = natural.shape
+    points = staged.shape[1]
+    return pl.pallas_call(
+        lambda *refs: first_kernel(whose, *refs),
+        out_shape=(
+            jax.ShapeDtypeStruct((steps, points), F32),
+            jax.ShapeDtypeStruct((lanes, steps), F32),
+        ),
+        in_specs=[vmem()] * (2 + len(held)),
+        out_specs=(vmem(),) * 2,
+        compiler_params=pltpu.CompilerParams(vmem_limit_bytes=MID),
+        cost_estimate=cost(FLOPS * len(held), FLOPS),
+        name="first_field",
+    )(staged, natural, *held)
+
+
+def next_kernel(whose, shapes_ref, before_ref, *refs):
+    def store(n, total):
+        refs[-1][:, n : n + WIDE] = total
+
+    field_tiles(whose, refs[:-1], [before_ref], shapes_ref, store)
+
+
+def next_field(whose, held, staged, before):
+    return pl.pallas_call(
+        lambda *refs: next_kernel(whose, *refs),
+        out_shape=jax.ShapeDtypeStruct(before.shape, F32),
+        in_specs=[vmem()] * (2 + len(held)),
+        out_specs=vmem(),
+        compiler_params=pltpu.CompilerParams(vmem_limit_bytes=MID),
+        cost_estimate=cost(FLOPS * len(whose), FLOPS),
+        name="next_field",
+    )(staged, before, *held)
+
+
+def last_kernel(whose, shapes_ref, before_ref, *refs):
+    held, (out_hbm, out_ref, sems) = refs[:-3], refs[-3:]
     copies = []
 
     def store(n, total):
@@ -373,44 +408,26 @@
         copy.start()
         copies.append(copy)
 
-    field_tiles(True, held_ref, [before_ref], shapes_ref, store)
+    field_tiles(whose, held, [before_ref], shapes_ref, store)
     for copy in copies:
         copy.wait()
 
 
-def near_field(held, staged, natural):
-    count, steps, lanes = held.shape
-    points = staged.shape[1]
-    return pl.pallas_call(
-        near_kernel,
-        out_shape=(
-            jax.ShapeDtypeStruct((steps, points), F32),
-            jax.ShapeDtypeStruct((lanes, steps), F32),
-        ),
-        in_specs=[vmem()] * 3,
-        out_specs=(vmem(), vmem()),
-        compiler_params=pltpu.CompilerParams(vmem_limit_bytes=MID),
-        cost_estimate=cost(2 * count * LANES * steps * points, 2 * count * LANES * points),
-        name="near_field",
-    )(held, staged, natural)
-
-
-def far_field(held, staged, before):
-    count, steps, _ = held.shape
-    points = staged.shape[1]
-    return pl.pallas_call(
-        far_kernel,
+def last_field(whose, held, staged, before):
+    steps, points = before.shape
+    return pl.pallas_call(
+        lambda *refs: last_kernel(whose, *refs),
         out_shape=jax.ShapeDtypeStruct((steps, points), BF16),
-        in_specs=[vmem()] * 3,
+        in_specs=[vmem()] * (2 + len(held)),
         out_specs=hbm(),
         scratch_shapes=[
             pltpu.VMEM((steps, points), BF16),
             pltpu.SemaphoreType.DMA((points // WIDE,)),
         ],
         compiler_params=pltpu.CompilerParams(vmem_limit_bytes=MID),
-        cost_estimate=cost(2 * count * LANES * steps * points, 2 * count * LANES * points),
-        name="far_field",
-    )(held, staged, before)
+        cost_estimate=cost(FLOPS * len(whose), FLOPS),
+        name="last_field",
+    )(staged, before, *held)
 
 
 def step_pairs(dx, dy):
@@ -445,11 +462,23 @@
     cr, ci, qr, qi, pre, whole = coef
     w, enter, payload = local_recurrence(parts, cr, ci, qr, qi, whole, groups)
     states = lax.all_to_all(payload, TM, 0, 0)
-    natural, out = make_history(states, enter, pre, w, qr, qi, lax.axis_size(XY))
-    near = lax.all_to_all(out, XY, 0, 0)
-    far = lax.ppermute(near, "core", pair)
-    field, history = near_field(near, staged, natural)
-    return far_field(far, staged, field), history
+    natural, mine = make_history(states, enter, pre, w, qr, qi)
+    near = [lax.ppermute(mine, XY, step_pairs(*step)) for step in SPREAD]
+    near.append(mine)
+    whose = [*SPREAD, (0, 0)]
+    early = (3, 1)
+    later = tuple(q for q in range(7) if q not in early)
+
+    def pick(chosen):
+        return [(whose[q], False) for q in chosen], [near[q] for q in chosen]
+
+    field, history = first_field(*pick((7, *early)), staged, natural)
+    sent = list(near)
+    field, sent[0] = lax.optimization_barrier((field, sent[0]))
+    far = [lax.ppermute(part, "core", pair) for part in sent]
+    field = next_field(*pick(later), staged, field)
+    field = last_field([(step, True) for step in whose], far, staged, field)
+    return field, history
 
 
 def solution(mesh):

time: 79.1 us -> 77.2 us (0.976); the launches traced: 78.9 us -> 75.7 us
  blocking collectives: 34.5 us -> 13.9 us
  starting transfers between devices: 18.3 us -> 28 us
  waiting for transfers between devices: 3.37 us -> 11.1 us
    all_to_all x1 -> x0, blocking collectives: 20.7 us -> none  [body(): near = lax.all_to_all(out, XY, 0, 0)]
    ppermute x1 -> x15, starting transfers between devices: 4 us -> 13.7 us  [the longest x8 7.06 us: body(): far = [lax.ppermute(part, 'core', pair) for part in sent]]
    ppermute x1 -> x15, waiting for transfers between devices: 0.01 us -> 7.72 us  [the longest x7 7.7 us: body(): near = [lax.ppermute(mine, XY, step_pairs(*step)) for step in SPREAD]]
    pallas_call x2 -> x3, Pallas kernels: 8.28 us -> 8.47 us  [the longest x1 4.21 us: last_field(): pl.pallas_call(lambda *refs: last_kernel(whose, *refs), out_shape=jax.Sha...]
  transfers between devices with their start and end apart: 10 -> 24, of which waited for: 2 -> 5; matrix products, arithmetic and copies ran while one was open for 0% -> 0% of each run, Pallas kernels for 16% -> 17%
where the time goes in v5:
time: 77.2 us; the launch traced here: 75.7 us
  starting transfers between devices  28 us (36%)
  Pallas kernels  21.8 us (28%)
  blocking collectives  13.9 us (18%)
  waiting for transfers between devices  11.1 us (14%)
  between operations  0.97 us (1%)
    all_to_all x1, blocking collectives, body(): states = lax.all_to_all(payload, TM, 0, 0)  13.9 us
    ppermute x7, starting transfers between devices, body(): lax.ppermute(part, XY, step_pairs(*step))  12.3 us
    ppermute x7, waiting for transfers between devices, body(): near = [lax.ppermute(mine, XY, step_pairs(*step)) for step in SPREAD]  7.7 us
    ppermute x8, starting transfers between devices, body(): far = [lax.ppermute(part, 'core', pair) for part in sent]  7.06 us
    ppermute x7, starting transfers between devices, body(): near = [lax.ppermute(mine, XY, step_pairs(*step)) for step in SPREAD]  6.63 us
    pallas_call x1, Pallas kernels, coefficients(): pl.pallas_call(coef_kernel, out_shape=(full, full, full, full, jax.ShapeD...  6.06 us
    pallas_call x1, Pallas kernels, last_field(): pl.pallas_call(lambda *refs: last_kernel(whose, *refs), out_shape=jax.Sha...  4.21 us
    pallas_call x1, Pallas kernels, open_partial(): pl.pallas_call(open_kernel, out_shape=(pltpu.VMEM((steps, rows), BF16), j...  3.91 us
  transfers between devices with their start and end apart: 24, of which 5 were waited for; matrix products, arithmetic and copies ran while one was open for 0% of the time, Pallas kernels for 17%

profile of v5, /device:TPU:1, one launch (start us, length us, event | category | flops | bytes accessed | tf_op | source)
XLA Modules:
  0.0 75.7 jit_solution(15100477499145461443)
XLA Ops:
  0.6 3.9 %open_partial.1 = (bf16[384,768]{1,0:T(8,128)(2,1)S(1)}, bf16[2,384,256]{2,1,0:T(8,128)(2,1)S(1)}, bf16[768,4096]{1,0:T(8,128)(2,1)S(1)}) custom-call(s32[1,512]{1,0:T(1,128)} %bitcast.7, bf16[384,512]{1,0:T(8,128)(2,1)} %loads_hbm.1, bf16[768,4096]{1,0:T(8,128)(2,1)} %phi_hbm.1), custom_call_target="tpu_custom_call" | custom-call | flops 603979776 | bytes 6291456 | tf_op jit(solution)/shard_map/open_partial/pallas_call | solution.py:93
  4.6 1.5 %collective-permute-start = (bf16[2,384,256]{2,1,0:T(8,128)(2,1)S(1)}, bf16[2,384,256]{2,1,0:T(8,128)(2,1)S(1)}, u32[]{:S(2)}, u32[]{:S(2)}) collective-permute-start(bf16[2,384,256]{2,1,0:T(8,128)(2,1)S(1)} %get-tuple-element.36), channel_id=1, source_target_pairs={{0,1},{1,0},{2,3},{3,2},{4,5},{5,4},{6,7},{7,6},{8,9},{9,8},{10,11... | collective-permute-start | bytes 1179656 | tf_op jit(solution)/shard_map/ppermute | solution.py:446
  6.0 1.1 %rest_partial.1 = bf16[6,384,256]{2,1,0:T(8,128)(2,1)S(1)} custom-call(bf16[384,768]{1,0:T(8,128)(2,1)S(1)} %get-tuple-element.34.scat_ref.refs_0_, bf16[768,4096]{1,0:T(8,128)(2,1)S(1)} %get-tuple-element.35.phi_ref.refs_1_), custom_call_target="tpu_custom_call" | custom-call | flops 603979776 | bytes 1572864 | tf_op jit(solution)/shard_map/rest_partial/pallas_call | solution.py:121
  7.2 0.0 copy-start
  7.2 0.2 collective-permute-done.refs_2_
  7.4 0.5 more_partial.2
  7.9 0.5 collective-permute-start.1
  8.3 3.8 %collective-permute-start.2 = (bf16[384,256]{1,0:T(8,128)(2,1)S(1)}, bf16[384,256]{1,0:T(8,128)(2,1)S(1)}, u32[]{:S(2)}, u32[]{:S(2)}) collective-permute-start(bf16[384,256]{1,0:T(8,128)(2,1)S(1)} %get-tuple-element.43), channel_id=1, source_target_pairs={{0,10},{2,8},{4,14},{6,12},{8,2},{10,0},{12,6},{14,4},{1,11},{3,9}... | collective-permute-start | bytes 589832 | tf_op jit(solution)/shard_map/ppermute | solution.py:454
  12.2 0.2 collective-permute-start.3
  12.4 0.0 collective-permute-done.1.refs_2_
  12.4 1.1 %more_partial.3 = (bf16[384,256]{1,0:T(8,128)(2,1)S(1)}, bf16[384,256]{1,0:T(8,128)(2,1)S(1)}, bf16[384,256]{1,0:T(8,128)(2,1)S(1)}, bf16[384,256]{1,0:T(8,128)(...) custom-call(bf16[384,768]{1,0:T(8,128)(2,1)S(1)} %get-tuple-element.34.scat_ref.refs_0_, ...), custom_call_target="tpu_custom_call" | custom-call | flops 905969664 | bytes 2359296 | tf_op jit(solution)/shard_map/more_partial/pallas_call | solution.py:140
  13.5 2.4 %collective-permute-start.4 = (bf16[384,256]{1,0:T(8,128)(2,1)S(1)}, bf16[384,256]{1,0:T(8,128)(2,1)S(1)}, u32[]{:S(2)}, u32[]{:S(2)}) collective-permute-start(bf16[384,256]{1,0:T(8,128)(2,1)S(1)} %get-tuple-element.45), channel_id=1, source_target_pairs={{0,12},{2,14},{4,0},{6,2},{8,4},{10,6},{12,8},{14,10},{1,13},{3,15... | collective-permute-start | bytes 589832 | tf_op jit(solution)/shard_map/ppermute | solution.py:454
  16.0 1.3 %collective-permute-start.6 = (bf16[384,256]{1,0:T(8,128)(2,1)S(1)}, bf16[384,256]{1,0:T(8,128)(2,1)S(1)}, u32[]{:S(2)}, u32[]{:S(2)}) collective-permute-start(bf16[384,256]{1,0:T(8,128)(2,1)S(1)} %get-tuple-element.47), channel_id=1, source_target_pairs={{0,2},{2,0},{4,6},{6,4},{8,10},{10,8},{12,14},{14,12},{1,3},{3,1},... | collective-permute-start | bytes 589832 | tf_op jit(solution)/shard_map/ppermute | solution.py:454
  17.3 1.1 %collective-permute-start.7 = (bf16[384,256]{1,0:T(8,128)(2,1)S(1)}, bf16[384,256]{1,0:T(8,128)(2,1)S(1)}, u32[]{:S(2)}, u32[]{:S(2)}) collective-permute-start(bf16[384,256]{1,0:T(8,128)(2,1)S(1)} %get-tuple-element.48), channel_id=1, source_target_pairs={{0,4},{2,6},{4,8},{6,10},{8,12},{10,14},{12,0},{14,2},{1,5},{3,7},... | collective-permute-start | bytes 589832 | tf_op jit(solution)/shard_map/ppermute | solution.py:454
  18.4 3.1 %collective-permute-done.3.refs_1_ = bf16[384,256]{1,0:T(8,128)(2,1)S(1)} collective-permute-done((bf16[384,256]{1,0:T(8,128)(2,1)S(1)}, bf16[384,256]{1,0:T(8,128)(2,1)S(1)}, u32[]{:S(2)}, u32[]{:S(2)}) %collective-permute-start.3) | collective-permute-done | bytes 196640 | tf_op jit(solution)/shard_map/ppermute | solution.py:454
  21.5 3.4 %collective-permute-start.8 = (bf16[384,256]{1,0:T(8,128)(2,1)S(1)}, bf16[384,256]{1,0:T(8,128)(2,1)S(1)}, u32[]{:S(2)}, u32[]{:S(2)}) collective-permute-start(bf16[384,256]{1,0:T(8,128)(2,1)S(1)} %get-tuple-element.49), channel_id=1, source_target_pairs={{0,14},{2,12},{4,2},{6,0},{8,6},{10,4},{12,10},{14,8},{1,15},{3,13... | collective-permute-start | bytes 589832 | tf_op jit(solution)/shard_map/ppermute | solution.py:454
  25.0 6.1 %coefficients.1 = (f32[48,8,256]{2,1,0:T(8,128)S(1)}, f32[48,8,256]{2,1,0:T(8,128)S(1)}, f32[48,8,256]{2,1,0:T(8,128)S(1)}, f32[48,8,256]{2,1,0:T(8,128)S(1)}, f...) custom-call(f32[1,384]{1,0:T(1,128)S(1)} %reshape.19.gains_ref, ...), custom_call_target="tpu_custom_call" | custom-call | flops 786432 | bytes 16777216 | tf_op jit(solution)/shard_map/coefficients/pallas_call | solution.py:205
  31.0 0.0 collective-permute-done.4.refs_2_
  31.1 0.0 collective-permute-done.5.refs_3_
  31.1 0.0 collective-permute-done.7.refs_5_
  31.1 0.0 collective-permute-done.8.refs_6_
  31.1 0.4 local_recurrence.1
  31.5 13.9 %all_to_all.5.got_ref = f32[8,8,256]{2,1,0:T(8,128)S(1)} all-to-all(f32[8,8,256]{2,1,0:T(8,128)S(1)} %get-tuple-element.56), channel_id=1, replica_groups=mesh['z'=4,'yh'=2,'x'=4,'yl'=2,'core'=2] {'z','yh'}, dimensions={0} | all-to-all | bytes 131072 | tf_op jit(solution)/shard_map/all_to_all | solution.py:464
  45.4 0.2 make_history.1
  45.6 0.6 collective-permute-start.10
  46.3 2.3 %collective-permute-start.9 = (bf16[384,256]{1,0:T(8,128)(2,1)S(1)}, bf16[384,256]{1,0:T(8,128)(2,1)S(1)}, u32[]{:S(2)}, u32[]{:S(2)}) collective-permute-start(bf16[384,256]{1,0:T(8,128)(2,1)S(1)} %get-tuple-element.61.refs_2_), channel_id=1, source_target_pairs={{0,2},{2,0},{4,6},{6,4},{8,10},{10,8},{12,14},{14,12},{1,3},{3,1},... | collective-permute-start | bytes 589832 | tf_op jit(solution)/shard_map/ppermute | solution.py:466
  48.6 1.3 %collective-permute-start.11 = (bf16[384,256]{1,0:T(8,128)(2,1)S(1)}, bf16[384,256]{1,0:T(8,128)(2,1)S(1)}, u32[]{:S(2)}, u32[]{:S(2)}) collective-permute-start(bf16[384,256]{1,0:T(8,128)(2,1)S(1)} %get-tuple-element.61.refs_2_), channel_id=1, source_target_pairs={{0,8},{2,10},{4,12},{6,14},{8,0},{10,2},{12,4},{14,6},{1,9},{3,11}... | collective-permute-start | bytes 589832 | tf_op jit(solution)/shard_map/ppermute | solution.py:466
  49.9 0.2 collective-permute-start.12
  50.1 2.2 %collective-permute-start.13 = (bf16[384,256]{1,0:T(8,128)(2,1)S(1)}, bf16[384,256]{1,0:T(8,128)(2,1)S(1)}, u32[]{:S(2)}, u32[]{:S(2)}) collective-permute-start(bf16[384,256]{1,0:T(8,128)(2,1)S(1)} %get-tuple-element.61.refs_2_), channel_id=1, source_target_pairs={{0,14},{2,12},{4,2},{6,0},{8,6},{10,4},{12,10},{14,8},{1,15},{3,13... | collective-permute-start | bytes 589832 | tf_op jit(solution)/shard_map/ppermute | solution.py:466
  52.3 0.5 collective-permute-done.10.refs_4_
  52.8 0.0 collective-permute-start.14
  52.8 6.4 %collective-permute-done.9.refs_3_ = bf16[384,256]{1,0:T(8,128)(2,1)S(1)} collective-permute-done((bf16[384,256]{1,0:T(8,128)(2,1)S(1)}, bf16[384,256]{1,0:T(8,128)(2,1)S(1)}, u32[]{:S(2)}, u32[]{:S(2)}) %collective-permute-start.9) | collective-permute-done | bytes 196640 | tf_op jit(solution)/shard_map/ppermute | solution.py:466
  59.2 0.0 collective-permute-start.15
  59.2 2.1 %first_field.1 = (f32[384,2048]{1,0:T(8,128)S(1)}, f32[256,384]{1,0:T(8,128)}) custom-call(bf16[4096,2048]{1,0:T(8,128)(2,1)S(1)} %get-tuple-element.42.refs_0_, f32[384,256]{1,0:T(8,128)S(1)} %get-tuple-element.60.refs_1_, bf16[384,256]{1,0:T(8,128)(2,1)S(1)} %get-tuple-element.61.refs_2_, bf16[384,256]{1,0:T(8,128)(2,1)S(1)} %collective-permute-done.9.refs_3_, ...), custom_call_target="tpu_custom_call" | custom-call | flops 1500000000 | bytes 500000000 | tf_op jit(solution)/shard_map/first_field/pallas_call | solution.py:365
  61.2 0.0 collective-permute-done.11.refs_2_
  61.2 3.9 %collective-permute-start.23 = (bf16[384,256]{1,0:T(8,128)(2,1)S(1)}, bf16[384,256]{1,0:T(8,128)(2,1)S(1)}, u32[]{:S(2)}, u32[]{:S(2)}) collective-permute-start(bf16[384,256]{1,0:T(8,128)(2,1)S(1)} %get-tuple-element.61.refs_2_), channel_id=1, source_target_pairs={{0,1},{1,0},{2,3},{3,2},{4,5},{5,4},{6,7},{7,6},{8,9},{9,8},{10,11... | collective-permute-start | bytes 589832 | tf_op jit(solution)/shard_map/ppermute | solution.py:478
  65.1 0.0 collective-permute-done.12.refs_3_
  65.1 0.1 collective-permute-start.16
  65.2 0.0 collective-permute-done.13.refs_4_
  65.2 0.4 collective-permute-start.17
  65.6 0.8 %collective-permute-done.14.refs_5_ = bf16[384,256]{1,0:T(8,128)(2,1)S(1)} collective-permute-done((bf16[384,256]{1,0:T(8,128)(2,1)S(1)}, bf16[384,256]{1,0:T(8,128)(2,1)S(1)}, u32[]{:S(2)}, u32[]{:S(2)}) %collective-permute-start.14) | collective-permute-done | bytes 196640 | tf_op jit(solution)/shard_map/ppermute | solution.py:466
  66.4 1.7 %collective-permute-start.19 = (bf16[384,256]{1,0:T(8,128)(2,1)S(1)}, bf16[384,256]{1,0:T(8,128)(2,1)S(1)}, u32[]{:S(2)}, u32[]{:S(2)}) collective-permute-start(bf16[384,256]{1,0:T(8,128)(2,1)S(1)} %collective-permute-done.9.refs_3_), channel_id=1, source_target_pairs={{0,1},{1,0},{2,3},{3,2},{4,5},{5,4},{6,7},{7,6},{8,9},{9,8},{10,11... | collective-permute-start | bytes 589832 | tf_op jit(solution)/shard_map/ppermute | solution.py:478
  68.1 0.0 collective-permute-start.18
  68.1 0.5 collective-permute-start.20
  68.6 0.1 collective-permute-start.21
  68.7 0.4 collective-permute-start.22
  69.1 2.2 %next_field.1.refs_1_ = f32[384,2048]{1,0:T(8,128)S(1)} custom-call(bf16[4096,2048]{1,0:T(8,128)(2,1)S(1)} %get-tuple-element.42.refs_0_, f32[384,2048]{1,0:T(8,128)S(1)} %get-tuple-element.63.refs_1_, bf16[384,256]{1,0:T(8,128)(2,1)S(1)} %collective-permute-done.11.refs_2_, bf16[384,256]{1,0:T(8,128)(2,1)S(1)} %collective-permute-done.12.refs_3_, ...), custom_call_target="tpu_custom_call" | custom-call | flops 2500000000 | bytes 500000000 | tf_op jit(solution)/shard_map/next_field/pallas_call | solution.py:387
  71.4 4.2 %last_field.1 = bf16[384,2048]{1,0:T(8,128)(2,1)} custom-call(bf16[4096,2048]{1,0:T(8,128)(2,1)S(1)} %get-tuple-element.42.refs_0_, f32[384,2048]{1,0:T(8,128)S(1)} %next_field.1.refs_1_, bf16[384,256]{1,0:T(8,128)(2,1)S(1)} %collective-permute-done.16.refs_2_, bf16[384,256]{1,0:T(8,128)(2,1)S(1)} %collective-permute-done.17.refs_3_, ...), custom_call_target="tpu_custom_call" | custom-call | flops 4000000000 | bytes 500000000 | tf_op jit(solution)/shard_map/last_field/pallas_call | solution.py:418
  (19 shorter events, 0.1 us)
Async XLA Ops:
  4.6 2.8 %collective-permute-start = (bf16[2,384,256]{2,1,0:T(8,128)(2,1)S(1)}, bf16[2,384,256]{2,1,0:T(8,128)(2,1)S(1)}, u32[]{:S(2)}, u32[]{:S(2)}) collective-permute-start(bf16[2,384,256]{2,1,0:T(8,128)(2,1)S(1)} %get-tuple-element.36), channel_id=1, source_target_pairs={{0,1},{1,0},{2,3},{3,2},{4,5},{5,4},{6,7},{7,6},{8,9},{9,8},{10,11... | collective-permute-start | bytes 1179656 | tf_op jit(solution)/shard_map/ppermute | solution.py:446
  7.2 5.2 %copy-start = (f32[384]{0:T(512)S(1)}, f32[384]{0:T(512)}, u32[]{:S(2)}) copy-start(f32[384]{0:T(512)} %param.12) | copy-start | bytes 4612
  7.9 4.5 %collective-permute-start.1 = (bf16[6,384,256]{2,1,0:T(8,128)(2,1)S(1)}, bf16[6,384,256]{2,1,0:T(8,128)(2,1)S(1)}, u32[]{:S(2)}, u32[]{:S(2)}) collective-permute-start(bf16[6,384,256]{2,1,0:T(8,128)(2,1)S(1)} %rest_partial.1), channel_id=1, source_target_pairs={{0,1},{1,0},{2,3},{3,2},{4,5},{5,4},{6,7},{7,6},{8,9},{9,8},{10,11... | collective-permute-start | bytes 3538952 | tf_op jit(solution)/shard_map/ppermute | solution.py:450
  8.3 8.9 %collective-permute-start.2 = (bf16[384,256]{1,0:T(8,128)(2,1)S(1)}, bf16[384,256]{1,0:T(8,128)(2,1)S(1)}, u32[]{:S(2)}, u32[]{:S(2)}) collective-permute-start(bf16[384,256]{1,0:T(8,128)(2,1)S(1)} %get-tuple-element.43), channel_id=1, source_target_pairs={{0,10},{2,8},{4,14},{6,12},{8,2},{10,0},{12,6},{14,4},{1,11},{3,9}... | collective-permute-start | bytes 589832 | tf_op jit(solution)/shard_map/ppermute | solution.py:454
  12.2 9.3 %collective-permute-start.3 = (bf16[384,256]{1,0:T(8,128)(2,1)S(1)}, bf16[384,256]{1,0:T(8,128)(2,1)S(1)}, u32[]{:S(2)}, u32[]{:S(2)}) collective-permute-start(bf16[384,256]{1,0:T(8,128)(2,1)S(1)} %get-tuple-element.44), channel_id=1, source_target_pairs={{0,6},{2,4},{4,10},{6,8},{8,14},{10,12},{12,2},{14,0},{1,7},{3,5},... | collective-permute-start | bytes 589832 | tf_op jit(solution)/shard_map/ppermute | solution.py:454
  12.4 12.6 %copy-start.1 = (f32[256]{0:T(256)S(1)}, f32[256]{0:T(256)}, u32[]{:S(2)}) copy-start(f32[256]{0:T(256)} %param.11) | copy-start | bytes 3076
  12.4 12.6 %copy-start.2 = (f32[256]{0:T(256)S(1)}, f32[256]{0:T(256)}, u32[]{:S(2)}) copy-start(f32[256]{0:T(256)} %param.10) | copy-start | bytes 3076
  13.5 17.5 %collective-permute-start.4 = (bf16[384,256]{1,0:T(8,128)(2,1)S(1)}, bf16[384,256]{1,0:T(8,128)(2,1)S(1)}, u32[]{:S(2)}, u32[]{:S(2)}) collective-permute-start(bf16[384,256]{1,0:T(8,128)(2,1)S(1)} %get-tuple-element.45), channel_id=1, source_target_pairs={{0,12},{2,14},{4,0},{6,2},{8,4},{10,6},{12,8},{14,10},{1,13},{3,15... | collective-permute-start | bytes 589832 | tf_op jit(solution)/shard_map/ppermute | solution.py:454
  16.0 15.1 %collective-permute-start.5 = (bf16[384,256]{1,0:T(8,128)(2,1)S(1)}, bf16[384,256]{1,0:T(8,128)(2,1)S(1)}, u32[]{:S(2)}, u32[]{:S(2)}) collective-permute-start(bf16[384,256]{1,0:T(8,128)(2,1)S(1)} %get-tuple-element.46), channel_id=1, source_target_pairs={{0,8},{2,10},{4,12},{6,14},{8,0},{10,2},{12,4},{14,6},{1,9},{3,11}... | collective-permute-start | bytes 589832 | tf_op jit(solution)/shard_map/ppermute | solution.py:454
  16.0 15.1 %collective-permute-start.6 = (bf16[384,256]{1,0:T(8,128)(2,1)S(1)}, bf16[384,256]{1,0:T(8,128)(2,1)S(1)}, u32[]{:S(2)}, u32[]{:S(2)}) collective-permute-start(bf16[384,256]{1,0:T(8,128)(2,1)S(1)} %get-tuple-element.47), channel_id=1, source_target_pairs={{0,2},{2,0},{4,6},{6,4},{8,10},{10,8},{12,14},{14,12},{1,3},{3,1},... | collective-permute-start | bytes 589832 | tf_op jit(solution)/shard_map/ppermute | solution.py:454
  17.3 13.8 %collective-permute-start.7 = (bf16[384,256]{1,0:T(8,128)(2,1)S(1)}, bf16[384,256]{1,0:T(8,128)(2,1)S(1)}, u32[]{:S(2)}, u32[]{:S(2)}) collective-permute-start(bf16[384,256]{1,0:T(8,128)(2,1)S(1)} %get-tuple-element.48), channel_id=1, source_target_pairs={{0,4},{2,6},{4,8},{6,10},{8,12},{10,14},{12,0},{14,2},{1,5},{3,7},... | collective-permute-start | bytes 589832 | tf_op jit(solution)/shard_map/ppermute | solution.py:454
  21.5 9.6 %collective-permute-start.8 = (bf16[384,256]{1,0:T(8,128)(2,1)S(1)}, bf16[384,256]{1,0:T(8,128)(2,1)S(1)}, u32[]{:S(2)}, u32[]{:S(2)}) collective-permute-start(bf16[384,256]{1,0:T(8,128)(2,1)S(1)} %get-tuple-element.49), channel_id=1, source_target_pairs={{0,14},{2,12},{4,2},{6,0},{8,6},{10,4},{12,10},{14,8},{1,15},{3,13... | collective-permute-start | bytes 589832 | tf_op jit(solution)/shard_map/ppermute | solution.py:454
  45.6 7.1 %collective-permute-start.10 = (bf16[384,256]{1,0:T(8,128)(2,1)S(1)}, bf16[384,256]{1,0:T(8,128)(2,1)S(1)}, u32[]{:S(2)}, u32[]{:S(2)}) collective-permute-start(bf16[384,256]{1,0:T(8,128)(2,1)S(1)} %get-tuple-element.61.refs_2_), channel_id=1, source_target_pairs={{0,10},{2,8},{4,14},{6,12},{8,2},{10,0},{12,6},{14,4},{1,11},{3,9}... | collective-permute-start | bytes 589832 | tf_op jit(solution)/shard_map/ppermute | solution.py:466
  46.3 12.9 %collective-permute-start.9 = (bf16[384,256]{1,0:T(8,128)(2,1)S(1)}, bf16[384,256]{1,0:T(8,128)(2,1)S(1)}, u32[]{:S(2)}, u32[]{:S(2)}) collective-permute-start(bf16[384,256]{1,0:T(8,128)(2,1)S(1)} %get-tuple-element.61.refs_2_), channel_id=1, source_target_pairs={{0,2},{2,0},{4,6},{6,4},{8,10},{10,8},{12,14},{14,12},{1,3},{3,1},... | collective-permute-start | bytes 589832 | tf_op jit(solution)/shard_map/ppermute | solution.py:466
  48.6 12.7 %collective-permute-start.11 = (bf16[384,256]{1,0:T(8,128)(2,1)S(1)}, bf16[384,256]{1,0:T(8,128)(2,1)S(1)}, u32[]{:S(2)}, u32[]{:S(2)}) collective-permute-start(bf16[384,256]{1,0:T(8,128)(2,1)S(1)} %get-tuple-element.61.refs_2_), channel_id=1, source_target_pairs={{0,8},{2,10},{4,12},{6,14},{8,0},{10,2},{12,4},{14,6},{1,9},{3,11}... | collective-permute-start | bytes 589832 | tf_op jit(solution)/shard_map/ppermute | solution.py:466
  49.9 15.2 %collective-permute-start.12 = (bf16[384,256]{1,0:T(8,128)(2,1)S(1)}, bf16[384,256]{1,0:T(8,128)(2,1)S(1)}, u32[]{:S(2)}, u32[]{:S(2)}) collective-permute-start(bf16[384,256]{1,0:T(8,128)(2,1)S(1)} %get-tuple-element.61.refs_2_), channel_id=1, source_target_pairs={{0,4},{2,6},{4,8},{6,10},{8,12},{10,14},{12,0},{14,2},{1,5},{3,7},... | collective-permute-start | bytes 589832 | tf_op jit(solution)/shard_map/ppermute | solution.py:466
  50.1 15.1 %collective-permute-start.13 = (bf16[384,256]{1,0:T(8,128)(2,1)S(1)}, bf16[384,256]{1,0:T(8,128)(2,1)S(1)}, u32[]{:S(2)}, u32[]{:S(2)}) collective-permute-start(bf16[384,256]{1,0:T(8,128)(2,1)S(1)} %get-tuple-element.61.refs_2_), channel_id=1, source_target_pairs={{0,14},{2,12},{4,2},{6,0},{8,6},{10,4},{12,10},{14,8},{1,15},{3,13... | collective-permute-start | bytes 589832 | tf_op jit(solution)/shard_map/ppermute | solution.py:466
  52.8 13.7 %collective-permute-start.14 = (bf16[384,256]{1,0:T(8,128)(2,1)S(1)}, bf16[384,256]{1,0:T(8,128)(2,1)S(1)}, u32[]{:S(2)}, u32[]{:S(2)}) collective-permute-start(bf16[384,256]{1,0:T(8,128)(2,1)S(1)} %get-tuple-element.61.refs_2_), channel_id=1, source_target_pairs={{0,6},{2,4},{4,10},{6,8},{8,14},{10,12},{12,2},{14,0},{1,7},{3,5},... | collective-permute-start | bytes 589832 | tf_op jit(solution)/shard_map/ppermute | solution.py:466
  59.2 8.9 %collective-permute-start.15 = (bf16[384,256]{1,0:T(8,128)(2,1)S(1)}, bf16[384,256]{1,0:T(8,128)(2,1)S(1)}, u32[]{:S(2)}, u32[]{:S(2)}) collective-permute-start(bf16[384,256]{1,0:T(8,128)(2,1)S(1)} %get-tuple-element.61.refs_2_), channel_id=1, source_target_pairs={{0,12},{2,14},{4,0},{6,2},{8,4},{10,6},{12,8},{14,10},{1,13},{3,15... | collective-permute-start | bytes 589832 | tf_op jit(solution)/shard_map/ppermute | solution.py:466
  61.2 6.9 %collective-permute-start.23 = (bf16[384,256]{1,0:T(8,128)(2,1)S(1)}, bf16[384,256]{1,0:T(8,128)(2,1)S(1)}, u32[]{:S(2)}, u32[]{:S(2)}) collective-permute-start(bf16[384,256]{1,0:T(8,128)(2,1)S(1)} %get-tuple-element.61.refs_2_), channel_id=1, source_target_pairs={{0,1},{1,0},{2,3},{3,2},{4,5},{5,4},{6,7},{7,6},{8,9},{9,8},{10,11... | collective-permute-start | bytes 589832 | tf_op jit(solution)/shard_map/ppermute | solution.py:478
  65.1 3.5 %collective-permute-start.16 = (bf16[384,256]{1,0:T(8,128)(2,1)S(1)}, bf16[384,256]{1,0:T(8,128)(2,1)S(1)}, u32[]{:S(2)}, u32[]{:S(2)}) collective-permute-start(bf16[384,256]{1,0:T(8,128)(2,1)S(1)} %collective-permute-done.11.refs_2_), channel_id=1, source_target_pairs={{0,1},{1,0},{2,3},{3,2},{4,5},{5,4},{6,7},{7,6},{8,9},{9,8},{10,11... | collective-permute-start | bytes 589832 | tf_op jit(solution)/shard_map/ppermute | solution.py:478
  65.2 3.5 %collective-permute-start.17 = (bf16[384,256]{1,0:T(8,128)(2,1)S(1)}, bf16[384,256]{1,0:T(8,128)(2,1)S(1)}, u32[]{:S(2)}, u32[]{:S(2)}) collective-permute-start(bf16[384,256]{1,0:T(8,128)(2,1)S(1)} %collective-permute-done.10.refs_4_), channel_id=1, source_target_pairs={{0,1},{1,0},{2,3},{3,2},{4,5},{5,4},{6,7},{7,6},{8,9},{9,8},{10,11... | collective-permute-start | bytes 589832 | tf_op jit(solution)/shard_map/ppermute | solution.py:478
  66.4 4.9 %collective-permute-start.19 = (bf16[384,256]{1,0:T(8,128)(2,1)S(1)}, bf16[384,256]{1,0:T(8,128)(2,1)S(1)}, u32[]{:S(2)}, u32[]{:S(2)}) collective-permute-start(bf16[384,256]{1,0:T(8,128)(2,1)S(1)} %collective-permute-done.9.refs_3_), channel_id=1, source_target_pairs={{0,1},{1,0},{2,3},{3,2},{4,5},{5,4},{6,7},{7,6},{8,9},{9,8},{10,11... | collective-permute-start | bytes 589832 | tf_op jit(solution)/shard_map/ppermute | solution.py:478
  68.1 3.2 %collective-permute-start.18 = (bf16[384,256]{1,0:T(8,128)(2,1)S(1)}, bf16[384,256]{1,0:T(8,128)(2,1)S(1)}, u32[]{:S(2)}, u32[]{:S(2)}) collective-permute-start(bf16[384,256]{1,0:T(8,128)(2,1)S(1)} %collective-permute-done.12.refs_3_), channel_id=1, source_target_pairs={{0,1},{1,0},{2,3},{3,2},{4,5},{5,4},{6,7},{7,6},{8,9},{9,8},{10,11... | collective-permute-start | bytes 589832 | tf_op jit(solution)/shard_map/ppermute | solution.py:478
  68.1 3.2 %collective-permute-start.20 = (bf16[384,256]{1,0:T(8,128)(2,1)S(1)}, bf16[384,256]{1,0:T(8,128)(2,1)S(1)}, u32[]{:S(2)}, u32[]{:S(2)}) collective-permute-start(bf16[384,256]{1,0:T(8,128)(2,1)S(1)} %collective-permute-done.13.refs_4_), channel_id=1, source_target_pairs={{0,1},{1,0},{2,3},{3,2},{4,5},{5,4},{6,7},{7,6},{8,9},{9,8},{10,11... | collective-permute-start | bytes 589832 | tf_op jit(solution)/shard_map/ppermute | solution.py:478
  68.6 2.7 %collective-permute-start.21 = (bf16[384,256]{1,0:T(8,128)(2,1)S(1)}, bf16[384,256]{1,0:T(8,128)(2,1)S(1)}, u32[]{:S(2)}, u32[]{:S(2)}) collective-permute-start(bf16[384,256]{1,0:T(8,128)(2,1)S(1)} %collective-permute-done.14.refs_5_), channel_id=1, source_target_pairs={{0,1},{1,0},{2,3},{3,2},{4,5},{5,4},{6,7},{7,6},{8,9},{9,8},{10,11... | collective-permute-start | bytes 589832 | tf_op jit(solution)/shard_map/ppermute | solution.py:478
  68.7 2.7 %collective-permute-start.22 = (bf16[384,256]{1,0:T(8,128)(2,1)S(1)}, bf16[384,256]{1,0:T(8,128)(2,1)S(1)}, u32[]{:S(2)}, u32[]{:S(2)}) collective-permute-start(bf16[384,256]{1,0:T(8,128)(2,1)S(1)} %collective-permute-done.15.refs_6_), channel_id=1, source_target_pairs={{0,1},{1,0},{2,3},{3,2},{4,5},{5,4},{6,7},{7,6},{8,9},{9,8},{10,11... | collective-permute-start | bytes 589832 | tf_op jit(solution)/shard_map/ppermute | solution.py:478

commit v6 on v5

--- a/solution.py
+++ b/solution.py
@@ -466,17 +466,17 @@
     near = [lax.ppermute(mine, XY, step_pairs(*step)) for step in SPREAD]
     near.append(mine)
     whose = [*SPREAD, (0, 0)]
-    early = (3, 1)
-    later = tuple(q for q in range(7) if q not in early)
 
     def pick(chosen):
         return [(whose[q], False) for q in chosen], [near[q] for q in chosen]
 
-    field, history = first_field(*pick((7, *early)), staged, natural)
     sent = list(near)
+    field, history = first_field(*pick((7, 3, 1)), staged, natural)
     field, sent[0] = lax.optimization_barrier((field, sent[0]))
+    field = next_field(*pick((0, 2, 4)), staged, field)
+    field, sent[5] = lax.optimization_barrier((field, sent[5]))
     far = [lax.ppermute(part, "core", pair) for part in sent]
-    field = next_field(*pick(later), staged, field)
+    field = next_field(*pick((5, 6)), staged, field)
     field = last_field([(step, True) for step in whose], far, staged, field)
     return field, history
 

time: 77.2 us -> 76.9 us (level)
  the two profiles are of different devices: /device:TPU:1 before, /device:TPU:17 now
where the time goes in v6:
time: 76.9 us; the launch traced here: 76.7 us
  starting transfers between devices  32 us (42%)
  Pallas kernels  21.9 us (28%)
  blocking collectives  11.7 us (15%)
  waiting for transfers between devices  9.97 us (13%)
  between operations  0.98 us (1%)
    ppermute x8, starting transfers between devices, body(): far = [lax.ppermute(part, 'core', pair) for part in sent]  11.7 us
    all_to_all x1, blocking collectives, body(): states = lax.all_to_all(payload, TM, 0, 0)  11.7 us
    ppermute x7, starting transfers between devices, body(): lax.ppermute(part, XY, step_pairs(*step))  11.4 us
    ppermute x7, starting transfers between devices, body(): near = [lax.ppermute(mine, XY, step_pairs(*step)) for step in SPREAD]  7.65 us
    pallas_call x1, Pallas kernels, coefficients(): pl.pallas_call(coef_kernel, out_shape=(full, full, full, full, jax.ShapeD...  6.06 us
    ppermute x7, waiting for transfers between devices, body(): near = [lax.ppermute(mine, XY, step_pairs(*step)) for step in SPREAD]  5.45 us
    pallas_call x1, Pallas kernels, last_field(): pl.pallas_call(lambda *refs: last_kernel(whose, *refs), out_shape=jax.Sha...  4.19 us
    pallas_call x1, Pallas kernels, open_partial(): pl.pallas_call(open_kernel, out_shape=(pltpu.VMEM((steps, rows), BF16), j...  3.91 us
  transfers between devices with their start and end apart: 24, of which 7 were waited for; matrix products, arithmetic and copies ran while one was open for 0% of the time, Pallas kernels for 17%

profile of v6, /device:TPU:17, one launch (start us, length us, event | category | flops | bytes accessed | tf_op | source)
XLA Modules:
  0.0 76.7 jit_solution(12441842364425684174)
XLA Ops:
  0.6 3.9 %open_partial.1 = (bf16[384,768]{1,0:T(8,128)(2,1)S(1)}, bf16[2,384,256]{2,1,0:T(8,128)(2,1)S(1)}, bf16[768,4096]{1,0:T(8,128)(2,1)S(1)}) custom-call(s32[1,512]{1,0:T(1,128)} %bitcast.7, bf16[384,512]{1,0:T(8,128)(2,1)} %loads_hbm.1, bf16[768,4096]{1,0:T(8,128)(2,1)} %phi_hbm.1), custom_call_target="tpu_custom_call" | custom-call | flops 603979776 | bytes 6291456 | tf_op jit(solution)/shard_map/open_partial/pallas_call | solution.py:93
  4.6 0.7 collective-permute-start
  5.3 1.1 %rest_partial.1 = bf16[6,384,256]{2,1,0:T(8,128)(2,1)S(1)} custom-call(bf16[384,768]{1,0:T(8,128)(2,1)S(1)} %get-tuple-element.36.scat_ref.refs_0_, bf16[768,4096]{1,0:T(8,128)(2,1)S(1)} %get-tuple-element.37.phi_ref.refs_1_), custom_call_target="tpu_custom_call" | custom-call | flops 603979776 | bytes 1572864 | tf_op jit(solution)/shard_map/rest_partial/pallas_call | solution.py:121
  6.4 0.0 copy-start
  6.4 0.2 collective-permute-done.refs_2_
  6.7 0.5 more_partial.2
  7.1 0.5 collective-permute-start.1
  7.6 3.5 %collective-permute-start.2 = (bf16[384,256]{1,0:T(8,128)(2,1)S(1)}, bf16[384,256]{1,0:T(8,128)(2,1)S(1)}, u32[]{:S(2)}, u32[]{:S(2)}) collective-permute-start(bf16[384,256]{1,0:T(8,128)(2,1)S(1)} %get-tuple-element.45), channel_id=1, source_target_pairs={{0,10},{2,8},{4,14},{6,12},{8,2},{10,0},{12,6},{14,4},{1,11},{3,9}... | collective-permute-start | bytes 589832 | tf_op jit(solution)/shard_map/ppermute | solution.py:454
  11.1 0.5 collective-permute-start.3
  11.6 1.1 %more_partial.3 = (bf16[384,256]{1,0:T(8,128)(2,1)S(1)}, bf16[384,256]{1,0:T(8,128)(2,1)S(1)}, bf16[384,256]{1,0:T(8,128)(2,1)S(1)}, bf16[384,256]{1,0:T(8,128)(...) custom-call(bf16[384,768]{1,0:T(8,128)(2,1)S(1)} %get-tuple-element.36.scat_ref.refs_0_, ...), custom_call_target="tpu_custom_call" | custom-call | flops 905969664 | bytes 2359296 | tf_op jit(solution)/shard_map/more_partial/pallas_call | solution.py:140
  12.7 2.4 %collective-permute-start.4 = (bf16[384,256]{1,0:T(8,128)(2,1)S(1)}, bf16[384,256]{1,0:T(8,128)(2,1)S(1)}, u32[]{:S(2)}, u32[]{:S(2)}) collective-permute-start(bf16[384,256]{1,0:T(8,128)(2,1)S(1)} %get-tuple-element.47), channel_id=1, source_target_pairs={{0,12},{2,14},{4,0},{6,2},{8,4},{10,6},{12,8},{14,10},{1,13},{3,15... | collective-permute-start | bytes 589832 | tf_op jit(solution)/shard_map/ppermute | solution.py:454
  15.1 1.0 %collective-permute-start.6 = (bf16[384,256]{1,0:T(8,128)(2,1)S(1)}, bf16[384,256]{1,0:T(8,128)(2,1)S(1)}, u32[]{:S(2)}, u32[]{:S(2)}) collective-permute-start(bf16[384,256]{1,0:T(8,128)(2,1)S(1)} %get-tuple-element.49), channel_id=1, source_target_pairs={{0,2},{2,0},{4,6},{6,4},{8,10},{10,8},{12,14},{14,12},{1,3},{3,1},... | collective-permute-start | bytes 589832 | tf_op jit(solution)/shard_map/ppermute | solution.py:454
  16.1 0.2 collective-permute-done.2.refs_0_
  16.4 1.2 %collective-permute-start.7 = (bf16[384,256]{1,0:T(8,128)(2,1)S(1)}, bf16[384,256]{1,0:T(8,128)(2,1)S(1)}, u32[]{:S(2)}, u32[]{:S(2)}) collective-permute-start(bf16[384,256]{1,0:T(8,128)(2,1)S(1)} %get-tuple-element.50), channel_id=1, source_target_pairs={{0,4},{2,6},{4,8},{6,10},{8,12},{10,14},{12,0},{14,2},{1,5},{3,7},... | collective-permute-start | bytes 589832 | tf_op jit(solution)/shard_map/ppermute | solution.py:454
  17.6 3.4 %collective-permute-done.3.refs_1_ = bf16[384,256]{1,0:T(8,128)(2,1)S(1)} collective-permute-done((bf16[384,256]{1,0:T(8,128)(2,1)S(1)}, bf16[384,256]{1,0:T(8,128)(2,1)S(1)}, u32[]{:S(2)}, u32[]{:S(2)}) %collective-permute-start.3) | collective-permute-done | bytes 196640 | tf_op jit(solution)/shard_map/ppermute | solution.py:454
  21.0 2.8 %collective-permute-start.8 = (bf16[384,256]{1,0:T(8,128)(2,1)S(1)}, bf16[384,256]{1,0:T(8,128)(2,1)S(1)}, u32[]{:S(2)}, u32[]{:S(2)}) collective-permute-start(bf16[384,256]{1,0:T(8,128)(2,1)S(1)} %get-tuple-element.51), channel_id=1, source_target_pairs={{0,14},{2,12},{4,2},{6,0},{8,6},{10,4},{12,10},{14,8},{1,15},{3,13... | collective-permute-start | bytes 589832 | tf_op jit(solution)/shard_map/ppermute | solution.py:454
  23.9 6.1 %coefficients.1 = (f32[48,8,256]{2,1,0:T(8,128)S(1)}, f32[48,8,256]{2,1,0:T(8,128)S(1)}, f32[48,8,256]{2,1,0:T(8,128)S(1)}, f32[48,8,256]{2,1,0:T(8,128)S(1)}, f...) custom-call(f32[1,384]{1,0:T(1,128)S(1)} %reshape.19.gains_ref, ...), custom_call_target="tpu_custom_call" | custom-call | flops 786432 | bytes 16777216 | tf_op jit(solution)/shard_map/coefficients/pallas_call | solution.py:205
  29.9 0.0 collective-permute-done.4.refs_2_
  29.9 0.0 collective-permute-done.6.refs_4_
  30.0 0.0 collective-permute-done.7.refs_5_
  30.0 0.4 local_recurrence.1
  30.4 11.7 %all_to_all.5.got_ref = f32[8,8,256]{2,1,0:T(8,128)S(1)} all-to-all(f32[8,8,256]{2,1,0:T(8,128)S(1)} %get-tuple-element.58), channel_id=1, replica_groups=mesh['z'=4,'yh'=2,'x'=4,'yl'=2,'core'=2] {'z','yh'}, dimensions={0} | all-to-all | bytes 131072 | tf_op jit(solution)/shard_map/all_to_all | solution.py:464
  42.1 0.2 make_history.1
  42.4 1.2 %collective-permute-start.10 = (bf16[384,256]{1,0:T(8,128)(2,1)S(1)}, bf16[384,256]{1,0:T(8,128)(2,1)S(1)}, u32[]{:S(2)}, u32[]{:S(2)}) collective-permute-start(bf16[384,256]{1,0:T(8,128)(2,1)S(1)} %get-tuple-element.63.refs_2_), channel_id=1, source_target_pairs={{0,10},{2,8},{4,14},{6,12},{8,2},{10,0},{12,6},{14,4},{1,11},{3,9}... | collective-permute-start | bytes 589832 | tf_op jit(solution)/shard_map/ppermute | solution.py:466
  43.6 1.7 %collective-permute-start.9 = (bf16[384,256]{1,0:T(8,128)(2,1)S(1)}, bf16[384,256]{1,0:T(8,128)(2,1)S(1)}, u32[]{:S(2)}, u32[]{:S(2)}) collective-permute-start(bf16[384,256]{1,0:T(8,128)(2,1)S(1)} %get-tuple-element.63.refs_2_), channel_id=1, source_target_pairs={{0,2},{2,0},{4,6},{6,4},{8,10},{10,8},{12,14},{14,12},{1,3},{3,1},... | collective-permute-start | bytes 589832 | tf_op jit(solution)/shard_map/ppermute | solution.py:466
  45.3 1.3 %collective-permute-start.11 = (bf16[384,256]{1,0:T(8,128)(2,1)S(1)}, bf16[384,256]{1,0:T(8,128)(2,1)S(1)}, u32[]{:S(2)}, u32[]{:S(2)}) collective-permute-start(bf16[384,256]{1,0:T(8,128)(2,1)S(1)} %get-tuple-element.63.refs_2_), channel_id=1, source_target_pairs={{0,8},{2,10},{4,12},{6,14},{8,0},{10,2},{12,4},{14,6},{1,9},{3,11}... | collective-permute-start | bytes 589832 | tf_op jit(solution)/shard_map/ppermute | solution.py:466
  46.6 0.2 collective-permute-start.12
  46.8 2.6 %collective-permute-start.13 = (bf16[384,256]{1,0:T(8,128)(2,1)S(1)}, bf16[384,256]{1,0:T(8,128)(2,1)S(1)}, u32[]{:S(2)}, u32[]{:S(2)}) collective-permute-start(bf16[384,256]{1,0:T(8,128)(2,1)S(1)} %get-tuple-element.63.refs_2_), channel_id=1, source_target_pairs={{0,14},{2,12},{4,2},{6,0},{8,6},{10,4},{12,10},{14,8},{1,15},{3,13... | collective-permute-start | bytes 589832 | tf_op jit(solution)/shard_map/ppermute | solution.py:466
  49.5 0.0 collective-permute-done.10.refs_4_
  49.5 0.6 collective-permute-start.14
  50.0 5.4 %collective-permute-done.9.refs_3_ = bf16[384,256]{1,0:T(8,128)(2,1)S(1)} collective-permute-done((bf16[384,256]{1,0:T(8,128)(2,1)S(1)}, bf16[384,256]{1,0:T(8,128)(2,1)S(1)}, u32[]{:S(2)}, u32[]{:S(2)}) %collective-permute-start.9) | collective-permute-done | bytes 196640 | tf_op jit(solution)/shard_map/ppermute | solution.py:466
  55.5 2.1 %first_field.1 = (f32[384,2048]{1,0:T(8,128)S(1)}, f32[256,384]{1,0:T(8,128)}) custom-call(bf16[4096,2048]{1,0:T(8,128)(2,1)S(1)} %get-tuple-element.44.refs_0_, f32[384,256]{1,0:T(8,128)S(1)} %get-tuple-element.62.refs_1_, bf16[384,256]{1,0:T(8,128)(2,1)S(1)} %get-tuple-element.63.refs_2_, bf16[384,256]{1,0:T(8,128)(2,1)S(1)} %collective-permute-done.9.refs_3_, ...), custom_call_target="tpu_custom_call" | custom-call | flops 1500000000 | bytes 500000000 | tf_op jit(solution)/shard_map/first_field/pallas_call | solution.py:365
  57.5 10.2 %collective-permute-start.23 = (bf16[384,256]{1,0:T(8,128)(2,1)S(1)}, bf16[384,256]{1,0:T(8,128)(2,1)S(1)}, u32[]{:S(2)}, u32[]{:S(2)}) collective-permute-start(bf16[384,256]{1,0:T(8,128)(2,1)S(1)} %get-tuple-element.63.refs_2_), channel_id=1, source_target_pairs={{0,1},{1,0},{2,3},{3,2},{4,5},{5,4},{6,7},{7,6},{8,9},{9,8},{10,11... | collective-permute-start | bytes 589832 | tf_op jit(solution)/shard_map/ppermute | solution.py:478
  67.7 0.0 collective-permute-done.12.refs_3_
  67.7 1.4 %next_field.2.refs_1_ = f32[384,2048]{1,0:T(8,128)S(1)} custom-call(bf16[4096,2048]{1,0:T(8,128)(2,1)S(1)} %get-tuple-element.44.refs_0_, f32[384,2048]{1,0:T(8,128)S(1)} %get-tuple-element.65.refs_1_, bf16[384,256]{1,0:T(8,128)(2,1)S(1)} %collective-permute-done.11.refs_2_, bf16[384,256]{1,0:T(8,128)(2,1)S(1)} %collective-permute-done.12.refs_3_, ...), custom_call_target="tpu_custom_call" | custom-call | flops 1500000000 | bytes 500000000 | tf_op jit(solution)/shard_map/next_field/pallas_call | solution.py:387
  69.1 0.0 collective-permute-done.14.refs_2_
  69.1 0.1 collective-permute-start.21
  69.2 0.5 collective-permute-start.16
  69.7 0.1 collective-permute-start.17
  69.8 0.4 collective-permute-start.18
  70.2 0.1 collective-permute-start.19
  70.3 0.3 collective-permute-done.21.refs_7_
  70.6 0.1 collective-permute-start.20
  70.8 0.1 collective-permute-done.16.refs_2_
  70.9 0.2 collective-permute-start.22
  71.2 1.0 %next_field.3.refs_1_ = f32[384,2048]{1,0:T(8,128)S(1)} custom-call(bf16[4096,2048]{1,0:T(8,128)(2,1)S(1)} %get-tuple-element.44.refs_0_, f32[384,2048]{1,0:T(8,128)S(1)} %next_field.2.refs_1_, bf16[384,256]{1,0:T(8,128)(2,1)S(1)} %collective-permute-done.14.refs_2_, bf16[384,256]{1,0:T(8,128)(2,1)S(1)} %collective-permute-done.15.refs_3_), custom_call_target="tpu_custom_call" | custom-call | flops 1000000000 | bytes 500000000 | tf_op jit(solution)/shard_map/next_field/pallas_call | solution.py:387
  72.2 0.2 collective-permute-done.22.refs_8_
  72.4 4.2 %last_field.1 = bf16[384,2048]{1,0:T(8,128)(2,1)} custom-call(bf16[4096,2048]{1,0:T(8,128)(2,1)S(1)} %get-tuple-element.44.refs_0_, f32[384,2048]{1,0:T(8,128)S(1)} %next_field.3.refs_1_, bf16[384,256]{1,0:T(8,128)(2,1)S(1)} %collective-permute-done.16.refs_2_, bf16[384,256]{1,0:T(8,128)(2,1)S(1)} %collective-permute-done.17.refs_3_, ...), custom_call_target="tpu_custom_call" | custom-call | flops 4000000000 | bytes 500000000 | tf_op jit(solution)/shard_map/last_field/pallas_call | solution.py:418
  (20 shorter events, 0.1 us)
Async XLA Ops:
  4.6 2.1 %collective-permute-start = (bf16[2,384,256]{2,1,0:T(8,128)(2,1)S(1)}, bf16[2,384,256]{2,1,0:T(8,128)(2,1)S(1)}, u32[]{:S(2)}, u32[]{:S(2)}) collective-permute-start(bf16[2,384,256]{2,1,0:T(8,128)(2,1)S(1)} %get-tuple-element.38), channel_id=1, source_target_pairs={{0,1},{1,0},{2,3},{3,2},{4,5},{5,4},{6,7},{7,6},{8,9},{9,8},{10,11... | collective-permute-start | bytes 1179656 | tf_op jit(solution)/shard_map/ppermute | solution.py:446
  6.4 5.1 %copy-start = (f32[384]{0:T(512)S(1)}, f32[384]{0:T(512)}, u32[]{:S(2)}) copy-start(f32[384]{0:T(512)} %param.12) | copy-start | bytes 4612
  7.1 4.4 %collective-permute-start.1 = (bf16[6,384,256]{2,1,0:T(8,128)(2,1)S(1)}, bf16[6,384,256]{2,1,0:T(8,128)(2,1)S(1)}, u32[]{:S(2)}, u32[]{:S(2)}) collective-permute-start(bf16[6,384,256]{2,1,0:T(8,128)(2,1)S(1)} %rest_partial.1), channel_id=1, source_target_pairs={{0,1},{1,0},{2,3},{3,2},{4,5},{5,4},{6,7},{7,6},{8,9},{9,8},{10,11... | collective-permute-start | bytes 3538952 | tf_op jit(solution)/shard_map/ppermute | solution.py:450
  7.6 8.8 %collective-permute-start.2 = (bf16[384,256]{1,0:T(8,128)(2,1)S(1)}, bf16[384,256]{1,0:T(8,128)(2,1)S(1)}, u32[]{:S(2)}, u32[]{:S(2)}) collective-permute-start(bf16[384,256]{1,0:T(8,128)(2,1)S(1)} %get-tuple-element.45), channel_id=1, source_target_pairs={{0,10},{2,8},{4,14},{6,12},{8,2},{10,0},{12,6},{14,4},{1,11},{3,9}... | collective-permute-start | bytes 589832 | tf_op jit(solution)/shard_map/ppermute | solution.py:454
  11.1 9.9 %collective-permute-start.3 = (bf16[384,256]{1,0:T(8,128)(2,1)S(1)}, bf16[384,256]{1,0:T(8,128)(2,1)S(1)}, u32[]{:S(2)}, u32[]{:S(2)}) collective-permute-start(bf16[384,256]{1,0:T(8,128)(2,1)S(1)} %get-tuple-element.46), channel_id=1, source_target_pairs={{0,6},{2,4},{4,10},{6,8},{8,14},{10,12},{12,2},{14,0},{1,7},{3,5},... | collective-permute-start | bytes 589832 | tf_op jit(solution)/shard_map/ppermute | solution.py:454
  11.6 12.3 %copy-start.1 = (f32[256]{0:T(256)S(1)}, f32[256]{0:T(256)}, u32[]{:S(2)}) copy-start(f32[256]{0:T(256)} %param.11) | copy-start | bytes 3076
  11.6 12.3 %copy-start.2 = (f32[256]{0:T(256)S(1)}, f32[256]{0:T(256)}, u32[]{:S(2)}) copy-start(f32[256]{0:T(256)} %param.10) | copy-start | bytes 3076
  12.7 17.2 %collective-permute-start.4 = (bf16[384,256]{1,0:T(8,128)(2,1)S(1)}, bf16[384,256]{1,0:T(8,128)(2,1)S(1)}, u32[]{:S(2)}, u32[]{:S(2)}) collective-permute-start(bf16[384,256]{1,0:T(8,128)(2,1)S(1)} %get-tuple-element.47), channel_id=1, source_target_pairs={{0,12},{2,14},{4,0},{6,2},{8,4},{10,6},{12,8},{14,10},{1,13},{3,15... | collective-permute-start | bytes 589832 | tf_op jit(solution)/shard_map/ppermute | solution.py:454
  15.1 14.8 %collective-permute-start.5 = (bf16[384,256]{1,0:T(8,128)(2,1)S(1)}, bf16[384,256]{1,0:T(8,128)(2,1)S(1)}, u32[]{:S(2)}, u32[]{:S(2)}) collective-permute-start(bf16[384,256]{1,0:T(8,128)(2,1)S(1)} %get-tuple-element.48), channel_id=1, source_target_pairs={{0,8},{2,10},{4,12},{6,14},{8,0},{10,2},{12,4},{14,6},{1,9},{3,11}... | collective-permute-start | bytes 589832 | tf_op jit(solution)/shard_map/ppermute | solution.py:454
  15.1 14.8 %collective-permute-start.6 = (bf16[384,256]{1,0:T(8,128)(2,1)S(1)}, bf16[384,256]{1,0:T(8,128)(2,1)S(1)}, u32[]{:S(2)}, u32[]{:S(2)}) collective-permute-start(bf16[384,256]{1,0:T(8,128)(2,1)S(1)} %get-tuple-element.49), channel_id=1, source_target_pairs={{0,2},{2,0},{4,6},{6,4},{8,10},{10,8},{12,14},{14,12},{1,3},{3,1},... | collective-permute-start | bytes 589832 | tf_op jit(solution)/shard_map/ppermute | solution.py:454
  16.4 13.6 %collective-permute-start.7 = (bf16[384,256]{1,0:T(8,128)(2,1)S(1)}, bf16[384,256]{1,0:T(8,128)(2,1)S(1)}, u32[]{:S(2)}, u32[]{:S(2)}) collective-permute-start(bf16[384,256]{1,0:T(8,128)(2,1)S(1)} %get-tuple-element.50), channel_id=1, source_target_pairs={{0,4},{2,6},{4,8},{6,10},{8,12},{10,14},{12,0},{14,2},{1,5},{3,7},... | collective-permute-start | bytes 589832 | tf_op jit(solution)/shard_map/ppermute | solution.py:454
  21.0 9.0 %collective-permute-start.8 = (bf16[384,256]{1,0:T(8,128)(2,1)S(1)}, bf16[384,256]{1,0:T(8,128)(2,1)S(1)}, u32[]{:S(2)}, u32[]{:S(2)}) collective-permute-start(bf16[384,256]{1,0:T(8,128)(2,1)S(1)} %get-tuple-element.51), channel_id=1, source_target_pairs={{0,14},{2,12},{4,2},{6,0},{8,6},{10,4},{12,10},{14,8},{1,15},{3,13... | collective-permute-start | bytes 589832 | tf_op jit(solution)/shard_map/ppermute | solution.py:454
  42.4 7.1 %collective-permute-start.10 = (bf16[384,256]{1,0:T(8,128)(2,1)S(1)}, bf16[384,256]{1,0:T(8,128)(2,1)S(1)}, u32[]{:S(2)}, u32[]{:S(2)}) collective-permute-start(bf16[384,256]{1,0:T(8,128)(2,1)S(1)} %get-tuple-element.63.refs_2_), channel_id=1, source_target_pairs={{0,10},{2,8},{4,14},{6,12},{8,2},{10,0},{12,6},{14,4},{1,11},{3,9}... | collective-permute-start | bytes 589832 | tf_op jit(solution)/shard_map/ppermute | solution.py:466
  43.6 11.9 %collective-permute-start.9 = (bf16[384,256]{1,0:T(8,128)(2,1)S(1)}, bf16[384,256]{1,0:T(8,128)(2,1)S(1)}, u32[]{:S(2)}, u32[]{:S(2)}) collective-permute-start(bf16[384,256]{1,0:T(8,128)(2,1)S(1)} %get-tuple-element.63.refs_2_), channel_id=1, source_target_pairs={{0,2},{2,0},{4,6},{6,4},{8,10},{10,8},{12,14},{14,12},{1,3},{3,1},... | collective-permute-start | bytes 589832 | tf_op jit(solution)/shard_map/ppermute | solution.py:466
  45.3 12.2 %collective-permute-start.11 = (bf16[384,256]{1,0:T(8,128)(2,1)S(1)}, bf16[384,256]{1,0:T(8,128)(2,1)S(1)}, u32[]{:S(2)}, u32[]{:S(2)}) collective-permute-start(bf16[384,256]{1,0:T(8,128)(2,1)S(1)} %get-tuple-element.63.refs_2_), channel_id=1, source_target_pairs={{0,8},{2,10},{4,12},{6,14},{8,0},{10,2},{12,4},{14,6},{1,9},{3,11}... | collective-permute-start | bytes 589832 | tf_op jit(solution)/shard_map/ppermute | solution.py:466
  46.6 21.1 %collective-permute-start.12 = (bf16[384,256]{1,0:T(8,128)(2,1)S(1)}, bf16[384,256]{1,0:T(8,128)(2,1)S(1)}, u32[]{:S(2)}, u32[]{:S(2)}) collective-permute-start(bf16[384,256]{1,0:T(8,128)(2,1)S(1)} %get-tuple-element.63.refs_2_), channel_id=1, source_target_pairs={{0,4},{2,6},{4,8},{6,10},{8,12},{10,14},{12,0},{14,2},{1,5},{3,7},... | collective-permute-start | bytes 589832 | tf_op jit(solution)/shard_map/ppermute | solution.py:466
  46.8 20.9 %collective-permute-start.13 = (bf16[384,256]{1,0:T(8,128)(2,1)S(1)}, bf16[384,256]{1,0:T(8,128)(2,1)S(1)}, u32[]{:S(2)}, u32[]{:S(2)}) collective-permute-start(bf16[384,256]{1,0:T(8,128)(2,1)S(1)} %get-tuple-element.63.refs_2_), channel_id=1, source_target_pairs={{0,14},{2,12},{4,2},{6,0},{8,6},{10,4},{12,10},{14,8},{1,15},{3,13... | collective-permute-start | bytes 589832 | tf_op jit(solution)/shard_map/ppermute | solution.py:466
  49.5 19.6 %collective-permute-start.14 = (bf16[384,256]{1,0:T(8,128)(2,1)S(1)}, bf16[384,256]{1,0:T(8,128)(2,1)S(1)}, u32[]{:S(2)}, u32[]{:S(2)}) collective-permute-start(bf16[384,256]{1,0:T(8,128)(2,1)S(1)} %get-tuple-element.63.refs_2_), channel_id=1, source_target_pairs={{0,6},{2,4},{4,10},{6,8},{8,14},{10,12},{12,2},{14,0},{1,7},{3,5},... | collective-permute-start | bytes 589832 | tf_op jit(solution)/shard_map/ppermute | solution.py:466
  55.5 14.4 %collective-permute-start.15 = (bf16[384,256]{1,0:T(8,128)(2,1)S(1)}, bf16[384,256]{1,0:T(8,128)(2,1)S(1)}, u32[]{:S(2)}, u32[]{:S(2)}) collective-permute-start(bf16[384,256]{1,0:T(8,128)(2,1)S(1)} %get-tuple-element.63.refs_2_), channel_id=1, source_target_pairs={{0,12},{2,14},{4,0},{6,2},{8,4},{10,6},{12,8},{14,10},{1,13},{3,15... | collective-permute-start | bytes 589832 | tf_op jit(solution)/shard_map/ppermute | solution.py:466
  57.5 12.7 %collective-permute-start.23 = (bf16[384,256]{1,0:T(8,128)(2,1)S(1)}, bf16[384,256]{1,0:T(8,128)(2,1)S(1)}, u32[]{:S(2)}, u32[]{:S(2)}) collective-permute-start(bf16[384,256]{1,0:T(8,128)(2,1)S(1)} %get-tuple-element.63.refs_2_), channel_id=1, source_target_pairs={{0,1},{1,0},{2,3},{3,2},{4,5},{5,4},{6,7},{7,6},{8,9},{9,8},{10,11... | collective-permute-start | bytes 589832 | tf_op jit(solution)/shard_map/ppermute | solution.py:478
  69.1 1.5 %collective-permute-start.21 = (bf16[384,256]{1,0:T(8,128)(2,1)S(1)}, bf16[384,256]{1,0:T(8,128)(2,1)S(1)}, u32[]{:S(2)}, u32[]{:S(2)}) collective-permute-start(bf16[384,256]{1,0:T(8,128)(2,1)S(1)} %collective-permute-done.14.refs_2_), channel_id=1, source_target_pairs={{0,1},{1,0},{2,3},{3,2},{4,5},{5,4},{6,7},{7,6},{8,9},{9,8},{10,11... | collective-permute-start | bytes 589832 | tf_op jit(solution)/shard_map/ppermute | solution.py:478
  69.2 1.7 %collective-permute-start.16 = (bf16[384,256]{1,0:T(8,128)(2,1)S(1)}, bf16[384,256]{1,0:T(8,128)(2,1)S(1)}, u32[]{:S(2)}, u32[]{:S(2)}) collective-permute-start(bf16[384,256]{1,0:T(8,128)(2,1)S(1)} %collective-permute-done.11.refs_2_), channel_id=1, source_target_pairs={{0,1},{1,0},{2,3},{3,2},{4,5},{5,4},{6,7},{7,6},{8,9},{9,8},{10,11... | collective-permute-start | bytes 589832 | tf_op jit(solution)/shard_map/ppermute | solution.py:478
  69.7 2.4 %collective-permute-start.17 = (bf16[384,256]{1,0:T(8,128)(2,1)S(1)}, bf16[384,256]{1,0:T(8,128)(2,1)S(1)}, u32[]{:S(2)}, u32[]{:S(2)}) collective-permute-start(bf16[384,256]{1,0:T(8,128)(2,1)S(1)} %collective-permute-done.10.refs_4_), channel_id=1, source_target_pairs={{0,1},{1,0},{2,3},{3,2},{4,5},{5,4},{6,7},{7,6},{8,9},{9,8},{10,11... | collective-permute-start | bytes 589832 | tf_op jit(solution)/shard_map/ppermute | solution.py:478
  69.8 2.4 %collective-permute-start.18 = (bf16[384,256]{1,0:T(8,128)(2,1)S(1)}, bf16[384,256]{1,0:T(8,128)(2,1)S(1)}, u32[]{:S(2)}, u32[]{:S(2)}) collective-permute-start(bf16[384,256]{1,0:T(8,128)(2,1)S(1)} %collective-permute-done.12.refs_3_), channel_id=1, source_target_pairs={{0,1},{1,0},{2,3},{3,2},{4,5},{5,4},{6,7},{7,6},{8,9},{9,8},{10,11... | collective-permute-start | bytes 589832 | tf_op jit(solution)/shard_map/ppermute | solution.py:478
  70.2 1.9 %collective-permute-start.19 = (bf16[384,256]{1,0:T(8,128)(2,1)S(1)}, bf16[384,256]{1,0:T(8,128)(2,1)S(1)}, u32[]{:S(2)}, u32[]{:S(2)}) collective-permute-start(bf16[384,256]{1,0:T(8,128)(2,1)S(1)} %collective-permute-done.9.refs_3_), channel_id=1, source_target_pairs={{0,1},{1,0},{2,3},{3,2},{4,5},{5,4},{6,7},{7,6},{8,9},{9,8},{10,11... | collective-permute-start | bytes 589832 | tf_op jit(solution)/shard_map/ppermute | solution.py:478
  70.6 1.5 %collective-permute-start.20 = (bf16[384,256]{1,0:T(8,128)(2,1)S(1)}, bf16[384,256]{1,0:T(8,128)(2,1)S(1)}, u32[]{:S(2)}, u32[]{:S(2)}) collective-permute-start(bf16[384,256]{1,0:T(8,128)(2,1)S(1)} %collective-permute-done.13.refs_4_), channel_id=1, source_target_pairs={{0,1},{1,0},{2,3},{3,2},{4,5},{5,4},{6,7},{7,6},{8,9},{9,8},{10,11... | collective-permute-start | bytes 589832 | tf_op jit(solution)/shard_map/ppermute | solution.py:478
  70.9 1.4 %collective-permute-start.22 = (bf16[384,256]{1,0:T(8,128)(2,1)S(1)}, bf16[384,256]{1,0:T(8,128)(2,1)S(1)}, u32[]{:S(2)}, u32[]{:S(2)}) collective-permute-start(bf16[384,256]{1,0:T(8,128)(2,1)S(1)} %collective-permute-done.15.refs_3_), channel_id=1, source_target_pairs={{0,1},{1,0},{2,3},{3,2},{4,5},{5,4},{6,7},{7,6},{8,9},{9,8},{10,11... | collective-permute-start | bytes 589832 | tf_op jit(solution)/shard_map/ppermute | solution.py:478

commit v7 on v6

--- a/solution.py
+++ b/solution.py
@@ -16,7 +16,7 @@
 DEEP = 256
 EARLY = 2
 FLOPS = 500 * 1000 * 1000
-STEPS = ((2, 1), (1, 1), (3, 0), (2, 0), (0, 1), (1, 0), (3, 1), (0, 0))
+STEPS = ((2, 1), (3, 1), (1, 0), (2, 0), (0, 1), (3, 0), (1, 1), (0, 0))
 SPREAD = ((2, 0), (2, 1), (1, 0), (0, 1), (3, 1), (1, 1), (3, 0))
 
 

time: 76.9 us -> 76.7 us (level)
  the two profiles are of different devices: /device:TPU:17 before, /device:TPU:1 now
where the time goes in v7:
time: 76.7 us; the launch traced here: 76.5 us
  starting transfers between devices  28.3 us (37%)
  Pallas kernels  21.9 us (29%)
  blocking collectives  13.6 us (18%)
  waiting for transfers between devices  11.7 us (15%)
  between operations  0.96 us (1%)
    all_to_all x1, blocking collectives, body(): states = lax.all_to_all(payload, TM, 0, 0)  13.6 us
    ppermute x7, starting transfers between devices, body(): lax.ppermute(part, XY, step_pairs(*step))  12.7 us
    ppermute x7, waiting for transfers between devices, body(): near = [lax.ppermute(mine, XY, step_pairs(*step)) for step in SPREAD]  8.55 us
    ppermute x7, starting transfers between devices, body(): near = [lax.ppermute(mine, XY, step_pairs(*step)) for step in SPREAD]  7.76 us
    pallas_call x1, Pallas kernels, coefficients(): pl.pallas_call(coef_kernel, out_shape=(full, full, full, full, jax.ShapeD...  6.06 us
    ppermute x8, starting transfers between devices, body(): far = [lax.ppermute(part, 'core', pair) for part in sent]  5.86 us
    pallas_call x1, Pallas kernels, last_field(): pl.pallas_call(lambda *refs: last_kernel(whose, *refs), out_shape=jax.Sha...  4.19 us
    pallas_call x1, Pallas kernels, open_partial(): pl.pallas_call(open_kernel, out_shape=(pltpu.VMEM((steps, rows), BF16), j...  3.91 us
  transfers between devices with their start and end apart: 24, of which 9 were waited for; matrix products, arithmetic and copies ran while one was open for 0% of the time, Pallas kernels for 17%

profile of v7, /device:TPU:1, one launch (start us, length us, event | category | flops | bytes accessed | tf_op | source)
XLA Modules:
  0.0 76.5 jit_solution(14496346729138505112)
XLA Ops:
  0.6 3.9 %open_partial.1 = (bf16[384,768]{1,0:T(8,128)(2,1)S(1)}, bf16[2,384,256]{2,1,0:T(8,128)(2,1)S(1)}, bf16[768,4096]{1,0:T(8,128)(2,1)S(1)}) custom-call(s32[1,512]{1,0:T(1,128)} %bitcast.7, bf16[384,512]{1,0:T(8,128)(2,1)} %loads_hbm.1, bf16[768,4096]{1,0:T(8,128)(2,1)} %phi_hbm.1), custom_call_target="tpu_custom_call" | custom-call | flops 603979776 | bytes 6291456 | tf_op jit(solution)/shard_map/open_partial/pallas_call | solution.py:93
  4.6 1.5 %collective-permute-start = (bf16[2,384,256]{2,1,0:T(8,128)(2,1)S(1)}, bf16[2,384,256]{2,1,0:T(8,128)(2,1)S(1)}, u32[]{:S(2)}, u32[]{:S(2)}) collective-permute-start(bf16[2,384,256]{2,1,0:T(8,128)(2,1)S(1)} %get-tuple-element.38), channel_id=1, source_target_pairs={{0,1},{1,0},{2,3},{3,2},{4,5},{5,4},{6,7},{7,6},{8,9},{9,8},{10,11... | collective-permute-start | bytes 1179656 | tf_op jit(solution)/shard_map/ppermute | solution.py:446
  6.0 1.1 %rest_partial.1 = bf16[6,384,256]{2,1,0:T(8,128)(2,1)S(1)} custom-call(bf16[384,768]{1,0:T(8,128)(2,1)S(1)} %get-tuple-element.36.scat_ref.refs_0_, bf16[768,4096]{1,0:T(8,128)(2,1)S(1)} %get-tuple-element.37.phi_ref.refs_1_), custom_call_target="tpu_custom_call" | custom-call | flops 603979776 | bytes 1572864 | tf_op jit(solution)/shard_map/rest_partial/pallas_call | solution.py:121
  7.2 0.0 copy-start
  7.2 0.2 collective-permute-done.refs_2_
  7.4 0.5 more_partial.2
  7.9 0.5 collective-permute-start.1
  8.3 3.8 %collective-permute-start.2 = (bf16[384,256]{1,0:T(8,128)(2,1)S(1)}, bf16[384,256]{1,0:T(8,128)(2,1)S(1)}, u32[]{:S(2)}, u32[]{:S(2)}) collective-permute-start(bf16[384,256]{1,0:T(8,128)(2,1)S(1)} %get-tuple-element.45), channel_id=1, source_target_pairs={{0,10},{2,8},{4,14},{6,12},{8,2},{10,0},{12,6},{14,4},{1,11},{3,9}... | collective-permute-start | bytes 589832 | tf_op jit(solution)/shard_map/ppermute | solution.py:454
  12.2 0.7 collective-permute-start.3
  12.9 0.0 collective-permute-done.1.refs_2_
  13.0 1.1 %more_partial.3 = (bf16[384,256]{1,0:T(8,128)(2,1)S(1)}, bf16[384,256]{1,0:T(8,128)(2,1)S(1)}, bf16[384,256]{1,0:T(8,128)(2,1)S(1)}, bf16[384,256]{1,0:T(8,128)(...) custom-call(bf16[384,768]{1,0:T(8,128)(2,1)S(1)} %get-tuple-element.36.scat_ref.refs_0_, ...), custom_call_target="tpu_custom_call" | custom-call | flops 905969664 | bytes 2359296 | tf_op jit(solution)/shard_map/more_partial/pallas_call | solution.py:140
  14.1 0.7 collective-permute-start.4
  14.8 1.0 %collective-permute-start.5 = (bf16[384,256]{1,0:T(8,128)(2,1)S(1)}, bf16[384,256]{1,0:T(8,128)(2,1)S(1)}, u32[]{:S(2)}, u32[]{:S(2)}) collective-permute-start(bf16[384,256]{1,0:T(8,128)(2,1)S(1)} %get-tuple-element.48), channel_id=1, source_target_pairs={{0,8},{2,10},{4,12},{6,14},{8,0},{10,2},{12,4},{14,6},{1,9},{3,11}... | collective-permute-start | bytes 589832 | tf_op jit(solution)/shard_map/ppermute | solution.py:454
  15.7 1.3 %collective-permute-start.6 = (bf16[384,256]{1,0:T(8,128)(2,1)S(1)}, bf16[384,256]{1,0:T(8,128)(2,1)S(1)}, u32[]{:S(2)}, u32[]{:S(2)}) collective-permute-start(bf16[384,256]{1,0:T(8,128)(2,1)S(1)} %get-tuple-element.49), channel_id=1, source_target_pairs={{0,2},{2,0},{4,6},{6,4},{8,10},{10,8},{12,14},{14,12},{1,3},{3,1},... | collective-permute-start | bytes 589832 | tf_op jit(solution)/shard_map/ppermute | solution.py:454
  17.0 0.1 collective-permute-done.2.refs_0_
  17.1 2.6 %collective-permute-start.7 = (bf16[384,256]{1,0:T(8,128)(2,1)S(1)}, bf16[384,256]{1,0:T(8,128)(2,1)S(1)}, u32[]{:S(2)}, u32[]{:S(2)}) collective-permute-start(bf16[384,256]{1,0:T(8,128)(2,1)S(1)} %get-tuple-element.50), channel_id=1, source_target_pairs={{0,12},{2,14},{4,0},{6,2},{8,4},{10,6},{12,8},{14,10},{1,13},{3,15... | collective-permute-start | bytes 589832 | tf_op jit(solution)/shard_map/ppermute | solution.py:454
  19.7 1.9 %collective-permute-done.3.refs_1_ = bf16[384,256]{1,0:T(8,128)(2,1)S(1)} collective-permute-done((bf16[384,256]{1,0:T(8,128)(2,1)S(1)}, bf16[384,256]{1,0:T(8,128)(2,1)S(1)}, u32[]{:S(2)}, u32[]{:S(2)}) %collective-permute-start.3) | collective-permute-done | bytes 196640 | tf_op jit(solution)/shard_map/ppermute | solution.py:454
  21.6 2.6 %collective-permute-start.8 = (bf16[384,256]{1,0:T(8,128)(2,1)S(1)}, bf16[384,256]{1,0:T(8,128)(2,1)S(1)}, u32[]{:S(2)}, u32[]{:S(2)}) collective-permute-start(bf16[384,256]{1,0:T(8,128)(2,1)S(1)} %get-tuple-element.51), channel_id=1, source_target_pairs={{0,6},{2,4},{4,10},{6,8},{8,14},{10,12},{12,2},{14,0},{1,7},{3,5},... | collective-permute-start | bytes 589832 | tf_op jit(solution)/shard_map/ppermute | solution.py:454
  24.2 6.1 %coefficients.1 = (f32[48,8,256]{2,1,0:T(8,128)S(1)}, f32[48,8,256]{2,1,0:T(8,128)S(1)}, f32[48,8,256]{2,1,0:T(8,128)S(1)}, f32[48,8,256]{2,1,0:T(8,128)S(1)}, f...) custom-call(f32[1,384]{1,0:T(1,128)S(1)} %reshape.19.gains_ref, ...), custom_call_target="tpu_custom_call" | custom-call | flops 786432 | bytes 16777216 | tf_op jit(solution)/shard_map/coefficients/pallas_call | solution.py:205
  30.3 0.0 collective-permute-done.4.refs_2_
  30.3 0.0 collective-permute-done.7.refs_5_
  30.3 0.5 collective-permute-done.8.refs_6_
  30.8 0.4 local_recurrence.1
  31.3 13.6 %all_to_all.5.got_ref = f32[8,8,256]{2,1,0:T(8,128)S(1)} all-to-all(f32[8,8,256]{2,1,0:T(8,128)S(1)} %get-tuple-element.58), channel_id=1, replica_groups=mesh['z'=4,'yh'=2,'x'=4,'yl'=2,'core'=2] {'z','yh'}, dimensions={0} | all-to-all | bytes 131072 | tf_op jit(solution)/shard_map/all_to_all | solution.py:464
  44.9 0.2 make_history.1
  45.1 2.3 %collective-permute-start.10 = (bf16[384,256]{1,0:T(8,128)(2,1)S(1)}, bf16[384,256]{1,0:T(8,128)(2,1)S(1)}, u32[]{:S(2)}, u32[]{:S(2)}) collective-permute-start(bf16[384,256]{1,0:T(8,128)(2,1)S(1)} %get-tuple-element.63.refs_2_), channel_id=1, source_target_pairs={{0,10},{2,8},{4,14},{6,12},{8,2},{10,0},{12,6},{14,4},{1,11},{3,9}... | collective-permute-start | bytes 589832 | tf_op jit(solution)/shard_map/ppermute | solution.py:466
  47.4 1.6 %collective-permute-start.9 = (bf16[384,256]{1,0:T(8,128)(2,1)S(1)}, bf16[384,256]{1,0:T(8,128)(2,1)S(1)}, u32[]{:S(2)}, u32[]{:S(2)}) collective-permute-start(bf16[384,256]{1,0:T(8,128)(2,1)S(1)} %get-tuple-element.63.refs_2_), channel_id=1, source_target_pairs={{0,2},{2,0},{4,6},{6,4},{8,10},{10,8},{12,14},{14,12},{1,3},{3,1},... | collective-permute-start | bytes 589832 | tf_op jit(solution)/shard_map/ppermute | solution.py:466
  49.0 0.4 collective-permute-start.11
  49.3 0.9 %collective-permute-start.12 = (bf16[384,256]{1,0:T(8,128)(2,1)S(1)}, bf16[384,256]{1,0:T(8,128)(2,1)S(1)}, u32[]{:S(2)}, u32[]{:S(2)}) collective-permute-start(bf16[384,256]{1,0:T(8,128)(2,1)S(1)} %get-tuple-element.63.refs_2_), channel_id=1, source_target_pairs={{0,4},{2,6},{4,8},{6,10},{8,12},{10,14},{12,0},{14,2},{1,5},{3,7},... | collective-permute-start | bytes 589832 | tf_op jit(solution)/shard_map/ppermute | solution.py:466
  50.2 1.8 %collective-permute-start.13 = (bf16[384,256]{1,0:T(8,128)(2,1)S(1)}, bf16[384,256]{1,0:T(8,128)(2,1)S(1)}, u32[]{:S(2)}, u32[]{:S(2)}) collective-permute-start(bf16[384,256]{1,0:T(8,128)(2,1)S(1)} %get-tuple-element.63.refs_2_), channel_id=1, source_target_pairs={{0,14},{2,12},{4,2},{6,0},{8,6},{10,4},{12,10},{14,8},{1,15},{3,13... | collective-permute-start | bytes 589832 | tf_op jit(solution)/shard_map/ppermute | solution.py:466
  52.0 0.3 collective-permute-done.10.refs_4_
  52.2 0.9 %collective-permute-start.14 = (bf16[384,256]{1,0:T(8,128)(2,1)S(1)}, bf16[384,256]{1,0:T(8,128)(2,1)S(1)}, u32[]{:S(2)}, u32[]{:S(2)}) collective-permute-start(bf16[384,256]{1,0:T(8,128)(2,1)S(1)} %get-tuple-element.63.refs_2_), channel_id=1, source_target_pairs={{0,6},{2,4},{4,10},{6,8},{8,14},{10,12},{12,2},{14,0},{1,7},{3,5},... | collective-permute-start | bytes 589832 | tf_op jit(solution)/shard_map/ppermute | solution.py:466
  53.1 5.3 %collective-permute-done.9.refs_3_ = bf16[384,256]{1,0:T(8,128)(2,1)S(1)} collective-permute-done((bf16[384,256]{1,0:T(8,128)(2,1)S(1)}, bf16[384,256]{1,0:T(8,128)(2,1)S(1)}, u32[]{:S(2)}, u32[]{:S(2)}) %collective-permute-start.9) | collective-permute-done | bytes 196640 | tf_op jit(solution)/shard_map/ppermute | solution.py:466
  58.4 2.1 %first_field.1 = (f32[384,2048]{1,0:T(8,128)S(1)}, f32[256,384]{1,0:T(8,128)}) custom-call(bf16[4096,2048]{1,0:T(8,128)(2,1)S(1)} %get-tuple-element.44.refs_0_, f32[384,256]{1,0:T(8,128)S(1)} %get-tuple-element.62.refs_1_, bf16[384,256]{1,0:T(8,128)(2,1)S(1)} %get-tuple-element.63.refs_2_, bf16[384,256]{1,0:T(8,128)(2,1)S(1)} %collective-permute-done.9.refs_3_, ...), custom_call_target="tpu_custom_call" | custom-call | flops 1500000000 | bytes 500000000 | tf_op jit(solution)/shard_map/first_field/pallas_call | solution.py:365
  60.5 2.8 %collective-permute-start.23 = (bf16[384,256]{1,0:T(8,128)(2,1)S(1)}, bf16[384,256]{1,0:T(8,128)(2,1)S(1)}, u32[]{:S(2)}, u32[]{:S(2)}) collective-permute-start(bf16[384,256]{1,0:T(8,128)(2,1)S(1)} %get-tuple-element.63.refs_2_), channel_id=1, source_target_pairs={{0,1},{1,0},{2,3},{3,2},{4,5},{5,4},{6,7},{7,6},{8,9},{9,8},{10,11... | collective-permute-start | bytes 589832 | tf_op jit(solution)/shard_map/ppermute | solution.py:478
  63.3 1.4 %next_field.2.refs_1_ = f32[384,2048]{1,0:T(8,128)S(1)} custom-call(bf16[4096,2048]{1,0:T(8,128)(2,1)S(1)} %get-tuple-element.44.refs_0_, f32[384,2048]{1,0:T(8,128)S(1)} %get-tuple-element.65.refs_1_, bf16[384,256]{1,0:T(8,128)(2,1)S(1)} %collective-permute-done.11.refs_2_, bf16[384,256]{1,0:T(8,128)(2,1)S(1)} %collective-permute-done.12.refs_3_, ...), custom_call_target="tpu_custom_call" | custom-call | flops 1500000000 | bytes 500000000 | tf_op jit(solution)/shard_map/next_field/pallas_call | solution.py:387
  64.7 3.0 %collective-permute-done.14.refs_2_ = bf16[384,256]{1,0:T(8,128)(2,1)S(1)} collective-permute-done((bf16[384,256]{1,0:T(8,128)(2,1)S(1)}, bf16[384,256]{1,0:T(8,128)(2,1)S(1)}, u32[]{:S(2)}, u32[]{:S(2)}) %collective-permute-start.14) | collective-permute-done | bytes 196640 | tf_op jit(solution)/shard_map/ppermute | solution.py:466
  67.7 1.1 %collective-permute-start.21 = (bf16[384,256]{1,0:T(8,128)(2,1)S(1)}, bf16[384,256]{1,0:T(8,128)(2,1)S(1)}, u32[]{:S(2)}, u32[]{:S(2)}) collective-permute-start(bf16[384,256]{1,0:T(8,128)(2,1)S(1)} %collective-permute-done.14.refs_2_), channel_id=1, source_target_pairs={{0,1},{1,0},{2,3},{3,2},{4,5},{5,4},{6,7},{7,6},{8,9},{9,8},{10,11... | collective-permute-start | bytes 589832 | tf_op jit(solution)/shard_map/ppermute | solution.py:478
  68.8 0.0 collective-permute-start.16
  68.9 0.5 collective-permute-start.17
  69.4 0.8 %collective-permute-start.18 = (bf16[384,256]{1,0:T(8,128)(2,1)S(1)}, bf16[384,256]{1,0:T(8,128)(2,1)S(1)}, u32[]{:S(2)}, u32[]{:S(2)}) collective-permute-start(bf16[384,256]{1,0:T(8,128)(2,1)S(1)} %collective-permute-done.12.refs_3_), channel_id=1, source_target_pairs={{0,1},{1,0},{2,3},{3,2},{4,5},{5,4},{6,7},{7,6},{8,9},{9,8},{10,11... | collective-permute-start | bytes 589832 | tf_op jit(solution)/shard_map/ppermute | solution.py:478
  70.2 0.0 collective-permute-start.19
  70.2 0.5 collective-permute-start.20
  70.7 0.1 collective-permute-start.22
  70.8 1.0 %next_field.3.refs_1_ = f32[384,2048]{1,0:T(8,128)S(1)} custom-call(bf16[4096,2048]{1,0:T(8,128)(2,1)S(1)} %get-tuple-element.44.refs_0_, f32[384,2048]{1,0:T(8,128)S(1)} %next_field.2.refs_1_, bf16[384,256]{1,0:T(8,128)(2,1)S(1)} %collective-permute-done.14.refs_2_, bf16[384,256]{1,0:T(8,128)(2,1)S(1)} %collective-permute-done.15.refs_3_), custom_call_target="tpu_custom_call" | custom-call | flops 1000000000 | bytes 500000000 | tf_op jit(solution)/shard_map/next_field/pallas_call | solution.py:387
  71.8 0.1 collective-permute-done.20.refs_6_
  71.9 0.3 collective-permute-done.22.refs_8_
  72.2 4.2 %last_field.1 = bf16[384,2048]{1,0:T(8,128)(2,1)} custom-call(bf16[4096,2048]{1,0:T(8,128)(2,1)S(1)} %get-tuple-element.44.refs_0_, f32[384,2048]{1,0:T(8,128)S(1)} %next_field.3.refs_1_, bf16[384,256]{1,0:T(8,128)(2,1)S(1)} %collective-permute-done.16.refs_2_, bf16[384,256]{1,0:T(8,128)(2,1)S(1)} %collective-permute-done.17.refs_3_, ...), custom_call_target="tpu_custom_call" | custom-call | flops 4000000000 | bytes 500000000 | tf_op jit(solution)/shard_map/last_field/pallas_call | solution.py:418
  (20 shorter events, 0.1 us)
Async XLA Ops:
  4.6 2.8 %collective-permute-start = (bf16[2,384,256]{2,1,0:T(8,128)(2,1)S(1)}, bf16[2,384,256]{2,1,0:T(8,128)(2,1)S(1)}, u32[]{:S(2)}, u32[]{:S(2)}) collective-permute-start(bf16[2,384,256]{2,1,0:T(8,128)(2,1)S(1)} %get-tuple-element.38), channel_id=1, source_target_pairs={{0,1},{1,0},{2,3},{3,2},{4,5},{5,4},{6,7},{7,6},{8,9},{9,8},{10,11... | collective-permute-start | bytes 1179656 | tf_op jit(solution)/shard_map/ppermute | solution.py:446
  7.2 5.8 %copy-start = (f32[384]{0:T(512)S(1)}, f32[384]{0:T(512)}, u32[]{:S(2)}) copy-start(f32[384]{0:T(512)} %param.12) | copy-start | bytes 4612
  7.9 5.1 %collective-permute-start.1 = (bf16[6,384,256]{2,1,0:T(8,128)(2,1)S(1)}, bf16[6,384,256]{2,1,0:T(8,128)(2,1)S(1)}, u32[]{:S(2)}, u32[]{:S(2)}) collective-permute-start(bf16[6,384,256]{2,1,0:T(8,128)(2,1)S(1)} %rest_partial.1), channel_id=1, source_target_pairs={{0,1},{1,0},{2,3},{3,2},{4,5},{5,4},{6,7},{7,6},{8,9},{9,8},{10,11... | collective-permute-start | bytes 3538952 | tf_op jit(solution)/shard_map/ppermute | solution.py:450
  8.3 8.8 %collective-permute-start.2 = (bf16[384,256]{1,0:T(8,128)(2,1)S(1)}, bf16[384,256]{1,0:T(8,128)(2,1)S(1)}, u32[]{:S(2)}, u32[]{:S(2)}) collective-permute-start(bf16[384,256]{1,0:T(8,128)(2,1)S(1)} %get-tuple-element.45), channel_id=1, source_target_pairs={{0,10},{2,8},{4,14},{6,12},{8,2},{10,0},{12,6},{14,4},{1,11},{3,9}... | collective-permute-start | bytes 589832 | tf_op jit(solution)/shard_map/ppermute | solution.py:454
  12.2 9.4 %collective-permute-start.3 = (bf16[384,256]{1,0:T(8,128)(2,1)S(1)}, bf16[384,256]{1,0:T(8,128)(2,1)S(1)}, u32[]{:S(2)}, u32[]{:S(2)}) collective-permute-start(bf16[384,256]{1,0:T(8,128)(2,1)S(1)} %get-tuple-element.46), channel_id=1, source_target_pairs={{0,14},{2,12},{4,2},{6,0},{8,6},{10,4},{12,10},{14,8},{1,15},{3,13... | collective-permute-start | bytes 589832 | tf_op jit(solution)/shard_map/ppermute | solution.py:454
  12.9 11.2 %copy-start.1 = (f32[256]{0:T(256)S(1)}, f32[256]{0:T(256)}, u32[]{:S(2)}) copy-start(f32[256]{0:T(256)} %param.11) | copy-start | bytes 3076
  12.9 11.2 %copy-start.2 = (f32[256]{0:T(256)S(1)}, f32[256]{0:T(256)}, u32[]{:S(2)}) copy-start(f32[256]{0:T(256)} %param.10) | copy-start | bytes 3076
  14.1 16.2 %collective-permute-start.4 = (bf16[384,256]{1,0:T(8,128)(2,1)S(1)}, bf16[384,256]{1,0:T(8,128)(2,1)S(1)}, u32[]{:S(2)}, u32[]{:S(2)}) collective-permute-start(bf16[384,256]{1,0:T(8,128)(2,1)S(1)} %get-tuple-element.47), channel_id=1, source_target_pairs={{0,4},{2,6},{4,8},{6,10},{8,12},{10,14},{12,0},{14,2},{1,5},{3,7},... | collective-permute-start | bytes 589832 | tf_op jit(solution)/shard_map/ppermute | solution.py:454
  14.8 15.5 %collective-permute-start.5 = (bf16[384,256]{1,0:T(8,128)(2,1)S(1)}, bf16[384,256]{1,0:T(8,128)(2,1)S(1)}, u32[]{:S(2)}, u32[]{:S(2)}) collective-permute-start(bf16[384,256]{1,0:T(8,128)(2,1)S(1)} %get-tuple-element.48), channel_id=1, source_target_pairs={{0,8},{2,10},{4,12},{6,14},{8,0},{10,2},{12,4},{14,6},{1,9},{3,11}... | collective-permute-start | bytes 589832 | tf_op jit(solution)/shard_map/ppermute | solution.py:454
  15.7 14.5 %collective-permute-start.6 = (bf16[384,256]{1,0:T(8,128)(2,1)S(1)}, bf16[384,256]{1,0:T(8,128)(2,1)S(1)}, u32[]{:S(2)}, u32[]{:S(2)}) collective-permute-start(bf16[384,256]{1,0:T(8,128)(2,1)S(1)} %get-tuple-element.49), channel_id=1, source_target_pairs={{0,2},{2,0},{4,6},{6,4},{8,10},{10,8},{12,14},{14,12},{1,3},{3,1},... | collective-permute-start | bytes 589832 | tf_op jit(solution)/shard_map/ppermute | solution.py:454
  17.1 13.2 %collective-permute-start.7 = (bf16[384,256]{1,0:T(8,128)(2,1)S(1)}, bf16[384,256]{1,0:T(8,128)(2,1)S(1)}, u32[]{:S(2)}, u32[]{:S(2)}) collective-permute-start(bf16[384,256]{1,0:T(8,128)(2,1)S(1)} %get-tuple-element.50), channel_id=1, source_target_pairs={{0,12},{2,14},{4,0},{6,2},{8,4},{10,6},{12,8},{14,10},{1,13},{3,15... | collective-permute-start | bytes 589832 | tf_op jit(solution)/shard_map/ppermute | solution.py:454
  21.6 9.3 %collective-permute-start.8 = (bf16[384,256]{1,0:T(8,128)(2,1)S(1)}, bf16[384,256]{1,0:T(8,128)(2,1)S(1)}, u32[]{:S(2)}, u32[]{:S(2)}) collective-permute-start(bf16[384,256]{1,0:T(8,128)(2,1)S(1)} %get-tuple-element.51), channel_id=1, source_target_pairs={{0,6},{2,4},{4,10},{6,8},{8,14},{10,12},{12,2},{14,0},{1,7},{3,5},... | collective-permute-start | bytes 589832 | tf_op jit(solution)/shard_map/ppermute | solution.py:454
  45.1 7.1 %collective-permute-start.10 = (bf16[384,256]{1,0:T(8,128)(2,1)S(1)}, bf16[384,256]{1,0:T(8,128)(2,1)S(1)}, u32[]{:S(2)}, u32[]{:S(2)}) collective-permute-start(bf16[384,256]{1,0:T(8,128)(2,1)S(1)} %get-tuple-element.63.refs_2_), channel_id=1, source_target_pairs={{0,10},{2,8},{4,14},{6,12},{8,2},{10,0},{12,6},{14,4},{1,11},{3,9}... | collective-permute-start | bytes 589832 | tf_op jit(solution)/shard_map/ppermute | solution.py:466
  47.4 11.0 %collective-permute-start.9 = (bf16[384,256]{1,0:T(8,128)(2,1)S(1)}, bf16[384,256]{1,0:T(8,128)(2,1)S(1)}, u32[]{:S(2)}, u32[]{:S(2)}) collective-permute-start(bf16[384,256]{1,0:T(8,128)(2,1)S(1)} %get-tuple-element.63.refs_2_), channel_id=1, source_target_pairs={{0,2},{2,0},{4,6},{6,4},{8,10},{10,8},{12,14},{14,12},{1,3},{3,1},... | collective-permute-start | bytes 589832 | tf_op jit(solution)/shard_map/ppermute | solution.py:466
  49.0 11.5 %collective-permute-start.11 = (bf16[384,256]{1,0:T(8,128)(2,1)S(1)}, bf16[384,256]{1,0:T(8,128)(2,1)S(1)}, u32[]{:S(2)}, u32[]{:S(2)}) collective-permute-start(bf16[384,256]{1,0:T(8,128)(2,1)S(1)} %get-tuple-element.63.refs_2_), channel_id=1, source_target_pairs={{0,8},{2,10},{4,12},{6,14},{8,0},{10,2},{12,4},{14,6},{1,9},{3,11}... | collective-permute-start | bytes 589832 | tf_op jit(solution)/shard_map/ppermute | solution.py:466
  49.3 13.9 %collective-permute-start.12 = (bf16[384,256]{1,0:T(8,128)(2,1)S(1)}, bf16[384,256]{1,0:T(8,128)(2,1)S(1)}, u32[]{:S(2)}, u32[]{:S(2)}) collective-permute-start(bf16[384,256]{1,0:T(8,128)(2,1)S(1)} %get-tuple-element.63.refs_2_), channel_id=1, source_target_pairs={{0,4},{2,6},{4,8},{6,10},{8,12},{10,14},{12,0},{14,2},{1,5},{3,7},... | collective-permute-start | bytes 589832 | tf_op jit(solution)/shard_map/ppermute | solution.py:466
  50.2 13.1 %collective-permute-start.13 = (bf16[384,256]{1,0:T(8,128)(2,1)S(1)}, bf16[384,256]{1,0:T(8,128)(2,1)S(1)}, u32[]{:S(2)}, u32[]{:S(2)}) collective-permute-start(bf16[384,256]{1,0:T(8,128)(2,1)S(1)} %get-tuple-element.63.refs_2_), channel_id=1, source_target_pairs={{0,14},{2,12},{4,2},{6,0},{8,6},{10,4},{12,10},{14,8},{1,15},{3,13... | collective-permute-start | bytes 589832 | tf_op jit(solution)/shard_map/ppermute | solution.py:466
  52.2 15.5 %collective-permute-start.14 = (bf16[384,256]{1,0:T(8,128)(2,1)S(1)}, bf16[384,256]{1,0:T(8,128)(2,1)S(1)}, u32[]{:S(2)}, u32[]{:S(2)}) collective-permute-start(bf16[384,256]{1,0:T(8,128)(2,1)S(1)} %get-tuple-element.63.refs_2_), channel_id=1, source_target_pairs={{0,6},{2,4},{4,10},{6,8},{8,14},{10,12},{12,2},{14,0},{1,7},{3,5},... | collective-permute-start | bytes 589832 | tf_op jit(solution)/shard_map/ppermute | solution.py:466
  58.4 11.0 %collective-permute-start.15 = (bf16[384,256]{1,0:T(8,128)(2,1)S(1)}, bf16[384,256]{1,0:T(8,128)(2,1)S(1)}, u32[]{:S(2)}, u32[]{:S(2)}) collective-permute-start(bf16[384,256]{1,0:T(8,128)(2,1)S(1)} %get-tuple-element.63.refs_2_), channel_id=1, source_target_pairs={{0,12},{2,14},{4,0},{6,2},{8,4},{10,6},{12,8},{14,10},{1,13},{3,15... | collective-permute-start | bytes 589832 | tf_op jit(solution)/shard_map/ppermute | solution.py:466
  60.5 9.7 %collective-permute-start.23 = (bf16[384,256]{1,0:T(8,128)(2,1)S(1)}, bf16[384,256]{1,0:T(8,128)(2,1)S(1)}, u32[]{:S(2)}, u32[]{:S(2)}) collective-permute-start(bf16[384,256]{1,0:T(8,128)(2,1)S(1)} %get-tuple-element.63.refs_2_), channel_id=1, source_target_pairs={{0,1},{1,0},{2,3},{3,2},{4,5},{5,4},{6,7},{7,6},{8,9},{9,8},{10,11... | collective-permute-start | bytes 589832 | tf_op jit(solution)/shard_map/ppermute | solution.py:478
  67.7 2.5 %collective-permute-start.21 = (bf16[384,256]{1,0:T(8,128)(2,1)S(1)}, bf16[384,256]{1,0:T(8,128)(2,1)S(1)}, u32[]{:S(2)}, u32[]{:S(2)}) collective-permute-start(bf16[384,256]{1,0:T(8,128)(2,1)S(1)} %collective-permute-done.14.refs_2_), channel_id=1, source_target_pairs={{0,1},{1,0},{2,3},{3,2},{4,5},{5,4},{6,7},{7,6},{8,9},{9,8},{10,11... | collective-permute-start | bytes 589832 | tf_op jit(solution)/shard_map/ppermute | solution.py:478
  68.8 1.8 %collective-permute-start.16 = (bf16[384,256]{1,0:T(8,128)(2,1)S(1)}, bf16[384,256]{1,0:T(8,128)(2,1)S(1)}, u32[]{:S(2)}, u32[]{:S(2)}) collective-permute-start(bf16[384,256]{1,0:T(8,128)(2,1)S(1)} %collective-permute-done.11.refs_2_), channel_id=1, source_target_pairs={{0,1},{1,0},{2,3},{3,2},{4,5},{5,4},{6,7},{7,6},{8,9},{9,8},{10,11... | collective-permute-start | bytes 589832 | tf_op jit(solution)/shard_map/ppermute | solution.py:478
  68.9 2.9 %collective-permute-start.17 = (bf16[384,256]{1,0:T(8,128)(2,1)S(1)}, bf16[384,256]{1,0:T(8,128)(2,1)S(1)}, u32[]{:S(2)}, u32[]{:S(2)}) collective-permute-start(bf16[384,256]{1,0:T(8,128)(2,1)S(1)} %collective-permute-done.10.refs_4_), channel_id=1, source_target_pairs={{0,1},{1,0},{2,3},{3,2},{4,5},{5,4},{6,7},{7,6},{8,9},{9,8},{10,11... | collective-permute-start | bytes 589832 | tf_op jit(solution)/shard_map/ppermute | solution.py:478
  69.4 2.4 %collective-permute-start.18 = (bf16[384,256]{1,0:T(8,128)(2,1)S(1)}, bf16[384,256]{1,0:T(8,128)(2,1)S(1)}, u32[]{:S(2)}, u32[]{:S(2)}) collective-permute-start(bf16[384,256]{1,0:T(8,128)(2,1)S(1)} %collective-permute-done.12.refs_3_), channel_id=1, source_target_pairs={{0,1},{1,0},{2,3},{3,2},{4,5},{5,4},{6,7},{7,6},{8,9},{9,8},{10,11... | collective-permute-start | bytes 589832 | tf_op jit(solution)/shard_map/ppermute | solution.py:478
  70.2 1.6 %collective-permute-start.19 = (bf16[384,256]{1,0:T(8,128)(2,1)S(1)}, bf16[384,256]{1,0:T(8,128)(2,1)S(1)}, u32[]{:S(2)}, u32[]{:S(2)}) collective-permute-start(bf16[384,256]{1,0:T(8,128)(2,1)S(1)} %collective-permute-done.9.refs_3_), channel_id=1, source_target_pairs={{0,1},{1,0},{2,3},{3,2},{4,5},{5,4},{6,7},{7,6},{8,9},{9,8},{10,11... | collective-permute-start | bytes 589832 | tf_op jit(solution)/shard_map/ppermute | solution.py:478
  70.2 1.7 %collective-permute-start.20 = (bf16[384,256]{1,0:T(8,128)(2,1)S(1)}, bf16[384,256]{1,0:T(8,128)(2,1)S(1)}, u32[]{:S(2)}, u32[]{:S(2)}) collective-permute-start(bf16[384,256]{1,0:T(8,128)(2,1)S(1)} %collective-permute-done.13.refs_4_), channel_id=1, source_target_pairs={{0,1},{1,0},{2,3},{3,2},{4,5},{5,4},{6,7},{7,6},{8,9},{9,8},{10,11... | collective-permute-start | bytes 589832 | tf_op jit(solution)/shard_map/ppermute | solution.py:478
  70.7 1.5 %collective-permute-start.22 = (bf16[384,256]{1,0:T(8,128)(2,1)S(1)}, bf16[384,256]{1,0:T(8,128)(2,1)S(1)}, u32[]{:S(2)}, u32[]{:S(2)}) collective-permute-start(bf16[384,256]{1,0:T(8,128)(2,1)S(1)} %collective-permute-done.15.refs_3_), channel_id=1, source_target_pairs={{0,1},{1,0},{2,3},{3,2},{4,5},{5,4},{6,7},{7,6},{8,9},{9,8},{10,11... | collective-permute-start | bytes 589832 | tf_op jit(solution)/shard_map/ppermute | solution.py:478
